TPU v7x, 128 devices: a whole 4x4x4 slice. The times are simulated.
128 devices in a mesh: fsdp: 128 (over y, z, x, core).
Axes of the slice: x: 4, y: 4, z: 4, core: 2. Of those that a mesh axis runs over, the one named last changes fastest.
Arguments:
- hidden_in: bfloat16 [16384, 1024], P('fsdp'), may hold values from -24 to 24
- norm1_gain: bfloat16 [1024], P('fsdp'), may hold values from 0.099609375 to 1.8984375
- in_weight: bfloat16 [1024, 3072], P('fsdp'), may hold values from -0.1875 to 0.1875
- conv_weight: bfloat16 [1024, 3], P('fsdp'), may hold values from -3 to 3
- out_weight: bfloat16 [1024, 1024], P('fsdp'), may hold values from -0.1875 to 0.1875
- norm2_gain: bfloat16 [1024], P('fsdp'), may hold values from 0.099609375 to 1.8984375
- gate_weight: bfloat16 [1024, 4608], P('fsdp'), may hold values from -0.1875 to 0.1875
- up_weight: bfloat16 [1024, 4608], P('fsdp'), may hold values from -0.1875 to 0.1875
- down_weight: bfloat16 [4608, 1024], P('fsdp'), may hold values from -0.125 to 0.125
- segment_ids: int32 [16384], P('fsdp'), may hold values from 0 to 63, never falling along the last dimension, each value on 1 to 512 neighbouring positions
- cotangent: bfloat16 [16384, 1024], P('fsdp'), may hold values from -6 to 6
Outputs:
- block_out: bfloat16 [16384, 1024], P('fsdp')
- input_grad: float32 [16384, 1024], P('fsdp')
- norm1_gain_grad: float32 [1024], P('fsdp')
- in_weight_grad: float32 [1024, 3072], P('fsdp')
- conv_weight_grad: float32 [1024, 3], P('fsdp')
- out_weight_grad: float32 [1024, 1024], P('fsdp')
- norm2_gain_grad: float32 [1024], P('fsdp')
- gate_weight_grad: float32 [1024, 4608], P('fsdp')
- up_weight_grad: float32 [1024, 4608], P('fsdp')
- down_weight_grad: float32 [4608, 1024], P('fsdp')
Inputs may be any that keep to these rules, and one draw needn't show every extreme that they name: `segment_ids`: document numbers never fall along the tokens; each document covers 1 to 512 tokens, one exactly 512.
All inputs are finite; a program needn't handle non-finite values.
Results may differ from a plain program's by a relative error of at most 0.011.
Values may be sent and summed in bfloat16 or wider, within the bound.
A program may use at most 192 MiB of HBM per device.

v0:
```python
import jax
import jax.numpy as jnp
from jax import lax
from jax.sharding import PartitionSpec as P

CONV = 3


EPS = 1e-05


def shifted(value, axis, by):
    size = lax.axis_size(axis)
    pairs = [(i, i + by) for i in range(size) if 0 <= i + by < size]
    return lax.ppermute(value, axis, pairs)


def rms_scale(values):
    return lax.rsqrt(jnp.mean(values * values, axis=-1, keepdims=True) + EPS)


def per_device(
    hidden_in,
    norm1_gain,
    in_weight,
    conv_weight,
    out_weight,
    norm2_gain,
    gate_weight,
    up_weight,
    down_weight,
    segment_ids,
    cotangent,
):
    rows = hidden_in.shape[0]
    width = hidden_in.shape[1]
    gathered = (
        lax.all_gather(norm1_gain, "fsdp", axis=0, tiled=True),
        lax.all_gather(in_weight, "fsdp", axis=0, tiled=True),
        lax.all_gather(conv_weight, "fsdp", axis=0, tiled=True),
        lax.all_gather(out_weight, "fsdp", axis=0, tiled=True),
        lax.all_gather(norm2_gain, "fsdp", axis=0, tiled=True),
        lax.all_gather(gate_weight, "fsdp", axis=0, tiled=True),
        lax.all_gather(up_weight, "fsdp", axis=0, tiled=True),
        lax.all_gather(down_weight, "fsdp", axis=0, tiled=True),
    )
    gain1, w_in, w_conv, w_out, gain2, w_gate, w_up, w_down = gathered
    xf = hidden_in.astype(jnp.float32)
    s1 = rms_scale(xf)
    h = (xf * s1 * gain1.astype(jnp.float32)).astype(jnp.bfloat16)
    proj = jnp.dot(h, w_in, preferred_element_type=jnp.float32)
    bgate = proj[:, :width]
    cgate = proj[:, width : 2 * width]
    xv = proj[:, 2 * width :]
    bx = (bgate * xv).astype(jnp.bfloat16)
    prev_rows, prev_ids = shifted(
        (bx[rows - 2 :], segment_ids[rows - 2 :].astype(jnp.bfloat16)), "fsdp", 1
    )
    ext_bx = jnp.concatenate([prev_rows, bx], axis=0).astype(jnp.float32)
    ext_ids = jnp.concatenate([prev_ids.astype(jnp.int32), segment_ids], axis=0)
    taps = w_conv.astype(jnp.float32)
    masks = [
        (ext_ids[2 - k : 2 - k + rows] == segment_ids).astype(jnp.float32)[:, None]
        for k in range(CONV)
    ]
    conv_out = jnp.zeros((rows, width), jnp.float32)
    for k in range(CONV):
        conv_out = conv_out + taps[:, k] * masks[k] * ext_bx[2 - k : 2 - k + rows]
    y = (cgate * conv_out).astype(jnp.bfloat16)
    resid = xf + jnp.dot(y, w_out, preferred_element_type=jnp.float32)
    s2 = rms_scale(resid)
    gain2f = gain2.astype(jnp.float32)
    h2 = (resid * s2 * gain2f).astype(jnp.bfloat16)
    a = jnp.dot(h2, w_gate, preferred_element_type=jnp.float32)
    b = jnp.dot(h2, w_up, preferred_element_type=jnp.float32)
    sig = jax.nn.sigmoid(a)
    act = a * sig
    z = (act * b).astype(jnp.bfloat16)
    block_out = (resid + jnp.dot(z, w_down, preferred_element_type=jnp.float32)).astype(
        jnp.bfloat16
    )
    again = (
        lax.all_gather(norm1_gain, "fsdp", axis=0, tiled=True),
        lax.all_gather(in_weight, "fsdp", axis=0, tiled=True),
        lax.all_gather(conv_weight, "fsdp", axis=0, tiled=True),
        lax.all_gather(out_weight, "fsdp", axis=0, tiled=True),
        lax.all_gather(norm2_gain, "fsdp", axis=0, tiled=True),
        lax.all_gather(gate_weight, "fsdp", axis=0, tiled=True),
        lax.all_gather(up_weight, "fsdp", axis=0, tiled=True),
        lax.all_gather(down_weight, "fsdp", axis=0, tiled=True),
    )
    gain1, w_in, w_conv, w_out, gain2, w_gate, w_up, w_down = again
    taps = w_conv.astype(jnp.float32)
    gain2f = gain2.astype(jnp.float32)
    dz = lax.dot_general(
        cotangent, w_down, (((1,), (1,)), ((), ())), preferred_element_type=jnp.float32
    )
    da = (dz * b * sig * (1.0 + a * (1.0 - sig))).astype(jnp.bfloat16)
    db = (dz * act).astype(jnp.bfloat16)
    g_down = lax.dot_general(
        z, cotangent, (((0,), (0,)), ((), ())), preferred_element_type=jnp.float32
    )
    g_gate = lax.dot_general(h2, da, (((0,), (0,)), ((), ())), preferred_element_type=jnp.float32)
    g_up = lax.dot_general(h2, db, (((0,), (0,)), ((), ())), preferred_element_type=jnp.float32)
    dh2 = lax.dot_general(da, w_gate, (((1,), (1,)), ((), ())), preferred_element_type=jnp.float32)
    dh2 = dh2 + lax.dot_general(
        db, w_up, (((1,), (1,)), ((), ())), preferred_element_type=jnp.float32
    )
    g_gain2 = jnp.sum(dh2 * resid * s2, axis=0)
    dn2 = dh2 * gain2f
    d_resid = (
        cotangent.astype(jnp.float32)
        + s2 * dn2
        - resid * (s2 * s2 * s2) * jnp.mean(dn2 * resid, axis=-1, keepdims=True)
    )
    d_out = d_resid.astype(jnp.bfloat16)
    g_out = lax.dot_general(y, d_out, (((0,), (0,)), ((), ())), preferred_element_type=jnp.float32)
    dy = lax.dot_general(d_out, w_out, (((1,), (1,)), ((), ())), preferred_element_type=jnp.float32)
    d_cgate = dy * conv_out
    d_conv = dy * cgate
    d_ext = jnp.zeros((rows + 2, width), jnp.float32)
    tap_cols = []
    for k in range(CONV):
        term = d_conv * masks[k]
        d_ext = d_ext + jnp.pad(taps[:, k] * term, ((2 - k, k), (0, 0)))
        tap_cols.append(jnp.sum(term * ext_bx[2 - k : 2 - k + rows], axis=0))
    g_conv = jnp.stack(tap_cols, axis=1)
    returned = shifted(d_ext[:2], "fsdp", -1)
    d_bx = d_ext[2:] + jnp.pad(returned, ((rows - 2, 0), (0, 0)))
    d_proj = jnp.concatenate([d_bx * xv, d_cgate, d_bx * bgate], axis=1).astype(jnp.bfloat16)
    g_in = lax.dot_general(h, d_proj, (((0,), (0,)), ((), ())), preferred_element_type=jnp.float32)
    dh = lax.dot_general(d_proj, w_in, (((1,), (1,)), ((), ())), preferred_element_type=jnp.float32)
    g_gain1 = jnp.sum(dh * xf * s1, axis=0)
    dn1 = dh * gain1.astype(jnp.float32)
    input_grad = (
        d_resid + s1 * dn1 - xf * (s1 * s1 * s1) * jnp.mean(dn1 * xf, axis=-1, keepdims=True)
    )
    owned = (
        lax.psum_scatter(g_gain1, "fsdp", scatter_dimension=0, tiled=True),
        lax.psum_scatter(g_in, "fsdp", scatter_dimension=0, tiled=True),
        lax.psum_scatter(g_conv, "fsdp", scatter_dimension=0, tiled=True),
        lax.psum_scatter(g_out, "fsdp", scatter_dimension=0, tiled=True),
        lax.psum_scatter(g_gain2, "fsdp", scatter_dimension=0, tiled=True),
        lax.psum_scatter(g_gate, "fsdp", scatter_dimension=0, tiled=True),
        lax.psum_scatter(g_up, "fsdp", scatter_dimension=0, tiled=True),
        lax.psum_scatter(g_down, "fsdp", scatter_dimension=0, tiled=True),
    )
    return (block_out, input_grad) + tuple(owned)


def solution(mesh):
    return jax.shard_map(
        per_device,
        mesh=mesh,
        in_specs=(
            P("fsdp", None),
            P("fsdp"),
            P("fsdp", None),
            P("fsdp", None),
            P("fsdp", None),
            P("fsdp"),
            P("fsdp", None),
            P("fsdp", None),
            P("fsdp", None),
            P("fsdp"),
            P("fsdp", None),
        ),
        out_specs=(
            P("fsdp", None),
            P("fsdp", None),
            P("fsdp"),
            P("fsdp", None),
            P("fsdp", None),
            P("fsdp", None),
            P("fsdp"),
            P("fsdp", None),
            P("fsdp", None),
            P("fsdp", None),
        ),
        check_vma=False,
    )
```

profile of v0, /device:TPU:0, one launch (start us, length us, event | category | flops | bytes accessed | tf_op | source)
XLA Modules:
  0.0 1753.5 jit_solution(17368093625752151035)
XLA Ops:
  14.3 70.2 %all-reduce.12 = (bf16[1024]{0:T(1024)(128)(2,1)S(1)}, bf16[1024]{0:T(1024)(128)(2,1)S(1)}) all-reduce(bf16[1024]{0:T(1024)(128)(2,1)S(1)} %dynamic-update-slice, bf16[1024]{0:T(1024)(128)(2,1)S(1)} %dynamic-update-slice.1), channel_id=1, replica_groups=mesh['fsdp'=128] {'fsdp'}, use_global_device_ids=true, to_apply=%add.4 | all-reduce | flops 2048 | bytes 8192
  84.5 33.3 %all-gather = bf16[128,8,3]{1,2,0:T(4,128)(2,1)S(1)} all-gather(bf16[1,8,3]{1,2,0:T(4,128)(2,1)} %bitcast.48), channel_id=1, replica_groups=mesh['fsdp'=128] {'fsdp'}, dimensions={0}, use_global_device_ids=true | all-gather | bytes 6192 | tf_op jit(solution)/shard_map/all_gather | solution.py:40
  120.0 4.0 fusion.18
  124.1 2.4 collective-permute-start
  128.3 19.7 %all-gather.10.cloned.1.call-done = bf16[1024,1024]{1,0:T(8,128)(2,1)} async-done(((bf16[8,1024]{1,0:T(8,128)(2,1)}), bf16[1024,1024]{1,0:T(8,128)(2,1)}) %all-gather.10.cloned.1.call-update) | async-done | bytes 2097168 | tf_op jit(solution)/shard_map/all_gather | solution.py:41
  150.3 70.0 %all-gather.16.cloned.1.call-done = bf16[128,36,1024]{2,1,0:T(8,128)(2,1)} async-done(((bf16[1,36,1024]{2,1,0:T(8,128)(2,1)}), bf16[128,36,1024]{2,1,0:T(8,128)(2,1)}) %all-gather.16.cloned.1.call-update) | async-done | bytes 9437200 | tf_op jit(solution)/shard_map/all_gather | solution.py:45
  220.2 13.2 reshape.70
  233.4 58.8 %all-gather.14.cloned.1.call-done = bf16[1024,4608]{1,0:T(8,128)(2,1)} async-done(((bf16[8,4608]{1,0:T(8,128)(2,1)}), bf16[1024,4608]{1,0:T(8,128)(2,1)}) %all-gather.14.cloned.1.call-update) | async-done | bytes 9437200 | tf_op jit(solution)/shard_map/all_gather | solution.py:44
  292.2 6.5 fusion.24
  298.7 64.8 %all-gather.12.cloned.1.call-done = bf16[1024,4608]{1,0:T(8,128)(2,1)} async-done(((bf16[8,4608]{1,0:T(8,128)(2,1)}), bf16[1024,4608]{1,0:T(8,128)(2,1)}) %all-gather.12.cloned.1.call-update) | async-done | bytes 9437200 | tf_op jit(solution)/shard_map/all_gather | solution.py:43
  363.5 6.7 fusion.23
  371.4 6.1 multiply_convert_fusion
  377.5 7.6 fusion.25
  385.2 7.0 multiply_reduce_fusion
  393.2 2.8 fusion.13
  396.0 2.6 fusion.15
  403.2 6.4 fusion.11
  410.8 7.9 fusion.27
  420.0 7.8 fusion.26
  429.2 7.8 fusion.28
  437.0 369.9 %fusion = f32[40,1024]{1,0:T(8,128)S(1)} fusion(f32[4608,1024]{1,0:T(8,128)} %fusion.28), kind=kCustom, calls=%all-reduce-scatter | all-reduce-scatter fusion | flops 5242881 | bytes 19038208
  813.8 6.2 fusion.2
  820.0 2.3 fusion.10
  825.1 2.1 collective-permute-start.8
  829.9 3.4 collective-permute-start.5
  835.3 4.8 collective-permute-start.3
  841.1 86.2 %all-reduce.11 = (f32[1024]{0:T(1024)S(1)}, f32[1024,3]{0,1:T(4,128)S(1)}, f32[1024]{0:T(1024)S(1)}) all-reduce(f32[1024]{0:T(1024)S(1)} %get-tuple-element.15, f32[1024,3]{0,1:T(4,128)S(1)} %pad_maximum_fusion.3, f32[1024]{0:T(1024)S(1)} %get-tuple-element.13), channel_id=2, replica_groups=mesh['fsdp'=128] {'fsdp'}, use_global_device_ids=true, to_apply=%region_5.6.clone | all-reduce | flops 5120 | bytes 40960
  930.5 12.5 concatenate.13
  943.7 94.0 %reduce-scatter.10.cloned.1.call-done = f32[8,1024]{1,0:T(8,128)} async-done(((f32[1024,1024]{1,0:T(8,128)}), f32[8,1024]{1,0:T(8,128)}) %reduce-scatter.10.cloned.1.call-update) | async-done | bytes 32784 | tf_op jit(solution)/shard_map/reduce_scatter | solution.py:142
  1037.6 228.2 %reduce-scatter.8.cloned.1.call-done = f32[8,3072]{1,0:T(8,128)} async-done(((f32[1024,3072]{1,0:T(8,128)}), f32[8,3072]{1,0:T(8,128)}) %reduce-scatter.8.cloned.1.call-update) | async-done | bytes 98320 | tf_op jit(solution)/shard_map/reduce_scatter | solution.py:140
  1265.8 241.0 %reduce-scatter.14.cloned.1.call-done = f32[8,4608]{1,0:T(8,128)} async-done(((f32[1024,4608]{1,0:T(8,128)}), f32[8,4608]{1,0:T(8,128)}) %reduce-scatter.14.cloned.1.call-update) | async-done | bytes 147472 | tf_op jit(solution)/shard_map/reduce_scatter | solution.py:145
  1506.8 240.1 %reduce-scatter.12.cloned.1.call-done = f32[8,4608]{1,0:T(8,128)} async-done(((f32[1024,4608]{1,0:T(8,128)}), f32[8,4608]{1,0:T(8,128)}) %reduce-scatter.12.cloned.1.call-update) | async-done | bytes 147472 | tf_op jit(solution)/shard_map/reduce_scatter | solution.py:144
  (149 shorter events, 42.8 us)
Async XLA Ops:
  7.2 112.8 %all-gather.8.cloned.1.call-start = ((), (), s32[]{:S(2)}) async-start(), calls=%async_computation.4 | async-start | bytes 6340608 | tf_op jit(solution)/shard_map/all_gather | solution.py:39
  7.9 140.1 %all-gather.10.cloned.1.call-start = ((), (), s32[]{:S(2)}) async-start(), calls=%async_computation.5 | async-start | bytes 2113536 | tf_op jit(solution)/shard_map/all_gather | solution.py:41
  8.7 211.6 %all-gather.16.cloned.1.call-start = ((), (), s32[]{:S(2)}) async-start(), calls=%async_computation.12 | async-start | bytes 10567680 | tf_op jit(solution)/shard_map/all_gather | solution.py:45
  9.4 282.8 %all-gather.14.cloned.1.call-start = ((), (), s32[]{:S(2)}) async-start(), calls=%async_computation.7 | async-start | bytes 9510912 | tf_op jit(solution)/shard_map/all_gather | solution.py:44
  10.0 353.5 %all-gather.12.cloned.1.call-start = ((), (), s32[]{:S(2)}) async-start(), calls=%async_computation.6 | async-start | bytes 9510912 | tf_op jit(solution)/shard_map/all_gather | solution.py:43
  10.6 1027.1 %reduce-scatter.10.cloned.1.call-start = ((), (), s32[]{:S(2)}) async-start(), calls=%async_computation.9 | async-start | bytes 4227072 | tf_op jit(solution)/shard_map/reduce_scatter | solution.py:142
  11.3 107.9 %collective-permute-start.1 = (bf16[2]{0:T(256)(128)(2,1)S(1)}, bf16[2]{0:T(256)(128)(2,1)S(1)}, u32[]{:S(2)}, u32[]{:S(2)}) collective-permute-start(bf16[2]{0:T(256)(128)(2,1)S(1)} %slice.59), channel_id=1, source_target_pairs={{0,1},{1,2},{2,3},{3,4},{4,5},{5,6},{6,7},{7,8},{8,9},{9,10},{10,1... | collective-permute-start | bytes 20 | tf_op jit(solution)/shard_map/ppermute | solution.py:15
  124.0 24.0 %copy-start.2 = (bf16[128,1024]{1,0:T(8,128)(2,1)S(1)}, bf16[128,1024]{1,0:T(8,128)(2,1)}, u32[]{:S(2)}) copy-start(bf16[128,1024]{1,0:T(8,128)(2,1)} %param.11) | copy-start | bytes 786436
  124.1 3.1 collective-permute-start
  396.0 869.9 %reduce-scatter.8.cloned.1.call-start = ((), (), s32[]{:S(2)}) async-start(), calls=%async_computation.8 | async-start | bytes 12681216 | tf_op jit(solution)/shard_map/reduce_scatter | solution.py:140
  399.2 3.1 collective-permute-start.2
  409.6 1097.2 %reduce-scatter.14.cloned.1.call-start = ((), (), s32[]{:S(2)}) async-start(), calls=%async_computation.11 | async-start | bytes 19021824 | tf_op jit(solution)/shard_map/reduce_scatter | solution.py:145
  418.8 1328.1 %reduce-scatter.12.cloned.1.call-start = ((), (), s32[]{:S(2)}) async-start(), calls=%async_computation.10 | async-start | bytes 19021824 | tf_op jit(solution)/shard_map/reduce_scatter | solution.py:144
  437.0 383.0 %slice-start = ((s8[6291456]{0:T(1024)(128)(4,1)}), s8[2097152]{0:T(1024)(128)(4,1)S(1)}, s32[]{:S(2)}) async-start(s8[6291456]{0:T(1024)(128)(4,1)} %bitcast.36), calls=%async_computation.13 | async-start | bytes 4194304
  807.0 16.7 collective-permute-start.14
  808.5 16.5 collective-permute-start.13
  809.8 17.4 collective-permute-start.12
  811.1 17.4 collective-permute-start.11
  812.5 9.9 collective-permute-start.15
  820.0 20.0 %copy-start.4 = (f32[128,1024]{1,0:T(8,128)S(1)}, f32[128,1024]{1,0:T(8,128)}, u32[]{:S(2)}) copy-start(f32[128,1024]{1,0:T(8,128)} %copy-done.3) | copy-start | bytes 1572868
  822.4 18.7 %copy-start.27 = (f32[28,1024]{1,0:T(8,128)}, f32[28,1024]{1,0:T(8,128)S(1)}, u32[]{:S(2)}) copy-start(f32[28,1024]{1,0:T(8,128)S(1)} %collective-permute-done.15) | copy-start | bytes 344068
  822.4 7.5 collective-permute-start.10
  823.7 17.3 copy-start.17
  823.7 9.6 collective-permute-start.9
  825.0 16.0 copy-start.18
  825.1 10.2 collective-permute-start.8
  827.2 13.8 copy-start.19
  827.2 101.8 %collective-permute-start.7 = (f32[40,1024]{1,0:T(8,128)S(1)}, f32[40,1024]{1,0:T(8,128)S(1)}, u32[]{:S(2)}, u32[]{:S(2)}) collective-permute-start(f32[40,1024]{1,0:T(8,128)S(1)} %fusion), channel_id=1, source_target_pairs={{0,5},{1,6},{2,7},{3,8},{4,9},{5,10},{6,11},{7,12},{8,13},{9,14},{... | collective-permute-start | bytes 491528
  828.6 100.5 %collective-permute-start.6 = (f32[40,1024]{1,0:T(8,128)S(1)}, f32[40,1024]{1,0:T(8,128)S(1)}, u32[]{:S(2)}, u32[]{:S(2)}) collective-permute-start(f32[40,1024]{1,0:T(8,128)S(1)} %fusion), channel_id=1, source_target_pairs={{0,4},{1,5},{2,6},{3,7},{4,8},{5,9},{6,10},{7,11},{8,12},{9,13},{1... | collective-permute-start | bytes 491528
  829.9 99.2 %collective-permute-start.5 = (f32[40,1024]{1,0:T(8,128)S(1)}, f32[40,1024]{1,0:T(8,128)S(1)}, u32[]{:S(2)}, u32[]{:S(2)}) collective-permute-start(f32[40,1024]{1,0:T(8,128)S(1)} %fusion), channel_id=1, source_target_pairs={{0,3},{1,4},{2,5},{3,6},{4,7},{5,8},{6,9},{7,10},{8,11},{9,12},{10... | collective-permute-start | bytes 491528
  833.4 95.7 %collective-permute-start.4 = (f32[40,1024]{1,0:T(8,128)S(1)}, f32[40,1024]{1,0:T(8,128)S(1)}, u32[]{:S(2)}, u32[]{:S(2)}) collective-permute-start(f32[40,1024]{1,0:T(8,128)S(1)} %fusion), channel_id=1, source_target_pairs={{0,2},{1,3},{2,4},{3,5},{4,6},{5,7},{6,8},{7,9},{8,10},{9,11},{10,... | collective-permute-start | bytes 491528
  835.3 95.3 %collective-permute-start.3 = (f32[40,1024]{1,0:T(8,128)S(1)}, f32[40,1024]{1,0:T(8,128)}, u32[]{:S(2)}, u32[]{:S(2)}) collective-permute-start(f32[40,1024]{1,0:T(8,128)S(1)} %fusion), channel_id=1, source_target_pairs={{0,1},{1,2},{2,3},{3,4},{4,5},{5,6},{6,7},{7,8},{8,9},{9,10},{10,1... | collective-permute-start | bytes 491528
  (24 other events, 100.9 us)
Sparse Core Ops, SparseCore 0:
  11.1 70.6 all-gather.7
  85.0 62.9 all-gather.9
  151.1 69.0 all-gather.15
  223.1 69.0 all-gather.13
  295.1 68.3 all-gather.11
  396.1 641.5 reduce-scatter.9
  1044.0 221.7 reduce-scatter.7
  1272.5 234.2 reduce-scatter.13
  1512.7 234.1 reduce-scatter.11
where the time goes:
time: 1760 us; the launch traced here: 1750 us
  waiting for transfers between devices  1020 us (58%)
  blocking collectives  560 us (32%)
  matrix products  83.8 us (5%)
  local copies, waits for them, and re-layouts  38 us (2%)
  starting transfers between devices  29.8 us (2%)
    unnamed x3, blocking collectives  526 us
    reduce_scatter x1, waiting for transfers between devices, per_device(): lax.psum_scatter(g_up, 'fsdp', scatter_dimension=0, tiled=True)  241 us
    reduce_scatter x1, waiting for transfers between devices, per_device(): lax.psum_scatter(g_gate, 'fsdp', scatter_dimension=0, tiled=True)  240 us
    reduce_scatter x1, waiting for transfers between devices, per_device(): lax.psum_scatter(g_in, 'fsdp', scatter_dimension=0, tiled=True)  228 us
    reduce_scatter x1, waiting for transfers between devices, per_device(): lax.psum_scatter(g_out, 'fsdp', scatter_dimension=0, tiled=True)  94 us
    all_gather x1, waiting for transfers between devices, per_device(): lax.all_gather(down_weight, 'fsdp', axis=0, tiled=True)  70 us
    all_gather x1, waiting for transfers between devices, per_device(): lax.all_gather(gate_weight, 'fsdp', axis=0, tiled=True)  64.8 us
    all_gather x1, waiting for transfers between devices, per_device(): lax.all_gather(up_weight, 'fsdp', axis=0, tiled=True)  58.8 us
  transfers between devices with their start and end apart: 25, of which 10 were waited for; matrix products, arithmetic and copies ran while one was open for 26% of the time, Pallas kernels for 0%

commit v1 on v0

--- a/solution.py
+++ b/solution.py
@@ -4,9 +4,8 @@
 from jax.sharding import PartitionSpec as P
 
 CONV = 3
-
-
 EPS = 1e-05
+LANE = 256
 
 
 def shifted(value, axis, by):
@@ -17,6 +16,35 @@
 
 def rms_scale(values):
     return lax.rsqrt(jnp.mean(values * values, axis=-1, keepdims=True) + EPS)
+
+
+def pad_cols(x):
+    extra = (-x.shape[1]) % LANE
+    return jnp.pad(x, ((0, 0), (0, extra))) if extra else x
+
+
+def gather_packed(pieces):
+    widths = [p.shape[1] for p in pieces]
+    packed = jnp.concatenate(pieces, axis=1)
+    full = lax.all_gather(packed, "fsdp", axis=0, tiled=True)
+    out, at = [], 0
+    for w in widths:
+        out.append(full[:, at : at + w])
+        at += w
+    return out
+
+
+def scatter_packed(pieces):
+    widths = [p.shape[1] for p in pieces]
+    packed = jnp.concatenate(pieces, axis=1)
+    mine = lax.optimization_barrier(
+        lax.psum_scatter(packed, "fsdp", scatter_dimension=0, tiled=True)
+    )
+    out, at = [], 0
+    for w in widths:
+        out.append(mine[:, at : at + w])
+        at += w
+    return out
 
 
 def per_device(
@@ -34,17 +62,22 @@
 ):
     rows = hidden_in.shape[0]
     width = hidden_in.shape[1]
-    gathered = (
-        lax.all_gather(norm1_gain, "fsdp", axis=0, tiled=True),
-        lax.all_gather(in_weight, "fsdp", axis=0, tiled=True),
-        lax.all_gather(conv_weight, "fsdp", axis=0, tiled=True),
-        lax.all_gather(out_weight, "fsdp", axis=0, tiled=True),
-        lax.all_gather(norm2_gain, "fsdp", axis=0, tiled=True),
-        lax.all_gather(gate_weight, "fsdp", axis=0, tiled=True),
-        lax.all_gather(up_weight, "fsdp", axis=0, tiled=True),
-        lax.all_gather(down_weight, "fsdp", axis=0, tiled=True),
-    )
-    gain1, w_in, w_conv, w_out, gain2, w_gate, w_up, w_down = gathered
+    per = in_weight.shape[0]
+    n = lax.axis_size("fsdp")
+    down_rows = down_weight.shape[0]
+    small = jnp.concatenate(
+        [norm1_gain[:, None], norm2_gain[:, None], conv_weight], axis=1
+    )
+    n_small = small.shape[1]
+    w_in, w_out, small_full = gather_packed([in_weight, out_weight, pad_cols(small)])
+    w_gate, w_up, w_down_packed = gather_packed(
+        [gate_weight, up_weight, down_weight.reshape(per, -1)]
+    )
+    w_down = w_down_packed.reshape(n * down_rows, width)
+    gain1 = small_full[:, 0]
+    gain2 = small_full[:, 1]
+    w_conv = small_full[:, 2 : 2 + CONV]
+
     xf = hidden_in.astype(jnp.float32)
     s1 = rms_scale(xf)
     h = (xf * s1 * gain1.astype(jnp.float32)).astype(jnp.bfloat16)
@@ -79,19 +112,7 @@
     block_out = (resid + jnp.dot(z, w_down, preferred_element_type=jnp.float32)).astype(
         jnp.bfloat16
     )
-    again = (
-        lax.all_gather(norm1_gain, "fsdp", axis=0, tiled=True),
-        lax.all_gather(in_weight, "fsdp", axis=0, tiled=True),
-        lax.all_gather(conv_weight, "fsdp", axis=0, tiled=True),
-        lax.all_gather(out_weight, "fsdp", axis=0, tiled=True),
-        lax.all_gather(norm2_gain, "fsdp", axis=0, tiled=True),
-        lax.all_gather(gate_weight, "fsdp", axis=0, tiled=True),
-        lax.all_gather(up_weight, "fsdp", axis=0, tiled=True),
-        lax.all_gather(down_weight, "fsdp", axis=0, tiled=True),
-    )
-    gain1, w_in, w_conv, w_out, gain2, w_gate, w_up, w_down = again
-    taps = w_conv.astype(jnp.float32)
-    gain2f = gain2.astype(jnp.float32)
+
     dz = lax.dot_general(
         cotangent, w_down, (((1,), (1,)), ((), ())), preferred_element_type=jnp.float32
     )
@@ -102,6 +123,9 @@
     )
     g_gate = lax.dot_general(h2, da, (((0,), (0,)), ((), ())), preferred_element_type=jnp.float32)
     g_up = lax.dot_general(h2, db, (((0,), (0,)), ((), ())), preferred_element_type=jnp.float32)
+    own_gate, own_up, own_down = scatter_packed(
+        [g_gate, g_up, g_down.reshape(n * per, -1)]
+    )
     dh2 = lax.dot_general(da, w_gate, (((1,), (1,)), ((), ())), preferred_element_type=jnp.float32)
     dh2 = dh2 + lax.dot_general(
         db, w_up, (((1,), (1,)), ((), ())), preferred_element_type=jnp.float32
@@ -135,17 +159,20 @@
     input_grad = (
         d_resid + s1 * dn1 - xf * (s1 * s1 * s1) * jnp.mean(dn1 * xf, axis=-1, keepdims=True)
     )
-    owned = (
-        lax.psum_scatter(g_gain1, "fsdp", scatter_dimension=0, tiled=True),
-        lax.psum_scatter(g_in, "fsdp", scatter_dimension=0, tiled=True),
-        lax.psum_scatter(g_conv, "fsdp", scatter_dimension=0, tiled=True),
-        lax.psum_scatter(g_out, "fsdp", scatter_dimension=0, tiled=True),
-        lax.psum_scatter(g_gain2, "fsdp", scatter_dimension=0, tiled=True),
-        lax.psum_scatter(g_gate, "fsdp", scatter_dimension=0, tiled=True),
-        lax.psum_scatter(g_up, "fsdp", scatter_dimension=0, tiled=True),
-        lax.psum_scatter(g_down, "fsdp", scatter_dimension=0, tiled=True),
-    )
-    return (block_out, input_grad) + tuple(owned)
+    g_small = jnp.concatenate([g_gain1[:, None], g_gain2[:, None], g_conv], axis=1)
+    own_in, own_out, own_small = scatter_packed([g_in, g_out, pad_cols(g_small)])
+    return (
+        block_out,
+        input_grad,
+        own_small[:, 0],
+        own_in,
+        own_small[:, 2 : 2 + CONV],
+        own_out,
+        own_small[:, 1],
+        own_gate,
+        own_up,
+        own_down.reshape(down_rows, width),
+    )
 
 
 def solution(mesh):

time: 1760 us -> 1280 us (0.73)
  blocking collectives: 560 us -> 0 us
  other arithmetic: 5.91 us -> 62.7 us
  waiting for transfers between devices: 1020 us -> 1050 us
  starting transfers between devices: 29.8 us -> 5.07 us
  local copies, waits for them, and re-layouts: 38 us -> 57.6 us
    unnamed x3 -> x0, blocking collectives: 526 us -> none
    reduce_scatter x4 -> x2, waiting for transfers between devices: 803 us -> 899 us  [scatter_packed(): lax.psum_scatter(packed, 'fsdp', scatter_dimension=0, tiled=True)]
    all_gather x5 -> x2, waiting for transfers between devices: 213 us -> 153 us  [gather_packed(): full = lax.all_gather(packed, 'fsdp', axis=0, tiled=True)]
    concatenate x0 -> x5, other arithmetic: none -> 53.2 us  [the longest x2 49.4 us: scatter_packed(): packed = jnp.concatenate(pieces, axis=1)]
    reshape x0 -> x4, local copies, waits for them, and re-layouts: none -> 40.8 us  [the longest x1 21.6 us: per_device(): g_down.reshape(n * per, -1)]
    unnamed x73 -> x36, local copies, waits for them, and re-layouts: 37.6 us -> 0.83 us
    all_gather x1 -> x0, blocking collectives: 33.3 us -> none  [per_device(): lax.all_gather(conv_weight, 'fsdp', axis=0, tiled=True)]
    unnamed x13 -> x0, starting transfers between devices: 24.2 us -> none
  transfers between devices with their start and end apart: 25 -> 7, of which waited for: 10 -> 5; matrix products, arithmetic and copies ran while one was open for 26% -> 9% of each run, Pallas kernels for 0% -> 0%
where the time goes in v1:
time: 1280 us; the launch traced here: 1270 us
  waiting for transfers between devices  1050 us (82%)
  matrix products  81.7 us (6%)
  other arithmetic  62.7 us (5%)
  local copies, waits for them, and re-layouts  57.6 us (4%)
  between operations  14.2 us (1%)
    reduce_scatter x2, waiting for transfers between devices, scatter_packed(): lax.psum_scatter(packed, 'fsdp', scatter_dimension=0, tiled=True)  899 us
    all_gather x2, waiting for transfers between devices, gather_packed(): full = lax.all_gather(packed, 'fsdp', axis=0, tiled=True)  153 us
    concatenate x2, other arithmetic, scatter_packed(): packed = jnp.concatenate(pieces, axis=1)  49.4 us
  transfers between devices with their start and end apart: 7, of which 5 were waited for; matrix products, arithmetic and copies ran while one was open for 9% of the time, Pallas kernels for 0%

profile of v1, /device:TPU:0, one launch (start us, length us, event | category | flops | bytes accessed | tf_op | source)
XLA Modules:
  0.0 1274.9 jit_solution(17129408030517518262)
XLA Ops:
  8.0 1.5 fusion.39
  10.6 1.6 pad_maximum_fusion.4
  17.4 67.1 %all-gather.3.cloned.1.call-done = bf16[1024,4352]{1,0:T(8,128)(2,1)} async-done(((bf16[8,4352]{1,0:T(8,128)(2,1)}), bf16[1024,4352]{1,0:T(8,128)(2,1)}) %all-gather.3.cloned.1.call-update) | async-done | bytes 8912912 | tf_op jit(solution)/shard_map/all_gather | solution.py:29
  84.5 1.4 convert_reduce_fusion
  85.9 4.0 fusion.10
  89.9 2.2 collective-permute-start
  95.2 2.3 multiply_reduce_fusion.5
  97.6 85.5 %all-gather.5.cloned.1.call-done = bf16[1024,13824]{1,0:T(8,128)(2,1)} async-done(((bf16[8,13824]{1,0:T(8,128)(2,1)}), bf16[1024,13824]{1,0:T(8,128)(2,1)}) %all-gather.5.cloned.1.call-update) | async-done | bytes 28311568 | tf_op jit(solution)/shard_map/all_gather | solution.py:29
  183.1 7.9 slice.156
  191.1 17.4 %reshape.88 = bf16[4608,1024]{1,0:T(8,128)(2,1)} reshape(bf16[1024,4608]{1,0:T(8,128)(2,1)} %slice.156) | data formatting | bytes 18874368 | tf_op jit(solution)/shard_map/reshape | solution.py:76
  208.5 6.9 convolution_bitcast_fusion
  215.4 5.1 fusion.2
  220.5 5.8 multiply_convert_fusion.1
  226.3 7.6 fusion
  234.0 6.0 multiply_reduce_fusion.3
  240.3 2.7 fusion.34
  244.4 1.5 collective-permute-start.2
  246.0 1.6 collective-permute-done.2
  247.8 6.5 fusion.32
  254.2 3.0 fusion.31
  257.5 11.7 select_maximum_fusion
  269.2 7.9 fusion.45
  277.2 21.6 %reshape.89 = f32[1024,4608]{1,0:T(8,128)} reshape(f32[4608,1024]{1,0:T(8,128)} %fusion.45) | data formatting | bytes 37748736 | tf_op jit(solution)/shard_map/reshape | solution.py:127
  298.8 9.3 fusion.43
  308.1 7.9 fusion.44
  316.0 37.7 %pad_maximum_fusion = f32[1024,13824]{1,0:T(8,128)} fusion(f32[1024,4608]{1,0:T(8,128)} %reshape.89, f32[1024,4608]{1,0:T(8,128)} %fusion.44, f32[1024,4608]{1,0:T(8,128)} %fusion.43), kind=kLoop, calls=%fused_computation | loop fusion | flops 28311552 | bytes 113246208 | tf_op jit(solution)/shard_map/concatenate | solution.py:39
  353.7 5.9 fusion.23
  360.7 582.3 %reduce-scatter.3.cloned.1.call-done = f32[8,4352]{1,0:T(8,128)} async-done(((f32[1024,4352]{1,0:T(8,128)}), f32[8,4352]{1,0:T(8,128)}) %reduce-scatter.3.cloned.1.call-update) | async-done | bytes 139280 | tf_op jit(solution)/shard_map/reduce_scatter | solution.py:41
  945.0 1.5 slice.159
  947.2 1.5 slice_reduce_fusion.3
  948.7 317.1 %reduce-scatter.5.cloned.1.call-done = f32[8,13824]{1,0:T(8,128)} async-done(((f32[1024,13824]{1,0:T(8,128)}), f32[8,13824]{1,0:T(8,128)}) %reduce-scatter.5.cloned.1.call-update) | async-done | bytes 442384 | tf_op jit(solution)/shard_map/reduce_scatter | solution.py:41
  1265.8 1.8 fusion.42
  (80 shorter events, 17.0 us)
Async XLA Ops:
  7.2 77.3 %all-gather.3.cloned.1.call-start = ((), (), s32[]{:S(2)}) async-start(), calls=%async_computation.2 | async-start | bytes 8982528 | tf_op jit(solution)/shard_map/all_gather | solution.py:29
  9.5 173.6 %all-gather.5.cloned.1.call-start = ((), (), s32[]{:S(2)}) async-start(), calls=%async_computation.3 | async-start | bytes 28532736 | tf_op jit(solution)/shard_map/all_gather | solution.py:29
  12.2 930.7 %reduce-scatter.3.cloned.1.call-start = ((), (), s32[]{:S(2)}) async-start(), calls=%async_computation.4 | async-start | bytes 17965056 | tf_op jit(solution)/shard_map/reduce_scatter | solution.py:41
  13.0 2.9 collective-permute-start.1
  85.9 9.3 copy-start.3
  89.9 4.2 copy-start
  89.9 4.0 collective-permute-start
  95.2 95.9 %copy-start.10 = (bf16[128,1024]{1,0:T(8,128)(2,1)}, bf16[128,1024]{1,0:T(8,128)(2,1)S(1)}, u32[]{:S(2)}) copy-start(bf16[128,1024]{1,0:T(8,128)(2,1)S(1)} %get-tuple-element.55) | copy-start | bytes 786436
  191.1 17.4 %copy-start.2 = (bf16[128,1024]{1,0:T(8,128)(2,1)S(1)}, bf16[128,1024]{1,0:T(8,128)(2,1)}, u32[]{:S(2)}) copy-start(bf16[128,1024]{1,0:T(8,128)(2,1)} %param.21) | copy-start | bytes 786436
  226.3 7.6 copy-start.7
  226.3 7.7 copy-start.9
  233.9 9.1 slice-start
  234.0 6.3 copy-start.11
  234.0 9.0 slice-start.1
  234.0 9.0 slice-start.2
  240.1 3.8 copy-start.1
  240.1 3.8 copy-start.6
  243.8 3.9 copy-start.4
  244.4 3.2 collective-permute-start.2
  269.2 996.6 %reduce-scatter.5.cloned.1.call-start = ((), (), s32[]{:S(2)}) async-start(), calls=%async_computation.5 | async-start | bytes 57065472 | tf_op jit(solution)/shard_map/reduce_scatter | solution.py:41
  298.8 9.3 copy-start.8
  353.7 6.0 copy-start.5
  353.7 5.9 copy-start.12
  353.7 5.9 copy-start.13
Sparse Core Ops, SparseCore 0:
  11.5 72.8 all-gather.2
  87.5 95.5 all-gather.4
  269.3 673.5 reduce-scatter.2
  949.2 316.6 reduce-scatter.4

commit v2 on v1

--- a/solution.py
+++ b/solution.py
@@ -34,12 +34,19 @@
     return out
 
 
-def scatter_packed(pieces):
+def scatter_packed(pieces, exchange=True):
     widths = [p.shape[1] for p in pieces]
     packed = jnp.concatenate(pieces, axis=1)
-    mine = lax.optimization_barrier(
-        lax.psum_scatter(packed, "fsdp", scatter_dimension=0, tiled=True)
-    )
+    if exchange:
+        n = lax.axis_size("fsdp")
+        blocks = lax.all_to_all(
+            packed.astype(jnp.bfloat16), "fsdp", 0, 0, tiled=True
+        )
+        blocks = blocks.reshape(n, blocks.shape[0] // n, blocks.shape[1])
+        mine = jnp.sum(blocks.astype(jnp.float32), axis=0)
+    else:
+        mine = lax.psum_scatter(packed, "fsdp", scatter_dimension=0, tiled=True)
+    mine = lax.optimization_barrier(mine)
     out, at = [], 0
     for w in widths:
         out.append(mine[:, at : at + w])
@@ -160,7 +167,8 @@
         d_resid + s1 * dn1 - xf * (s1 * s1 * s1) * jnp.mean(dn1 * xf, axis=-1, keepdims=True)
     )
     g_small = jnp.concatenate([g_gain1[:, None], g_gain2[:, None], g_conv], axis=1)
-    own_in, own_out, own_small = scatter_packed([g_in, g_out, pad_cols(g_small)])
+    own_in, own_out = scatter_packed([g_in, g_out])
+    (own_small,) = scatter_packed([pad_cols(g_small)], exchange=False)
     return (
         block_out,
         input_grad,

time: 1280 us -> 1180 us (0.922)
  waiting for transfers between devices: 1050 us -> 947 us
  starting transfers between devices: 5.07 us -> 32 us
    reduce_scatter x2 -> x0, waiting for transfers between devices: 899 us -> none  [scatter_packed(): lax.psum_scatter(packed, 'fsdp', scatter_dimension=0, tiled=True)]
    unnamed x4, waiting for transfers between devices: 0.07 us -> 746 us
    all_to_all x0 -> x2, waiting for transfers between devices: none -> 47.2 us  [scatter_packed(): lax.all_to_all(packed.astype(jnp.bfloat16), 'fsdp', 0, 0, tiled=True)]
    all_to_all x0 -> x2, starting transfers between devices: none -> 26.7 us  [scatter_packed(): lax.all_to_all(packed.astype(jnp.bfloat16), 'fsdp', 0, 0, tiled=True)]
    concatenate x2, other arithmetic: 49.4 us -> 26.9 us  [scatter_packed(): packed = jnp.concatenate(pieces, axis=1)]
    reshape x1 -> x0, local copies, waits for them, and re-layouts: 21.6 us -> none  [per_device(): g_down.reshape(n * per, -1)]
    concatenate x0 -> x1, local copies, waits for them, and re-layouts: none -> 17.5 us  [scatter_packed(): packed = jnp.concatenate(pieces, axis=1)]
    reduce_sum x0 -> x2, other arithmetic: none -> 14.3 us  [scatter_packed(): mine = jnp.sum(blocks.astype(jnp.float32), axis=0)]
  transfers between devices with their start and end apart: 7 -> 8, of which waited for: 5 -> 5; matrix products, arithmetic and copies ran while one was open for 9% -> 8% of each run, Pallas kernels for 0% -> 0%
where the time goes in v2:
time: 1180 us; the launch traced here: 1170 us
  waiting for transfers between devices  947 us (80%)
  matrix products  74.9 us (6%)
  other arithmetic  54 us (5%)
  local copies, waits for them, and re-layouts  51.5 us (4%)
  starting transfers between devices  32 us (3%)
  between operations  14.2 us (1%)
    unnamed x4, waiting for transfers between devices  746 us
    all_gather x2, waiting for transfers between devices, gather_packed(): full = lax.all_gather(packed, 'fsdp', axis=0, tiled=True)  153 us
    all_to_all x2, waiting for transfers between devices, scatter_packed(): lax.all_to_all(packed.astype(jnp.bfloat16), 'fsdp', 0, 0, tiled=True)  47.2 us
    concatenate x2, other arithmetic, scatter_packed(): packed = jnp.concatenate(pieces, axis=1)  26.9 us
    all_to_all x2, starting transfers between devices, scatter_packed(): lax.all_to_all(packed.astype(jnp.bfloat16), 'fsdp', 0, 0, tiled=True)  26.7 us
  transfers between devices with their start and end apart: 8, of which 5 were waited for; matrix products, arithmetic and copies ran while one was open for 8% of the time, Pallas kernels for 0%

profile of v2, /device:TPU:0, one launch (start us, length us, event | category | flops | bytes accessed | tf_op | source)
XLA Modules:
  0.0 1174.1 jit_solution(6223689876194126609)
XLA Ops:
  8.0 1.5 fusion.39
  10.6 1.6 pad_maximum_fusion.5
  16.8 67.7 %all-gather.3.cloned.1.call-done = bf16[1024,4352]{1,0:T(8,128)(2,1)} async-done(((bf16[8,4352]{1,0:T(8,128)(2,1)}), bf16[1024,4352]{1,0:T(8,128)(2,1)}) %all-gather.3.cloned.1.call-update) | async-done | bytes 8912912 | tf_op jit(solution)/shard_map/all_gather | solution.py:29
  85.9 4.0 fusion.12
  90.0 2.2 collective-permute-start
  95.2 2.3 multiply_reduce_fusion.5
  97.6 85.5 %all-gather.5.cloned.1.call-done = bf16[1024,13824]{1,0:T(8,128)(2,1)} async-done(((bf16[8,13824]{1,0:T(8,128)(2,1)}), bf16[1024,13824]{1,0:T(8,128)(2,1)}) %all-gather.5.cloned.1.call-update) | async-done | bytes 28311568 | tf_op jit(solution)/shard_map/all_gather | solution.py:29
  183.1 7.9 slice.152
  191.1 17.4 %reshape.105 = bf16[4608,1024]{1,0:T(8,128)(2,1)} reshape(bf16[1024,4608]{1,0:T(8,128)(2,1)} %slice.152) | data formatting | bytes 18874368 | tf_op jit(solution)/shard_map/reshape | solution.py:83
  208.5 6.9 convolution_bitcast_fusion
  215.4 5.1 fusion.2
  220.5 5.8 multiply_convert_fusion.1
  226.3 7.6 fusion
  234.0 5.9 multiply_reduce_fusion.3
  240.2 2.0 convert_bitcast_fusion.1
  242.2 2.4 fusion.15
  245.2 1.5 collective-permute-start.2
  249.1 4.7 convert_bitcast_fusion
  253.7 7.6 pad_maximum_fusion.1
  261.3 13.8 %all-to-all-start = ((bf16[128,8,4096]{2,1,0:T(8,128)(2,1)}), bf16[128,8,4096]{2,1,0:T(8,128)(2,1)}, u32[]{:S(2)}, u32[]{:S(2)}) async-start(bf16[128,8,4096]{2,1,0:T(8,128)(2,1)} %pad_maximum_fusion.1), calls=%async_computation | async-start | bytes 16777216 | tf_op jit(solution)/shard_map/all_to_all | solution.py:42
  275.2 5.1 convolution_convert_fusion
  280.2 17.5 %concatenate.54 = bf16[128,8,4608]{2,1,0:T(8,128)(2,1)} reshape(bf16[4608,1024]{1,0:T(8,128)(2,1)} %convolution_convert_fusion) | data formatting | bytes 18874368 | tf_op jit(solution)/shard_map/concatenate | solution.py:39
  297.7 6.4 fusion.9
  304.1 5.1 fusion.8
  309.2 19.3 %pad_maximum_fusion = bf16[128,8,13824]{2,1,0:T(8,128)(2,1)} fusion(bf16[128,8,4608]{2,1,0:T(8,128)(2,1)} %concatenate.54, bf16[128,8,4608]{2,1,0:T(8,128)(2,1)} %fusion.9, bf16[128,8,4608]{2,1,0:T(8,128)(2,1)} %fusion.8), kind=kLoop, calls=%fused_computation.1 | loop fusion | flops 84934656 | bytes 56623104 | tf_op jit(solution)/shard_map/concatenate | solution.py:39
  328.6 47.2 %all-to-all-done = bf16[128,8,4096]{2,1,0:T(8,128)(2,1)} async-done(((bf16[128,8,4096]{2,1,0:T(8,128)(2,1)}), bf16[128,8,4096]{2,1,0:T(8,128)(2,1)}, u32[]{:S(2)}, u32[]{:S(2)}) %all-to-all-start) | async-done | bytes 8388640 | tf_op jit(solution)/shard_map/all_to_all | solution.py:42
  375.8 12.9 %all-to-all-start.1 = ((bf16[128,8,13824]{2,1,0:T(8,128)(2,1)}), bf16[128,8,13824]{2,1,0:T(8,128)(2,1)}, u32[]{:S(2)}, u32[]{:S(2)}) async-start(bf16[128,8,13824]{2,1,0:T(8,128)(2,1)} %pad_maximum_fusion), calls=%async_computation.1 | async-start | bytes 56623104 | tf_op jit(solution)/shard_map/all_to_all | solution.py:42
  389.0 5.8 fusion.33
  396.2 5.8 fusion.25
  403.0 745.6 %reduce-scatter.4.cloned.1.call-done = f32[8,256]{1,0:T(8,128)} async-done(((f32[1024,256]{1,0:T(8,128)}), f32[8,256]{1,0:T(8,128)}) %reduce-scatter.4.cloned.1.call-update) | async-done | bytes 8208
  1150.5 4.6 convert_reduce_fusion.1
  1156.4 9.8 convert_reduce_fusion
  (83 shorter events, 21.5 us)
Async XLA Ops:
  7.2 77.3 %all-gather.3.cloned.1.call-start = ((), (), s32[]{:S(2)}) async-start(), calls=%async_computation.3 | async-start | bytes 8982528 | tf_op jit(solution)/shard_map/all_gather | solution.py:29
  9.5 173.6 %all-gather.5.cloned.1.call-start = ((), (), s32[]{:S(2)}) async-start(), calls=%async_computation.4 | async-start | bytes 28532736 | tf_op jit(solution)/shard_map/all_gather | solution.py:29
  12.9 2.4 collective-permute-start.1
  85.9 9.3 copy-start.2
  89.9 4.2 copy-start
  90.0 4.0 collective-permute-start
  95.2 2.3 copy-start.14
  191.1 17.4 %copy-start.3 = (bf16[128,1024]{1,0:T(8,128)(2,1)S(1)}, bf16[128,1024]{1,0:T(8,128)(2,1)}, u32[]{:S(2)}) copy-start(bf16[128,1024]{1,0:T(8,128)(2,1)} %param.21) | copy-start | bytes 786436
  226.3 7.6 copy-start.9
  226.3 7.6 copy-start.7
  233.9 6.0 copy-start.4
  234.0 6.2 copy-start.15
  239.9 4.7 copy-start.1
  239.9 4.7 copy-start.6
  245.0 3.4 copy-start.10
  245.2 3.1 collective-permute-start.2
  248.4 0.7 copy-start.12
  261.3 13.8 %copy-start.5 = (bf16[128,1024]{1,0:T(8,128)(2,1)S(1)}, bf16[128,1024]{1,0:T(8,128)(2,1)}, u32[]{:S(2)}) copy-start(bf16[128,1024]{1,0:T(8,128)(2,1)} %param.21) | copy-start | bytes 786436
  261.3 114.5 %all-to-all-start = ((bf16[128,8,4096]{2,1,0:T(8,128)(2,1)}), bf16[128,8,4096]{2,1,0:T(8,128)(2,1)}, u32[]{:S(2)}, u32[]{:S(2)}) async-start(bf16[128,8,4096]{2,1,0:T(8,128)(2,1)} %pad_maximum_fusion.1), calls=%async_computation | async-start | bytes 16777216 | tf_op jit(solution)/shard_map/all_to_all | solution.py:42
  297.7 6.4 copy-start.8
  328.5 60.5 %copy-start.11 = (bf16[128,1024]{1,0:T(8,128)(2,1)S(1)}, bf16[128,1024]{1,0:T(8,128)(2,1)}, u32[]{:S(2)}) copy-start(bf16[128,1024]{1,0:T(8,128)(2,1)} %copy-done.10) | copy-start | bytes 786436
  328.5 60.5 %copy-start.13 = (bf16[128,1024]{1,0:T(8,128)(2,1)S(1)}, bf16[128,1024]{1,0:T(8,128)(2,1)}, u32[]{:S(2)}) copy-start(bf16[128,1024]{1,0:T(8,128)(2,1)} %copy-done.12) | copy-start | bytes 786436
  375.8 780.6 %all-to-all-start.1 = ((bf16[128,8,13824]{2,1,0:T(8,128)(2,1)}), bf16[128,8,13824]{2,1,0:T(8,128)(2,1)}, u32[]{:S(2)}, u32[]{:S(2)}) async-start(bf16[128,8,13824]{2,1,0:T(8,128)(2,1)} %pad_maximum_fusion), calls=%async_computation.1 | async-start | bytes 56623104 | tf_op jit(solution)/shard_map/all_to_all | solution.py:42
  388.7 759.9 %reduce-scatter.4.cloned.1.call-start = ((), (), s32[]{:S(2)}) async-start(), calls=%async_computation.5 | async-start | bytes 1056768
  396.2 5.9 copy-start.16
Sparse Core Ops, SparseCore 0:
  11.5 72.8 all-gather.2
  87.5 95.5 all-gather.4
  396.3 752.2 reduce-scatter.3

commit v3 on v1

--- a/solution.py
+++ b/solution.py
@@ -34,12 +34,13 @@
     return out
 
 
-def scatter_packed(pieces):
+def scatter_packed(pieces, dtype=jnp.bfloat16):
     widths = [p.shape[1] for p in pieces]
     packed = jnp.concatenate(pieces, axis=1)
-    mine = lax.optimization_barrier(
-        lax.psum_scatter(packed, "fsdp", scatter_dimension=0, tiled=True)
-    )
+    n = lax.axis_size("fsdp")
+    blocks = lax.all_to_all(packed.astype(dtype), "fsdp", 0, 0, tiled=True)
+    blocks = blocks.reshape(n, blocks.shape[0] // n, blocks.shape[1])
+    mine = lax.optimization_barrier(jnp.sum(blocks.astype(jnp.float32), axis=0))
     out, at = [], 0
     for w in widths:
         out.append(mine[:, at : at + w])
@@ -160,7 +161,8 @@
         d_resid + s1 * dn1 - xf * (s1 * s1 * s1) * jnp.mean(dn1 * xf, axis=-1, keepdims=True)
     )
     g_small = jnp.concatenate([g_gain1[:, None], g_gain2[:, None], g_conv], axis=1)
-    own_in, own_out, own_small = scatter_packed([g_in, g_out, pad_cols(g_small)])
+    own_in, own_out = scatter_packed([g_in, g_out])
+    (own_small,) = scatter_packed([pad_cols(g_small)], dtype=jnp.float32)
     return (
         block_out,
         input_grad,

time: 1280 us -> 861 us (0.67)
  the two profiles are of different devices: /device:TPU:0 before, /device:TPU:12 now
where the time goes in v3:
time: 861 us; the launch traced here: 859 us
  waiting for transfers between devices  624 us (72%)
  matrix products  72.5 us (8%)
  other arithmetic  55.5 us (6%)
  local copies, waits for them, and re-layouts  50.4 us (6%)
  starting transfers between devices  42.4 us (5%)
  between operations  14.5 us (2%)
    all_to_all x3, waiting for transfers between devices, scatter_packed(): blocks = lax.all_to_all(packed.astype(dtype), 'fsdp', 0, 0, tiled=True)  470 us
    all_gather x2, waiting for transfers between devices, gather_packed(): full = lax.all_gather(packed, 'fsdp', axis=0, tiled=True)  150 us
    all_to_all x3, starting transfers between devices, scatter_packed(): blocks = lax.all_to_all(packed.astype(dtype), 'fsdp', 0, 0, tiled=True)  35.7 us
    concatenate x2, other arithmetic, scatter_packed(): packed = jnp.concatenate(pieces, axis=1)  27 us
    concatenate x1, local copies, waits for them, and re-layouts, scatter_packed(): packed = jnp.concatenate(pieces, axis=1)  17.5 us
    reshape x1, local copies, waits for them, and re-layouts, per_device(): w_down = w_down_packed.reshape(n * down_rows, width)  17.4 us
  transfers between devices with their start and end apart: 8, of which 7 were waited for; matrix products, arithmetic and copies ran while one was open for 12% of the time, Pallas kernels for 0%

profile of v3, /device:TPU:12, one launch (start us, length us, event | category | flops | bytes accessed | tf_op | source)
XLA Modules:
  0.0 859.1 jit_solution(3929256298911301965)
XLA Ops:
  12.9 1.9 collective-permute-start.1
  15.9 1.8 collective-permute-done.1
  19.2 62.8 %all-gather.3.cloned.1.call-done = bf16[1024,4352]{1,0:T(8,128)(2,1)} async-done(((bf16[8,4352]{1,0:T(8,128)(2,1)}), bf16[1024,4352]{1,0:T(8,128)(2,1)}) %all-gather.3.cloned.1.call-update) | async-done | bytes 8912912 | tf_op jit(solution)/shard_map/all_gather | solution.py:29
  83.4 4.0 fusion.12
  87.5 2.2 collective-permute-start
  93.6 2.3 multiply_reduce_fusion.5
  96.1 86.8 %all-gather.5.cloned.1.call-done = bf16[1024,13824]{1,0:T(8,128)(2,1)} async-done(((bf16[8,13824]{1,0:T(8,128)(2,1)}), bf16[1024,13824]{1,0:T(8,128)(2,1)}) %all-gather.5.cloned.1.call-update) | async-done | bytes 28311568 | tf_op jit(solution)/shard_map/all_gather | solution.py:29
  182.9 7.9 slice.152
  190.8 17.4 %reshape.109 = bf16[4608,1024]{1,0:T(8,128)(2,1)} reshape(bf16[1024,4608]{1,0:T(8,128)(2,1)} %slice.152) | data formatting | bytes 18874368 | tf_op jit(solution)/shard_map/reshape | solution.py:77
  208.3 6.9 convolution_bitcast_fusion
  215.2 5.1 fusion.2
  220.2 5.8 multiply_convert_fusion.1
  226.1 7.6 fusion
  233.8 6.0 multiply_reduce_fusion.3
  241.4 2.5 collective-permute-start.2
  245.3 3.0 fusion.33
  249.6 12.6 %all-to-all-start = ((f32[128,8,256]{2,1,0:T(8,128)}), f32[128,8,256]{2,1,0:T(8,128)}, u32[]{:S(2)}, u32[]{:S(2)}) async-start(f32[128,8,256]{2,1,0:T(8,128)} %pad_bitcast_fusion), calls=%async_computation | async-start | bytes 2097152 | tf_op jit(solution)/shard_map/all_to_all | solution.py:41
  262.2 3.0 convert_bitcast_fusion.1
  265.2 5.7 convert_bitcast_fusion
  270.9 7.7 pad_maximum_fusion.1
  278.6 10.2 %all-to-all-start.1 = ((bf16[128,8,4096]{2,1,0:T(8,128)(2,1)}), bf16[128,8,4096]{2,1,0:T(8,128)(2,1)}, u32[]{:S(2)}, u32[]{:S(2)}) async-start(bf16[128,8,4096]{2,1,0:T(8,128)(2,1)} %pad_maximum_fusion.1), calls=%async_computation.1 | async-start | bytes 16777216 | tf_op jit(solution)/shard_map/all_to_all | solution.py:41
  288.9 5.1 convolution_convert_fusion
  293.9 17.5 %concatenate.54 = bf16[128,8,4608]{2,1,0:T(8,128)(2,1)} reshape(bf16[4608,1024]{1,0:T(8,128)(2,1)} %convolution_convert_fusion) | data formatting | bytes 18874368 | tf_op jit(solution)/shard_map/concatenate | solution.py:39
  311.4 6.4 fusion.9
  317.8 5.1 fusion.8
  322.9 19.3 %pad_maximum_fusion = bf16[128,8,13824]{2,1,0:T(8,128)(2,1)} fusion(bf16[128,8,4608]{2,1,0:T(8,128)(2,1)} %concatenate.54, bf16[128,8,4608]{2,1,0:T(8,128)(2,1)} %fusion.9, bf16[128,8,4608]{2,1,0:T(8,128)(2,1)} %fusion.8), kind=kLoop, calls=%fused_computation.1 | loop fusion | flops 84934656 | bytes 56623104 | tf_op jit(solution)/shard_map/concatenate | solution.py:39
  342.2 47.3 %all-to-all-done.1 = bf16[128,8,4096]{2,1,0:T(8,128)(2,1)} async-done(((bf16[128,8,4096]{2,1,0:T(8,128)(2,1)}), bf16[128,8,4096]{2,1,0:T(8,128)(2,1)}, u32[]{:S(2)}, u32[]{:S(2)}) %all-to-all-start.1) | async-done | bytes 8388640 | tf_op jit(solution)/shard_map/all_to_all | solution.py:41
  389.5 12.9 %all-to-all-start.2 = ((bf16[128,8,13824]{2,1,0:T(8,128)(2,1)}), bf16[128,8,13824]{2,1,0:T(8,128)(2,1)}, u32[]{:S(2)}, u32[]{:S(2)}) async-start(bf16[128,8,13824]{2,1,0:T(8,128)(2,1)} %pad_maximum_fusion), calls=%async_computation.2 | async-start | bytes 56623104 | tf_op jit(solution)/shard_map/all_to_all | solution.py:41
  402.4 5.8 fusion.25
  412.0 4.6 convert_reduce_fusion.1
  417.9 423.2 %all-to-all-done.2 = bf16[128,8,13824]{2,1,0:T(8,128)(2,1)} async-done(((bf16[128,8,13824]{2,1,0:T(8,128)(2,1)}), bf16[128,8,13824]{2,1,0:T(8,128)(2,1)}, u32[]{:S(2)}, u32[]{:S(2)}) %all-to-all-start.2) | async-done | bytes 28311584 | tf_op jit(solution)/shard_map/all_to_all | solution.py:41
  841.1 9.8 %convert_reduce_fusion = f32[8,13824]{1,0:T(8,128)S(1)} fusion(bf16[128,8,13824]{2,1,0:T(8,128)(2,1)} %all-to-all-done.2), kind=kLoop, calls=%fused_computation | loop fusion | flops 28200960 | bytes 28753920 | tf_op jit(solution)/shard_map/reduce_sum | solution.py:43
  (86 shorter events, 24.4 us)
Async XLA Ops:
  7.2 74.9 %all-gather.3.cloned.1.call-start = ((), (), s32[]{:S(2)}) async-start(), calls=%async_computation.3 | async-start | bytes 8982528 | tf_op jit(solution)/shard_map/all_gather | solution.py:29
  9.5 173.4 %all-gather.5.cloned.1.call-start = ((), (), s32[]{:S(2)}) async-start(), calls=%async_computation.4 | async-start | bytes 28532736 | tf_op jit(solution)/shard_map/all_gather | solution.py:29
  12.9 4.8 collective-permute-start.1
  83.4 10.2 %copy-start.2 = (bf16[128,1024]{1,0:T(8,128)(2,1)S(1)}, bf16[128,1024]{1,0:T(8,128)(2,1)}, u32[]{:S(2)}) copy-start(bf16[128,1024]{1,0:T(8,128)(2,1)} %param.11) | copy-start | bytes 786436
  87.4 5.1 copy-start
  87.5 4.9 collective-permute-start
  93.6 2.3 copy-start.13
  190.8 17.4 %copy-start.3 = (bf16[128,1024]{1,0:T(8,128)(2,1)S(1)}, bf16[128,1024]{1,0:T(8,128)(2,1)}, u32[]{:S(2)}) copy-start(bf16[128,1024]{1,0:T(8,128)(2,1)} %param.21) | copy-start | bytes 786436
  226.1 7.7 copy-start.9
  226.1 7.7 copy-start.7
  226.1 14.0 %slice-start = ((s8[8912896]{0:T(1024)(128)(4,1)}), s8[4194304]{0:T(1024)(128)(4,1)S(1)}, s32[]{:S(2)}) async-start(s8[8912896]{0:T(1024)(128)(4,1)} %bitcast.35), calls=%async_computation.5 | async-start | bytes 8388608
  226.1 14.0 %slice-start.1 = ((s8[8912896]{0:T(1024)(128)(4,1)}), s8[4194304]{0:T(1024)(128)(4,1)S(1)}, s32[]{:S(2)}) async-start(s8[8912896]{0:T(1024)(128)(4,1)} %bitcast.35), calls=%async_computation.6 | async-start | bytes 8388608
  233.8 6.1 copy-start.4
  233.8 6.3 slice-start.2
  233.8 7.1 copy-start.1
  233.8 7.1 copy-start.6
  241.2 7.0 copy-start.10
  241.4 3.7 collective-permute-start.2
  245.3 3.0 copy-start.11
  245.3 3.0 copy-start.12
  249.6 29.0 %all-to-all-start = ((f32[128,8,256]{2,1,0:T(8,128)}), f32[128,8,256]{2,1,0:T(8,128)}, u32[]{:S(2)}, u32[]{:S(2)}) async-start(f32[128,8,256]{2,1,0:T(8,128)} %pad_bitcast_fusion), calls=%async_computation | async-start | bytes 2097152 | tf_op jit(solution)/shard_map/all_to_all | solution.py:41
  278.6 10.2 %copy-start.5 = (bf16[128,1024]{1,0:T(8,128)(2,1)S(1)}, bf16[128,1024]{1,0:T(8,128)(2,1)}, u32[]{:S(2)}) copy-start(bf16[128,1024]{1,0:T(8,128)(2,1)} %param.21) | copy-start | bytes 786436
  278.6 110.9 %all-to-all-start.1 = ((bf16[128,8,4096]{2,1,0:T(8,128)(2,1)}), bf16[128,8,4096]{2,1,0:T(8,128)(2,1)}, u32[]{:S(2)}, u32[]{:S(2)}) async-start(bf16[128,8,4096]{2,1,0:T(8,128)(2,1)} %pad_maximum_fusion.1), calls=%async_computation.1 | async-start | bytes 16777216 | tf_op jit(solution)/shard_map/all_to_all | solution.py:41
  311.4 6.4 copy-start.8
  389.5 451.6 %all-to-all-start.2 = ((bf16[128,8,13824]{2,1,0:T(8,128)(2,1)}), bf16[128,8,13824]{2,1,0:T(8,128)(2,1)}, u32[]{:S(2)}, u32[]{:S(2)}) async-start(bf16[128,8,13824]{2,1,0:T(8,128)(2,1)} %pad_maximum_fusion), calls=%async_computation.2 | async-start | bytes 56623104 | tf_op jit(solution)/shard_map/all_to_all | solution.py:41
  402.4 5.9 copy-start.14
Sparse Core Ops, SparseCore 0:
  11.5 70.4 all-gather.2
  85.1 97.7 all-gather.4

commit v4 on v3

--- a/solution.py
+++ b/solution.py
@@ -26,7 +26,7 @@
 def gather_packed(pieces):
     widths = [p.shape[1] for p in pieces]
     packed = jnp.concatenate(pieces, axis=1)
-    full = lax.all_gather(packed, "fsdp", axis=0, tiled=True)
+    full = lax.all_gather(packed, AXES, axis=0, tiled=True)
     out, at = [], 0
     for w in widths:
         out.append(full[:, at : at + w])
@@ -34,13 +34,34 @@
     return out
 
 
+AXES = ("y", "z", "x", "core")
+FSDP = AXES
+
+
+def exchange_packed(pieces, dtype=jnp.float32):
+    widths = [p.shape[1] for p in pieces]
+    packed = jnp.concatenate(pieces, axis=1)
+    n = lax.axis_size(AXES)
+    blocks = lax.all_to_all(packed.astype(dtype), AXES, 0, 0, tiled=True)
+    blocks = blocks.reshape(n, blocks.shape[0] // n, blocks.shape[1])
+    mine = lax.optimization_barrier(jnp.sum(blocks.astype(jnp.float32), axis=0))
+    out, at = [], 0
+    for w in widths:
+        out.append(mine[:, at : at + w])
+        at += w
+    return out
+
+
 def scatter_packed(pieces, dtype=jnp.bfloat16):
     widths = [p.shape[1] for p in pieces]
-    packed = jnp.concatenate(pieces, axis=1)
-    n = lax.axis_size("fsdp")
-    blocks = lax.all_to_all(packed.astype(dtype), "fsdp", 0, 0, tiled=True)
-    blocks = blocks.reshape(n, blocks.shape[0] // n, blocks.shape[1])
-    mine = lax.optimization_barrier(jnp.sum(blocks.astype(jnp.float32), axis=0))
+    packed = jnp.concatenate(pieces, axis=1).astype(dtype)
+    sizes = [lax.axis_size(a) for a in AXES]
+    per = packed.shape[0] // (sizes[0] * sizes[1] * sizes[2] * sizes[3])
+    blocks = packed.reshape(sizes + [per, packed.shape[1]])
+    blocks = blocks.transpose(3, 2, 1, 0, 4, 5).reshape(packed.shape)
+    for axis in reversed(AXES):
+        blocks = lax.psum_scatter(blocks, axis, scatter_dimension=0, tiled=True)
+    mine = lax.optimization_barrier(blocks).astype(jnp.float32)
     out, at = [], 0
     for w in widths:
         out.append(mine[:, at : at + w])
@@ -64,7 +85,7 @@
     rows = hidden_in.shape[0]
     width = hidden_in.shape[1]
     per = in_weight.shape[0]
-    n = lax.axis_size("fsdp")
+    n = lax.axis_size(AXES)
     down_rows = down_weight.shape[0]
     small = jnp.concatenate(
         [norm1_gain[:, None], norm2_gain[:, None], conv_weight], axis=1
@@ -88,7 +109,7 @@
     xv = proj[:, 2 * width :]
     bx = (bgate * xv).astype(jnp.bfloat16)
     prev_rows, prev_ids = shifted(
-        (bx[rows - 2 :], segment_ids[rows - 2 :].astype(jnp.bfloat16)), "fsdp", 1
+        (bx[rows - 2 :], segment_ids[rows - 2 :].astype(jnp.bfloat16)), AXES, 1
     )
     ext_bx = jnp.concatenate([prev_rows, bx], axis=0).astype(jnp.float32)
     ext_ids = jnp.concatenate([prev_ids.astype(jnp.int32), segment_ids], axis=0)
@@ -150,7 +171,7 @@
         d_ext = d_ext + jnp.pad(taps[:, k] * term, ((2 - k, k), (0, 0)))
         tap_cols.append(jnp.sum(term * ext_bx[2 - k : 2 - k + rows], axis=0))
     g_conv = jnp.stack(tap_cols, axis=1)
-    returned = shifted(d_ext[:2], "fsdp", -1)
+    returned = shifted(d_ext[:2], AXES, -1)
     d_bx = d_ext[2:] + jnp.pad(returned, ((rows - 2, 0), (0, 0)))
     d_proj = jnp.concatenate([d_bx * xv, d_cgate, d_bx * bgate], axis=1).astype(jnp.bfloat16)
     g_in = lax.dot_general(h, d_proj, (((0,), (0,)), ((), ())), preferred_element_type=jnp.float32)
@@ -162,7 +183,7 @@
     )
     g_small = jnp.concatenate([g_gain1[:, None], g_gain2[:, None], g_conv], axis=1)
     own_in, own_out = scatter_packed([g_in, g_out])
-    (own_small,) = scatter_packed([pad_cols(g_small)], dtype=jnp.float32)
+    (own_small,) = exchange_packed([pad_cols(g_small)])
     return (
         block_out,
         input_grad,
@@ -178,33 +199,34 @@
 
 
 def solution(mesh):
+    torus = jax.sharding.Mesh(mesh.devices.reshape(4, 4, 4, 2), AXES)
     return jax.shard_map(
         per_device,
-        mesh=mesh,
+        mesh=torus,
         in_specs=(
-            P("fsdp", None),
-            P("fsdp"),
-            P("fsdp", None),
-            P("fsdp", None),
-            P("fsdp", None),
-            P("fsdp"),
-            P("fsdp", None),
-            P("fsdp", None),
-            P("fsdp", None),
-            P("fsdp"),
-            P("fsdp", None),
+            P(FSDP, None),
+            P(FSDP),
+            P(FSDP, None),
+            P(FSDP, None),
+            P(FSDP, None),
+            P(FSDP),
+            P(FSDP, None),
+            P(FSDP, None),
+            P(FSDP, None),
+            P(FSDP),
+            P(FSDP, None),
         ),
         out_specs=(
-            P("fsdp", None),
-            P("fsdp", None),
-            P("fsdp"),
-            P("fsdp", None),
-            P("fsdp", None),
-            P("fsdp", None),
-            P("fsdp"),
-            P("fsdp", None),
-            P("fsdp", None),
-            P("fsdp", None),
+            P(FSDP, None),
+            P(FSDP, None),
+            P(FSDP),
+            P(FSDP, None),
+            P(FSDP, None),
+            P(FSDP, None),
+            P(FSDP),
+            P(FSDP, None),
+            P(FSDP, None),
+            P(FSDP, None),
         ),
         check_vma=False,
     )

time: 861 us -> 706 us (0.82)
  the two profiles are of different devices: /device:TPU:12 before, /device:TPU:0 now
where the time goes in v4:
time: 706 us; the launch traced here: 704 us
  waiting for transfers between devices  477 us (68%)
  local copies, waits for them, and re-layouts  81.8 us (12%)
  matrix products  74.9 us (11%)
  other arithmetic  41.2 us (6%)
  between operations  14.6 us (2%)
  starting transfers between devices  14.1 us (2%)
    reduce_scatter x7, waiting for transfers between devices, scatter_packed(): blocks = lax.psum_scatter(blocks, axis, scatter_dimension=0, tiled=True)  264 us
    all_gather x2, waiting for transfers between devices, gather_packed(): full = lax.all_gather(packed, AXES, axis=0, tiled=True)  153 us
    unnamed x11, waiting for transfers between devices  46.4 us
    transpose x2, local copies, waits for them, and re-layouts, scatter_packed(): blocks = blocks.transpose(3, 2, 1, 0, 4, 5).reshape(packed.shape)  27.4 us
    transpose x2, other arithmetic, scatter_packed(): blocks = blocks.transpose(3, 2, 1, 0, 4, 5).reshape(packed.shape)  27 us
    concatenate x1, local copies, waits for them, and re-layouts, scatter_packed(): packed = jnp.concatenate(pieces, axis=1).astype(dtype)  18.1 us
    reshape x1, local copies, waits for them, and re-layouts, per_device(): w_down = w_down_packed.reshape(n * down_rows, width)  17.4 us
  transfers between devices with their start and end apart: 14, of which 10 were waited for; matrix products, arithmetic and copies ran while one was open for 16% of the time, Pallas kernels for 0%

profile of v4, /device:TPU:0, one launch (start us, length us, event | category | flops | bytes accessed | tf_op | source)
XLA Modules:
  0.0 703.7 jit_solution(15180487615690648324)
XLA Ops:
  16.8 67.6 %all-gather.3.cloned.1.call-done = bf16[1024,4352]{1,0:T(8,128)(2,1)} async-done(((bf16[8,4352]{1,0:T(8,128)(2,1)}), bf16[1024,4352]{1,0:T(8,128)(2,1)}) %all-gather.3.cloned.1.call-update) | async-done | bytes 8912912 | tf_op jit(solution)/shard_map/all_gather | solution.py:29
  85.9 4.0 fusion.10
  90.0 2.2 collective-permute-start
  95.2 2.3 multiply_reduce_fusion.5
  97.6 85.5 %all-gather.5.cloned.1.call-done = bf16[1024,13824]{1,0:T(8,128)(2,1)} async-done(((bf16[8,13824]{1,0:T(8,128)(2,1)}), bf16[1024,13824]{1,0:T(8,128)(2,1)}) %all-gather.5.cloned.1.call-update) | async-done | bytes 28311568 | tf_op jit(solution)/shard_map/all_gather | solution.py:29
  183.1 7.9 %slice.152 = bf16[1024,4608]{1,0:T(8,128)(2,1)} slice(bf16[1024,13824]{1,0:T(8,128)(2,1)} %all-gather.5.cloned.1.call-done), slice={[0:1024], [9216:13824]} | slice | bytes 18874368 | tf_op jit(solution)/shard_map/slice | solution.py:32
  191.1 17.4 %reshape.109 = bf16[4608,1024]{1,0:T(8,128)(2,1)} reshape(bf16[1024,4608]{1,0:T(8,128)(2,1)} %slice.152) | data formatting | bytes 18874368 | tf_op jit(solution)/shard_map/reshape | solution.py:98
  208.5 6.9 convolution_bitcast_fusion
  215.4 5.1 fusion.2
  220.5 5.8 multiply_convert_fusion.1
  226.3 7.6 %fusion = f32[128,1024]{1,0:T(8,128)S(1)} fusion(bf16[128,4608]{1,0:T(8,128)(2,1)S(1)} %get-tuple-element.48, bf16[1024,13824]{1,0:T(8,128)(2,1)} %all-gather.5.cloned.1.call-done), kind=kOutput, calls=%fused_computation.5 | convolution fusion | flops 1207959552 | bytes 11141120 | tf_op jit(solution)/shard_map/dot_general | solution.py:152
  234.0 5.9 multiply_reduce_fusion.3
  242.2 2.4 fusion.13
  248.4 4.6 convolution_convert_fusion.3
  253.0 7.7 %maximum_bitcast_fusion.1 = bf16[2,4,4,4,8,4096]{5,4,0,1,2,3:T(8,128)(2,1)} fusion(bf16[4,4,4,2,8,1024]{5,4,3,2,1,0:T(8,128)(2,1)} %bitcast.43, bf16[4,4,4,2,8,3072]{5,4,3,2,1,0:T(8,128)(2,1)} %bitcast.42), kind=kLoop, calls=%fused_computation.4 | loop fusion | flops 16777216 | bytes 16777216 | tf_op jit(solution)/shard_map/transpose | solution.py:61
  260.8 7.8 %copy.43 = bf16[2,4,4,4,8,4096]{5,4,3,2,1,0:T(8,128)(2,1)} copy(bf16[2,4,4,4,8,4096]{5,4,0,1,2,3:T(8,128)(2,1)} %maximum_bitcast_fusion.1) | data formatting | bytes 16777216 | tf_op jit(solution)/shard_map/transpose | solution.py:61
  269.5 5.0 convolution_convert_fusion
  274.6 18.1 %concatenate.54 = bf16[4,4,4,2,8,4608]{5,4,3,2,1,0:T(8,128)(2,1)} reshape(bf16[4608,1024]{1,0:T(8,128)(2,1)} %convolution_convert_fusion) | data formatting | bytes 18874368 | tf_op jit(solution)/shard_map/concatenate | solution.py:57
  292.7 6.4 convolution_convert_fusion.1
  299.1 5.1 convolution_convert_fusion.2
  304.2 19.3 %maximum_bitcast_fusion = bf16[2,4,4,4,8,13824]{5,4,0,1,2,3:T(8,128)(2,1)} fusion(bf16[4,4,4,2,8,4608]{5,4,3,2,1,0:T(8,128)(2,1)} %concatenate.54, bf16[4,4,4,2,8,4608]{5,4,3,2,1,0:T(8,128)(2,1)} %bitcast.39, bf16[4,4,4,2,8,4608]{5,4,3,2,1,0:T(8,128)(2,1)} %bitcast.40), kind=kLoop, calls=%fused_computation | loop fusion | flops 84934656 | bytes 56623104 | tf_op jit(solution)/shard_map/transpose | solution.py:61
  323.5 19.6 %copy.44 = bf16[2,4,4,4,8,13824]{5,4,3,2,1,0:T(8,128)(2,1)} copy(bf16[2,4,4,4,8,13824]{5,4,0,1,2,3:T(8,128)(2,1)} %maximum_bitcast_fusion) | data formatting | bytes 56623104 | tf_op jit(solution)/shard_map/transpose | solution.py:61
  343.8 45.8 %reduce-scatter.26.cloned.1.call-done = bf16[512,13824]{1,0:T(8,128)(2,1)} async-done(((bf16[1024,13824]{1,0:T(8,128)(2,1)}), bf16[512,13824]{1,0:T(8,128)(2,1)}) %reduce-scatter.26.cloned.1.call-update) | async-done | bytes 14155792
  389.6 50.6 %reduce-scatter.14.cloned.1.call-done = bf16[128,4096]{1,0:T(8,128)(2,1)} async-done(((bf16[512,4096]{1,0:T(8,128)(2,1)}), bf16[128,4096]{1,0:T(8,128)(2,1)}) %reduce-scatter.14.cloned.1.call-update) | async-done | bytes 1048592 | tf_op jit(solution)/shard_map/reduce_scatter | solution.py:63
  440.3 129.2 %reduce-scatter.20.cloned.1.call-done = bf16[128,13824]{1,0:T(8,128)(2,1)} async-done(((bf16[512,13824]{1,0:T(8,128)(2,1)}), bf16[128,13824]{1,0:T(8,128)(2,1)}) %reduce-scatter.20.cloned.1.call-update) | async-done | bytes 3538960 | tf_op jit(solution)/shard_map/reduce_scatter | solution.py:63
  569.6 25.9 %reduce-scatter.16.cloned.1.call-done = bf16[32,4096]{1,0:T(8,128)(2,1)} async-done(((bf16[128,4096]{1,0:T(8,128)(2,1)}), bf16[32,4096]{1,0:T(8,128)(2,1)}) %reduce-scatter.16.cloned.1.call-update) | async-done | bytes 262160 | tf_op jit(solution)/shard_map/reduce_scatter | solution.py:63
  595.5 43.8 %reduce-scatter.22.cloned.1.call-done = bf16[32,13824]{1,0:T(8,128)(2,1)} async-done(((bf16[128,13824]{1,0:T(8,128)(2,1)}), bf16[32,13824]{1,0:T(8,128)(2,1)}) %reduce-scatter.22.cloned.1.call-update) | async-done | bytes 884752 | tf_op jit(solution)/shard_map/reduce_scatter | solution.py:63
  639.4 5.8 fusion.31
  646.5 8.8 %all-to-all-start = ((f32[128,8,256]{2,1,0:T(8,128)}), f32[128,8,256]{2,1,0:T(8,128)}, u32[]{:S(2)}, u32[]{:S(2)}) async-start(f32[128,8,256]{2,1,0:T(8,128)} %pad_bitcast_fusion), calls=%async_computation | async-start | bytes 2097152 | tf_op jit(solution)/shard_map/all_to_all | solution.py:45
  655.3 5.9 fusion.23
  662.2 11.9 %all-to-all-done = f32[128,8,256]{2,1,0:T(8,128)} async-done(((f32[128,8,256]{2,1,0:T(8,128)}), f32[128,8,256]{2,1,0:T(8,128)}, u32[]{:S(2)}, u32[]{:S(2)}) %all-to-all-start) | async-done | bytes 1048608 | tf_op jit(solution)/shard_map/all_to_all | solution.py:45
  679.6 14.9 %reduce-scatter.24.cloned.1.call-done = bf16[8,13824]{1,0:T(8,128)(2,1)} async-done(((bf16[32,13824]{1,0:T(8,128)(2,1)}), bf16[8,13824]{1,0:T(8,128)(2,1)}) %reduce-scatter.24.cloned.1.call-update) | async-done | bytes 221200 | tf_op jit(solution)/shard_map/reduce_scatter | solution.py:63
  (103 shorter events, 32.4 us)
Async XLA Ops:
  7.2 77.3 %all-gather.3.cloned.1.call-start = ((), (), s32[]{:S(2)}) async-start(), calls=%async_computation.9 | async-start | bytes 8982528 | tf_op jit(solution)/shard_map/all_gather | solution.py:29
  9.5 173.6 %all-gather.5.cloned.1.call-start = ((), (), s32[]{:S(2)}) async-start(), calls=%async_computation.10 | async-start | bytes 28532736 | tf_op jit(solution)/shard_map/all_gather | solution.py:29
  12.2 331.0 %reduce-scatter.12.cloned.1.call-start = ((), (), s32[]{:S(2)}) async-start(), calls=%async_computation.11 | async-start | bytes 12582912 | tf_op jit(solution)/shard_map/reduce_scatter | solution.py:63
  13.0 2.4 collective-permute-start.1
  85.9 9.3 %copy-start.2 = (bf16[128,1024]{1,0:T(8,128)(2,1)S(1)}, bf16[128,1024]{1,0:T(8,128)(2,1)}, u32[]{:S(2)}) copy-start(bf16[128,1024]{1,0:T(8,128)(2,1)} %param.11) | copy-start | bytes 786436
  89.9 4.2 copy-start
  90.0 4.0 collective-permute-start
  95.2 2.3 copy-start.14
  191.1 17.4 %copy-start.3 = (bf16[128,1024]{1,0:T(8,128)(2,1)S(1)}, bf16[128,1024]{1,0:T(8,128)(2,1)}, u32[]{:S(2)}) copy-start(bf16[128,1024]{1,0:T(8,128)(2,1)} %param.21) | copy-start | bytes 786436
  226.3 7.6 %copy-start.9 = (bf16[128,4608]{1,0:T(8,128)(2,1)}, bf16[128,4608]{1,0:T(8,128)(2,1)S(1)}, u32[]{:S(2)}) copy-start(bf16[128,4608]{1,0:T(8,128)(2,1)S(1)} %get-tuple-element.48) | copy-start | bytes 3538948
  226.3 7.6 %copy-start.7 = (bf16[128,4608]{1,0:T(8,128)(2,1)}, bf16[128,4608]{1,0:T(8,128)(2,1)S(1)}, u32[]{:S(2)}) copy-start(bf16[128,4608]{1,0:T(8,128)(2,1)S(1)} %get-tuple-element.47) | copy-start | bytes 3538948
  233.9 6.0 copy-start.4
  234.0 6.2 copy-start.15
  239.9 4.8 copy-start.1
  239.9 4.8 copy-start.6
  245.0 8.0 %copy-start.10 = (bf16[128,1024]{1,0:T(8,128)(2,1)}, bf16[128,1024]{1,0:T(8,128)(2,1)S(1)}, u32[]{:S(2)}) copy-start(bf16[128,1024]{1,0:T(8,128)(2,1)S(1)} %get-tuple-element.52) | copy-start | bytes 786436
  245.2 3.1 collective-permute-start.2
  248.4 4.6 copy-start.12
  268.6 0.9 copy-start.5
  268.6 120.9 %reduce-scatter.26.cloned.1.call-start = ((), (), s32[]{:S(2)}) async-start(), calls=%async_computation.18 | async-start | bytes 42467328
  292.7 6.4 copy-start.8
  343.1 97.1 %reduce-scatter.14.cloned.1.call-start = ((), (), s32[]{:S(2)}) async-start(), calls=%async_computation.12 | async-start | bytes 5242880 | tf_op jit(solution)/shard_map/reduce_scatter | solution.py:63
  343.7 225.8 %reduce-scatter.20.cloned.1.call-start = ((), (), s32[]{:S(2)}) async-start(), calls=%async_computation.15 | async-start | bytes 17694720 | tf_op jit(solution)/shard_map/reduce_scatter | solution.py:63
  389.5 249.8 %copy-start.11 = (bf16[128,1024]{1,0:T(8,128)(2,1)S(1)}, bf16[128,1024]{1,0:T(8,128)(2,1)}, u32[]{:S(2)}) copy-start(bf16[128,1024]{1,0:T(8,128)(2,1)} %copy-done.10) | copy-start | bytes 786436
  389.5 249.8 %copy-start.13 = (bf16[128,1024]{1,0:T(8,128)(2,1)S(1)}, bf16[128,1024]{1,0:T(8,128)(2,1)}, u32[]{:S(2)}) copy-start(bf16[128,1024]{1,0:T(8,128)(2,1)} %copy-done.12) | copy-start | bytes 786436
  389.6 205.9 %reduce-scatter.16.cloned.1.call-start = ((), (), s32[]{:S(2)}) async-start(), calls=%async_computation.13 | async-start | bytes 1310720 | tf_op jit(solution)/shard_map/reduce_scatter | solution.py:63
  440.3 199.0 %reduce-scatter.22.cloned.1.call-start = ((), (), s32[]{:S(2)}) async-start(), calls=%async_computation.16 | async-start | bytes 4423680 | tf_op jit(solution)/shard_map/reduce_scatter | solution.py:63
  569.6 107.3 %reduce-scatter.18.cloned.1.call-start = ((), (), s32[]{:S(2)}) async-start(), calls=%async_computation.14 | async-start | bytes 327680 | tf_op jit(solution)/shard_map/reduce_scatter | solution.py:63
  595.5 99.0 %reduce-scatter.24.cloned.1.call-start = ((), (), s32[]{:S(2)}) async-start(), calls=%async_computation.17 | async-start | bytes 1105920 | tf_op jit(solution)/shard_map/reduce_scatter | solution.py:63
  646.5 27.5 %all-to-all-start = ((f32[128,8,256]{2,1,0:T(8,128)}), f32[128,8,256]{2,1,0:T(8,128)}, u32[]{:S(2)}, u32[]{:S(2)}) async-start(f32[128,8,256]{2,1,0:T(8,128)} %pad_bitcast_fusion), calls=%async_computation | async-start | bytes 2097152 | tf_op jit(solution)/shard_map/all_to_all | solution.py:45
  655.3 5.9 copy-start.16
Sparse Core Ops, SparseCore 0:
  11.5 72.8 all-gather.2
  87.5 95.5 all-gather.4
  268.7 24.1 reduce-scatter.11
  343.2 46.2 reduce-scatter.25
  391.9 48.2 reduce-scatter.13
  442.6 126.9 reduce-scatter.19
  571.9 23.4 reduce-scatter.15
  598.0 41.2 reduce-scatter.21
  641.8 22.8 reduce-scatter.17
  667.0 27.4 reduce-scatter.23

commit v5 on v4

--- a/solution.py
+++ b/solution.py
@@ -52,15 +52,23 @@
     return out
 
 
-def scatter_packed(pieces, dtype=jnp.bfloat16):
+def scatter_packed(pieces, order=("core", "x", "z", "y"), direct=False):
     widths = [p.shape[1] for p in pieces]
-    packed = jnp.concatenate(pieces, axis=1).astype(dtype)
+    packed = jnp.concatenate(pieces, axis=1).astype(jnp.bfloat16)
     sizes = [lax.axis_size(a) for a in AXES]
-    per = packed.shape[0] // (sizes[0] * sizes[1] * sizes[2] * sizes[3])
+    count = sizes[0] * sizes[1] * sizes[2] * sizes[3]
+    per = packed.shape[0] // count
     blocks = packed.reshape(sizes + [per, packed.shape[1]])
-    blocks = blocks.transpose(3, 2, 1, 0, 4, 5).reshape(packed.shape)
-    for axis in reversed(AXES):
-        blocks = lax.psum_scatter(blocks, axis, scatter_dimension=0, tiled=True)
+    blocks = blocks.transpose([AXES.index(a) for a in order] + [4, 5])
+    blocks = blocks.reshape(packed.shape)
+    for axis in order:
+        if direct:
+            size = lax.axis_size(axis)
+            got = lax.all_to_all(blocks, axis, 0, 0, tiled=True)
+            got = got.reshape(size, got.shape[0] // size, got.shape[1])
+            blocks = jnp.sum(got.astype(jnp.float32), axis=0).astype(jnp.bfloat16)
+        else:
+            blocks = lax.psum_scatter(blocks, axis, scatter_dimension=0, tiled=True)
     mine = lax.optimization_barrier(blocks).astype(jnp.float32)
     out, at = [], 0
     for w in widths:
@@ -145,8 +153,9 @@
     )
     g_gate = lax.dot_general(h2, da, (((0,), (0,)), ((), ())), preferred_element_type=jnp.float32)
     g_up = lax.dot_general(h2, db, (((0,), (0,)), ((), ())), preferred_element_type=jnp.float32)
-    own_gate, own_up, own_down = scatter_packed(
-        [g_gate, g_up, g_down.reshape(n * per, -1)]
+    own_gate, own_up = scatter_packed([g_gate, g_up])
+    (own_down,) = scatter_packed(
+        [g_down.reshape(n * per, -1)], order=("core", "z", "y", "x"), direct=True
     )
     dh2 = lax.dot_general(da, w_gate, (((1,), (1,)), ((), ())), preferred_element_type=jnp.float32)
     dh2 = dh2 + lax.dot_general(
@@ -182,7 +191,9 @@
         d_resid + s1 * dn1 - xf * (s1 * s1 * s1) * jnp.mean(dn1 * xf, axis=-1, keepdims=True)
     )
     g_small = jnp.concatenate([g_gain1[:, None], g_gain2[:, None], g_conv], axis=1)
-    own_in, own_out = scatter_packed([g_in, g_out])
+    own_in, own_out = scatter_packed(
+        [g_in, g_out], order=("core", "y", "x", "z"), direct=True
+    )
     (own_small,) = exchange_packed([pad_cols(g_small)])
     return (
         block_out,

time: 706 us -> 607 us (0.86)
  waiting for transfers between devices: 477 us -> 307 us
  starting transfers between devices: 14.1 us -> 46.6 us
  other arithmetic: 41.2 us -> 65.6 us
  blocking collectives: 0 us -> 19.3 us
    reduce_scatter x7 -> x4, waiting for transfers between devices: 264 us -> 30.6 us  [scatter_packed(): blocks = lax.psum_scatter(blocks, axis, scatter_dimension=0, tiled=True)]
    all_to_all x0 -> x7, waiting for transfers between devices: none -> 111 us  [scatter_packed(): got = lax.all_to_all(blocks, axis, 0, 0, tiled=True)]
    unnamed x11 -> x6, waiting for transfers between devices: 46.4 us -> 1.07 us
    all_to_all x0 -> x7, starting transfers between devices: none -> 31.1 us  [scatter_packed(): got = lax.all_to_all(blocks, axis, 0, 0, tiled=True)]
    reduce_sum x0 -> x8, other arithmetic: none -> 29.5 us  [scatter_packed(): blocks = jnp.sum(got.astype(jnp.float32), axis=0).astype(jnp.bfloat16)]
    convert_element_type x0 -> x2, local copies, waits for them, and re-layouts: none -> 26.4 us  [scatter_packed(): packed = jnp.concatenate(pieces, axis=1).astype(jnp.bfloat16)]
    transpose x2 -> x1, local copies, waits for them, and re-layouts: 27.4 us -> 6.74 us  [scatter_packed(): blocks = blocks.transpose([AXES.index(a) for a in order] + [4, 5])]
    all_to_all x0 -> x1, blocking collectives: none -> 19.3 us  [scatter_packed(): got = lax.all_to_all(blocks, axis, 0, 0, tiled=True)]
  transfers between devices with their start and end apart: 14 -> 17, of which waited for: 10 -> 10; matrix products, arithmetic and copies ran while one was open for 16% -> 23% of each run, Pallas kernels for 0% -> 0%
where the time goes in v5:
time: 607 us; the launch traced here: 600 us
  waiting for transfers between devices  307 us (51%)
  local copies, waits for them, and re-layouts  76.6 us (13%)
  matrix products  70.5 us (12%)
  other arithmetic  65.6 us (11%)
  starting transfers between devices  46.6 us (8%)
  blocking collectives  19.3 us (3%)
  between operations  15.1 us (2%)
    all_gather x2, waiting for transfers between devices, gather_packed(): full = lax.all_gather(packed, AXES, axis=0, tiled=True)  153 us
    all_to_all x7, waiting for transfers between devices, scatter_packed(): got = lax.all_to_all(blocks, axis, 0, 0, tiled=True)  111 us
    all_to_all x7, starting transfers between devices, scatter_packed(): got = lax.all_to_all(blocks, axis, 0, 0, tiled=True)  31.1 us
    reduce_scatter x4, waiting for transfers between devices, scatter_packed(): blocks = lax.psum_scatter(blocks, axis, scatter_dimension=0, tiled=True)  30.6 us
    reduce_sum x8, other arithmetic, scatter_packed(): blocks = jnp.sum(got.astype(jnp.float32), axis=0).astype(jnp.bfloat16)  29.5 us
    convert_element_type x2, local copies, waits for them, and re-layouts, scatter_packed(): packed = jnp.concatenate(pieces, axis=1).astype(jnp.bfloat16)  26.4 us
    all_to_all x1, blocking collectives, scatter_packed(): got = lax.all_to_all(blocks, axis, 0, 0, tiled=True)  19.3 us
    reshape x1, local copies, waits for them, and re-layouts, per_device(): w_down = w_down_packed.reshape(n * down_rows, width)  17.5 us
  transfers between devices with their start and end apart: 17, of which 10 were waited for; matrix products, arithmetic and copies ran while one was open for 23% of the time, Pallas kernels for 0%

profile of v5, /device:TPU:0, one launch (start us, length us, event | category | flops | bytes accessed | tf_op | source)
XLA Modules:
  0.0 600.4 jit_solution(13005986473674291038)
XLA Ops:
  16.9 67.6 %all-gather.3.cloned.1.call-done = bf16[1024,4352]{1,0:T(8,128)(2,1)} async-done(((bf16[8,4352]{1,0:T(8,128)(2,1)}), bf16[1024,4352]{1,0:T(8,128)(2,1)}) %all-gather.3.cloned.1.call-update) | async-done | bytes 8912912 | tf_op jit(solution)/shard_map/all_gather | solution.py:29
  97.6 85.5 %all-gather.5.cloned.1.call-done = bf16[1024,13824]{1,0:T(8,128)(2,1)} async-done(((bf16[8,13824]{1,0:T(8,128)(2,1)}), bf16[1024,13824]{1,0:T(8,128)(2,1)}) %all-gather.5.cloned.1.call-update) | async-done | bytes 28311568 | tf_op jit(solution)/shard_map/all_gather | solution.py:29
  183.1 7.9 %slice.148 = bf16[1024,4608]{1,0:T(8,128)(2,1)} slice(bf16[1024,13824]{1,0:T(8,128)(2,1)} %all-gather.5.cloned.1.call-done), slice={[0:1024], [9216:13824]} | slice | bytes 18874368 | tf_op jit(solution)/shard_map/slice | solution.py:32
  191.1 17.5 %reshape.145 = bf16[4608,1024]{1,0:T(8,128)(2,1)} reshape(bf16[1024,4608]{1,0:T(8,128)(2,1)} %slice.148) | data formatting | bytes 18874368 | tf_op jit(solution)/shard_map/reshape | solution.py:106
  208.6 6.9 %convolution_bitcast_fusion = f32[128,4608]{1,0:T(8,128)S(1)} fusion(bf16[4608,1024]{1,0:T(8,128)(2,1)} %reshape.145, bf16[128,1024]{1,0:T(8,128)(2,1)S(1)} %copy-done.7), kind=kOutput, calls=%fused_computation.13 | convolution fusion | flops 1207959552 | bytes 12058624 | tf_op jit(solution)/shard_map/dot_general | solution.py:146
  215.5 5.1 fusion.2
  220.5 5.8 multiply_convert_fusion.1
  233.1 10.4 %maximum_bitcast_fusion = bf16[2,4,4,4,8,9216]{5,4,0,1,2,3:T(8,128)(2,1)S(1)} fusion(bf16[4,4,4,2,8,4608]{5,4,3,2,1,0:T(8,128)(2,1)S(1)} %bitcast.47, bf16[4,4,4,2,8,4608]{5,4,3,2,1,0:T(8,128)(2,1)S(1)} %bitcast.48), kind=kLoop, calls=%fused_computation | loop fusion | flops 37748736 | bytes 37748736 | tf_op jit(solution)/shard_map/transpose | solution.py:62
  243.6 6.7 %copy.58 = bf16[2,4,4,4,8,9216]{5,4,3,2,1,0:T(8,128)(2,1)} copy(bf16[2,4,4,4,8,9216]{5,4,0,1,2,3:T(8,128)(2,1)S(1)} %maximum_bitcast_fusion) | data formatting | bytes 37748736 | tf_op jit(solution)/shard_map/transpose | solution.py:62
  250.4 30.6 %reduce-scatter.5.cloned.1.call-done = bf16[512,9216]{1,0:T(8,128)(2,1)} async-done(((bf16[1024,9216]{1,0:T(8,128)(2,1)}), bf16[512,9216]{1,0:T(8,128)(2,1)}) %reduce-scatter.5.cloned.1.call-update) | async-done | bytes 9437200 | tf_op jit(solution)/shard_map/reduce_scatter | solution.py:71
  281.0 6.9 %fusion = f32[128,1024]{1,0:T(8,128)S(1)} fusion(bf16[128,4608]{1,0:T(8,128)(2,1)S(1)} %copy-done.14, bf16[1024,13824]{1,0:T(8,128)(2,1)} %all-gather.5.cloned.1.call-done), kind=kOutput, calls=%fused_computation.5 | convolution fusion | flops 1207959552 | bytes 11141120 | tf_op jit(solution)/shard_map/dot_general | solution.py:161
  287.9 6.1 %multiply_reduce_fusion.3 = (f32[1024]{0:T(1024)S(1)}, f32[128]{0:T(128)S(1)}, f32[128,1024]{1,0:T(8,128)S(1)}) fusion(f32[128,1024]{1,0:T(8,128)S(1)} %get-tuple-element.75, f32[128]{0:T(128)S(1)} %get-tuple-element.73, f32[1024]{0:T(1024)S(1)} %get-tuple-element.40, f32[128,1024]{1,0:T(8,128)S(1)} %fusion, bf16[128,4608]{1,0:T(8,128)(2,1)S(1)} %copy-done.12, ...), kind=kOutput, calls=%fused_computation.58 | convolution fusion | flops 1208875904 | bytes 12198912 | tf_op jit(solution)/shard_map/dot_general | solution.py:160
  302.3 5.0 convolution_convert_fusion
  308.3 17.5 %convert_element_type.140 = bf16[4,4,4,2,8,4608]{5,4,3,2,1,0:T(8,128)(2,1)} reshape(bf16[4608,1024]{1,0:T(8,128)(2,1)} %convolution_convert_fusion) | data formatting | bytes 18874368 | tf_op jit(solution)/shard_map/convert_element_type | solution.py:57
  325.8 8.9 %copy.59 = bf16[4,4,4,2,8,4608]{5,4,2,0,1,3:T(8,128)(2,1)} copy(bf16[4,4,4,2,8,4608]{5,4,3,2,1,0:T(8,128)(2,1)} %convert_element_type.140) | data formatting | bytes 18874368 | tf_op jit(solution)/shard_map/convert_element_type | solution.py:57
  334.7 7.4 %all-to-all-start.5 = ((bf16[2,512,4608]{2,1,0:T(8,128)(2,1)}), bf16[2,512,4608]{2,1,0:T(8,128)(2,1)}, u32[]{:S(2)}, u32[]{:S(2)}) async-start(bf16[2,512,4608]{2,1,0:T(8,128)(2,1)} %bitcast.49), calls=%async_computation.9 | async-start | bytes 18874368 | tf_op jit(solution)/shard_map/all_to_all | solution.py:67
  344.3 6.0 fusion.31
  350.5 5.5 convolution_convert_fusion.3
  356.0 7.9 %pad_maximum_fusion = bf16[4,4,4,2,8,4096]{5,4,3,2,1,0:T(8,128)(2,1)} fusion(bf16[4,4,4,2,8,1024]{5,4,3,2,1,0:T(8,128)(2,1)} %bitcast.54, bf16[4,4,4,2,8,3072]{5,4,3,2,1,0:T(8,128)(2,1)} %bitcast.51), kind=kLoop, calls=%fused_computation.4 | loop fusion | flops 16777216 | bytes 16777216 | tf_op jit(solution)/shard_map/concatenate | solution.py:57
  363.9 7.9 %copy.62 = bf16[4,4,4,2,8,4096]{5,4,1,2,0,3:T(8,128)(2,1)} copy(bf16[4,4,4,2,8,4096]{5,4,3,2,1,0:T(8,128)(2,1)} %pad_maximum_fusion) | data formatting | bytes 16777216 | tf_op jit(solution)/shard_map/concatenate | solution.py:57
  372.8 19.3 %all_to_all.81 = bf16[2,512,4096]{2,1,0:T(8,128)(2,1)} all-to-all(bf16[2,512,4096]{2,1,0:T(8,128)(2,1)} %bitcast.50), channel_id=1, replica_groups=mesh['y'=4,'z'=4,'x'=4,'core'=2] {'core'}, dimensions={0} | all-to-all | bytes 16777216 | tf_op jit(solution)/shard_map/all_to_all | solution.py:67
  392.1 10.5 %all-to-all-start = ((f32[128,8,256]{2,1,0:T(8,128)}), f32[128,8,256]{2,1,0:T(8,128)S(1)}, u32[]{:S(2)}, u32[]{:S(2)}) async-start(f32[128,8,256]{2,1,0:T(8,128)} %pad_bitcast_fusion), calls=%async_computation | async-start | bytes 2097152 | tf_op jit(solution)/shard_map/all_to_all | solution.py:45
  402.6 8.6 %reduce_sum.196 = bf16[512,4096]{1,0:T(8,128)(2,1)} reduce(bf16[2,512,4096]{2,1,0:T(8,128)(2,1)} %all_to_all.81, bf16[]{:T(256)} %constant.22.clone.1), dimensions={0}, to_apply=%region_10.11 | reduce | flops 2097152 | bytes 12582914 | tf_op jit(solution)/shard_map/reduce_sum | solution.py:69
  411.3 10.5 %all-to-all-done = f32[128,8,256]{2,1,0:T(8,128)S(1)} async-done(((f32[128,8,256]{2,1,0:T(8,128)}), f32[128,8,256]{2,1,0:T(8,128)S(1)}, u32[]{:S(2)}, u32[]{:S(2)}) %all-to-all-start) | async-done | bytes 1048608 | tf_op jit(solution)/shard_map/all_to_all | solution.py:45
  427.3 8.9 %reduce_sum.200 = bf16[512,4608]{1,0:T(8,128)(2,1)} reduce(bf16[2,512,4608]{2,1,0:T(8,128)(2,1)} %all-to-all-done.5, bf16[]{:T(256)} %constant.22.clone.1), dimensions={0}, to_apply=%region_18.19 | reduce | flops 2359296 | bytes 14155778 | tf_op jit(solution)/shard_map/reduce_sum | solution.py:69
  436.2 39.4 %all-to-all-done.2 = bf16[4,128,4096]{2,1,0:T(8,128)(2,1)} async-done(((bf16[4,128,4096]{2,1,0:T(8,128)(2,1)}), bf16[4,128,4096]{2,1,0:T(8,128)(2,1)}, u32[]{:S(2)}, u32[]{:S(2)}) %all-to-all-start.2) | async-done | bytes 4194336 | tf_op jit(solution)/shard_map/all_to_all | solution.py:67
  475.6 4.9 all-to-all-start.6
  484.9 49.4 %all-to-all-done.6 = bf16[4,128,4608]{2,1,0:T(8,128)(2,1)} async-done(((bf16[4,128,4608]{2,1,0:T(8,128)(2,1)}), bf16[4,128,4608]{2,1,0:T(8,128)(2,1)}, u32[]{:S(2)}, u32[]{:S(2)}) %all-to-all-start.6) | async-done | bytes 4718624 | tf_op jit(solution)/shard_map/all_to_all | solution.py:67
  542.2 8.9 %all-to-all-done.3 = bf16[4,32,4096]{2,1,0:T(8,128)(2,1)S(1)} async-done(((bf16[4,32,4096]{2,1,0:T(8,128)(2,1)}), bf16[4,32,4096]{2,1,0:T(8,128)(2,1)S(1)}, u32[]{:S(2)}, u32[]{:S(2)}) %all-to-all-start.3) | async-done | bytes 1048608 | tf_op jit(solution)/shard_map/all_to_all | solution.py:67
  556.2 5.8 fusion.23
  564.2 6.1 %all-to-all-done.7 = bf16[4,32,4608]{2,1,0:T(8,128)(2,1)S(1)} async-done(((bf16[4,32,4608]{2,1,0:T(8,128)(2,1)}), bf16[4,32,4608]{2,1,0:T(8,128)(2,1)S(1)}, u32[]{:S(2)}, u32[]{:S(2)}) %all-to-all-start.7) | async-done | bytes 1179680 | tf_op jit(solution)/shard_map/all_to_all | solution.py:67
  574.7 5.7 all-to-all-done.4
  (121 shorter events, 84.1 us)
Async XLA Ops:
  7.2 77.3 %all-gather.3.cloned.1.call-start = ((), (), s32[]{:S(2)}) async-start(), calls=%async_computation.13 | async-start | bytes 8982528 | tf_op jit(solution)/shard_map/all_gather | solution.py:29
  9.5 173.6 %all-gather.5.cloned.1.call-start = ((), (), s32[]{:S(2)}) async-start(), calls=%async_computation.14 | async-start | bytes 28532736 | tf_op jit(solution)/shard_map/all_gather | solution.py:29
  12.2 268.8 %reduce-scatter.5.cloned.1.call-start = ((), (), s32[]{:S(2)}) async-start(), calls=%async_computation.15 | async-start | bytes 28311552 | tf_op jit(solution)/shard_map/reduce_scatter | solution.py:71
  13.0 2.4 collective-permute-start.1
  85.9 9.3 %copy-start.5 = (bf16[128,1024]{1,0:T(8,128)(2,1)S(1)}, bf16[128,1024]{1,0:T(8,128)(2,1)}, u32[]{:S(2)}) copy-start(bf16[128,1024]{1,0:T(8,128)(2,1)} %param.11) | copy-start | bytes 786436
  90.0 4.0 collective-permute-start
  95.2 95.9 %copy-start.18 = (bf16[128,1024]{1,0:T(8,128)(2,1)}, bf16[128,1024]{1,0:T(8,128)(2,1)S(1)}, u32[]{:S(2)}) copy-start(bf16[128,1024]{1,0:T(8,128)(2,1)S(1)} %get-tuple-element.55) | copy-start | bytes 786436
  97.6 128.8 %copy-start.4 = (bf16[128,1024]{1,0:T(8,128)(2,1)}, bf16[128,1024]{1,0:T(8,128)(2,1)S(1)}, u32[]{:S(2)}) copy-start(bf16[128,1024]{1,0:T(8,128)(2,1)S(1)} %multiply_convert_fusion.6) | copy-start | bytes 786436
  191.1 17.5 %copy-start.7 = (bf16[128,1024]{1,0:T(8,128)(2,1)S(1)}, bf16[128,1024]{1,0:T(8,128)(2,1)}, u32[]{:S(2)}) copy-start(bf16[128,1024]{1,0:T(8,128)(2,1)} %param.21) | copy-start | bytes 786436
  250.3 30.6 %copy-start.14 = (bf16[128,4608]{1,0:T(8,128)(2,1)S(1)}, bf16[128,4608]{1,0:T(8,128)(2,1)}, u32[]{:S(2)}) copy-start(bf16[128,4608]{1,0:T(8,128)(2,1)} %copy-done.13) | copy-start | bytes 3538948
  250.4 176.4 %reduce-scatter.7.cloned.1.call-start = ((), (), s32[]{:S(2)}) async-start(), calls=%async_computation.16 | async-start | bytes 11796480 | tf_op jit(solution)/shard_map/reduce_scatter | solution.py:71
  281.0 6.9 %copy-start.12 = (bf16[128,4608]{1,0:T(8,128)(2,1)S(1)}, bf16[128,4608]{1,0:T(8,128)(2,1)}, u32[]{:S(2)}) copy-start(bf16[128,4608]{1,0:T(8,128)(2,1)} %copy-done.11) | copy-start | bytes 3538948
  287.9 6.1 %copy-start.8 = (bf16[128,1024]{1,0:T(8,128)(2,1)S(1)}, bf16[128,1024]{1,0:T(8,128)(2,1)}, u32[]{:S(2)}) copy-start(bf16[128,1024]{1,0:T(8,128)(2,1)} %param.21) | copy-start | bytes 786436
  287.9 8.8 %copy-start.10 = (f32[128,1024]{1,0:T(8,128)S(1)}, f32[128,1024]{1,0:T(8,128)}, u32[]{:S(2)}) copy-start(f32[128,1024]{1,0:T(8,128)} %get-tuple-element.56) | copy-start | bytes 1572868
  294.0 6.2 %copy-start.19 = (bf16[128,1024]{1,0:T(8,128)(2,1)S(1)}, bf16[128,1024]{1,0:T(8,128)(2,1)}, u32[]{:S(2)}) copy-start(bf16[128,1024]{1,0:T(8,128)(2,1)} %copy-done.18) | copy-start | bytes 786436
  298.9 43.3 %collective-permute-start.2 = (f32[2,1024]{1,0:T(2,128)S(1)}, f32[2,1024]{1,0:T(2,128)S(1)}, u32[]{:S(2)}, u32[]{:S(2)}) collective-permute-start(f32[2,1024]{1,0:T(2,128)S(1)} %pad_add_fusion.1), channel_id=1, source_target_pairs={{1,0},{2,1},{3,2},{4,3},{5,4},{6,5},{7,6},{8,7},{9,8},{10,9},{11,1... | collective-permute-start | bytes 24584 | tf_op jit(solution)/shard_map/ppermute | solution.py:14
  334.7 7.5 %copy-start.9 = (f32[130,1024]{1,0:T(8,128)S(1)}, f32[130,1024]{1,0:T(8,128)}, u32[]{:S(2)}) copy-start(f32[130,1024]{1,0:T(8,128)} %pad_add_fusion) | copy-start | bytes 1597444
  334.7 9.6 %copy-start.6 = (bf16[128,1024]{1,0:T(8,128)(2,1)S(1)}, bf16[128,1024]{1,0:T(8,128)(2,1)}, u32[]{:S(2)}) copy-start(bf16[128,1024]{1,0:T(8,128)(2,1)} %param.11) | copy-start | bytes 786436
  334.7 9.6 %copy-start.15 = (bf16[128,1024]{1,0:T(8,128)(2,1)S(1)}, bf16[128,1024]{1,0:T(8,128)(2,1)}, u32[]{:S(2)}) copy-start(bf16[128,1024]{1,0:T(8,128)(2,1)} %get-tuple-element.62) | copy-start | bytes 786436
  334.7 38.1 %all-to-all-start.5 = ((bf16[2,512,4608]{2,1,0:T(8,128)(2,1)}), bf16[2,512,4608]{2,1,0:T(8,128)(2,1)}, u32[]{:S(2)}, u32[]{:S(2)}) async-start(bf16[2,512,4608]{2,1,0:T(8,128)(2,1)} %bitcast.49), calls=%async_computation.9 | async-start | bytes 18874368 | tf_op jit(solution)/shard_map/all_to_all | solution.py:67
  343.6 6.7 %copy-start.17 = (bf16[128,1024]{1,0:T(8,128)(2,1)}, bf16[128,1024]{1,0:T(8,128)(2,1)S(1)}, u32[]{:S(2)}) copy-start(bf16[128,1024]{1,0:T(8,128)(2,1)S(1)} %get-tuple-element.61) | copy-start | bytes 786436
  392.1 29.7 %all-to-all-start = ((f32[128,8,256]{2,1,0:T(8,128)}), f32[128,8,256]{2,1,0:T(8,128)S(1)}, u32[]{:S(2)}, u32[]{:S(2)}) async-start(f32[128,8,256]{2,1,0:T(8,128)} %pad_bitcast_fusion), calls=%async_computation | async-start | bytes 2097152 | tf_op jit(solution)/shard_map/all_to_all | solution.py:45
  421.8 14.4 %copy-start.1 = (f32[128,8,256]{2,1,0:T(8,128)}, f32[128,8,256]{2,1,0:T(8,128)S(1)}, u32[]{:S(2)}) copy-start(f32[128,8,256]{2,1,0:T(8,128)S(1)} %all-to-all-done) | copy-start | bytes 3145732
  421.8 53.9 %all-to-all-start.2 = ((bf16[4,128,4096]{2,1,0:T(8,128)(2,1)}), bf16[4,128,4096]{2,1,0:T(8,128)(2,1)}, u32[]{:S(2)}, u32[]{:S(2)}) async-start(bf16[4,128,4096]{2,1,0:T(8,128)(2,1)} %bitcast.53), calls=%async_computation.2 | async-start | bytes 8388608 | tf_op jit(solution)/shard_map/all_to_all | solution.py:67
  426.7 129.0 %reduce-scatter.9.cloned.1.call-start = ((), (), s32[]{:S(2)}) async-start(), calls=%async_computation.17 | async-start | bytes 2949120 | tf_op jit(solution)/shard_map/reduce_scatter | solution.py:71
  475.6 58.6 %all-to-all-start.6 = ((bf16[4,128,4608]{2,1,0:T(8,128)(2,1)}), bf16[4,128,4608]{2,1,0:T(8,128)(2,1)}, u32[]{:S(2)}, u32[]{:S(2)}) async-start(bf16[4,128,4608]{2,1,0:T(8,128)(2,1)} %bitcast.52), calls=%async_computation.10 | async-start | bytes 9437184 | tf_op jit(solution)/shard_map/all_to_all | solution.py:67
  534.3 16.9 %all-to-all-start.3 = ((bf16[4,32,4096]{2,1,0:T(8,128)(2,1)}), bf16[4,32,4096]{2,1,0:T(8,128)(2,1)S(1)}, u32[]{:S(2)}, u32[]{:S(2)}) async-start(bf16[4,32,4096]{2,1,0:T(8,128)(2,1)} %bitcast.56), calls=%async_computation.3 | async-start | bytes 2097152 | tf_op jit(solution)/shard_map/all_to_all | solution.py:67
  552.1 18.2 %all-to-all-start.7 = ((bf16[4,32,4608]{2,1,0:T(8,128)(2,1)}), bf16[4,32,4608]{2,1,0:T(8,128)(2,1)S(1)}, u32[]{:S(2)}, u32[]{:S(2)}) async-start(bf16[4,32,4608]{2,1,0:T(8,128)(2,1)} %bitcast.55), calls=%async_computation.11 | async-start | bytes 2359296 | tf_op jit(solution)/shard_map/all_to_all | solution.py:67
  555.6 35.8 %reduce-scatter.11.cloned.1.call-start = ((), (), s32[]{:S(2)}) async-start(), calls=%async_computation.18 | async-start | bytes 737280 | tf_op jit(solution)/shard_map/reduce_scatter | solution.py:71
  562.0 23.9 %copy-start.2 = (f32[128,8,256]{2,1,0:T(8,128)S(1)}, f32[128,8,256]{2,1,0:T(8,128)}, u32[]{:S(2)}) copy-start(f32[128,8,256]{2,1,0:T(8,128)} %copy-done.1) | copy-start | bytes 3145732
  570.3 10.1 %all-to-all-start.4 = ((bf16[4,8,4096]{2,1,0:T(8,128)(2,1)}), bf16[4,8,4096]{2,1,0:T(8,128)(2,1)S(1)}, u32[]{:S(2)}, u32[]{:S(2)}) async-start(bf16[4,8,4096]{2,1,0:T(8,128)(2,1)} %bitcast.15), calls=%async_computation.4 | async-start | bytes 524288 | tf_op jit(solution)/shard_map/all_to_all | solution.py:67
  580.4 10.3 %all-to-all-start.8 = ((bf16[4,8,4608]{2,1,0:T(8,128)(2,1)}), bf16[4,8,4608]{2,1,0:T(8,128)(2,1)S(1)}, u32[]{:S(2)}, u32[]{:S(2)}) async-start(bf16[4,8,4608]{2,1,0:T(8,128)(2,1)} %bitcast.24), calls=%async_computation.12 | async-start | bytes 589824 | tf_op jit(solution)/shard_map/all_to_all | solution.py:67
  (5 other events, 11.7 us)
Sparse Core Ops, SparseCore 0:
  11.5 72.8 all-gather.2
  87.5 95.5 all-gather.4
  250.5 30.4 reduce-scatter.4
  283.3 90.3 reduce-scatter.6
  429.6 30.2 reduce-scatter.8
  558.6 20.2 reduce-scatter.10

commit v6 on v5

--- a/solution.py
+++ b/solution.py
@@ -99,9 +99,15 @@
         [norm1_gain[:, None], norm2_gain[:, None], conv_weight], axis=1
     )
     n_small = small.shape[1]
-    w_in, w_out, small_full = gather_packed([in_weight, out_weight, pad_cols(small)])
-    w_gate, w_up, w_down_packed = gather_packed(
-        [gate_weight, up_weight, down_weight.reshape(per, -1)]
+    w_in, w_out, small_full, w_gate, w_up, w_down_packed = gather_packed(
+        [
+            in_weight,
+            out_weight,
+            pad_cols(small),
+            gate_weight,
+            up_weight,
+            down_weight.reshape(per, -1),
+        ]
     )
     w_down = w_down_packed.reshape(n * down_rows, width)
     gain1 = small_full[:, 0]

time: 607 us -> 566 us (0.932)
  waiting for transfers between devices: 307 us -> 265 us
  local copies, waits for them, and re-layouts: 76.6 us -> 83.6 us
    all_gather x2 -> x1, waiting for transfers between devices: 153 us -> 110 us  [gather_packed(): full = lax.all_gather(packed, AXES, axis=0, tiled=True)]
  transfers between devices with their start and end apart: 17 -> 16, of which waited for: 10 -> 9; matrix products, arithmetic and copies ran while one was open for 23% -> 29% of each run, Pallas kernels for 0% -> 0%
where the time goes in v6:
time: 566 us; the launch traced here: 561 us
  waiting for transfers between devices  265 us (47%)
  local copies, waits for them, and re-layouts  83.6 us (15%)
  matrix products  69.5 us (12%)
  other arithmetic  61.6 us (11%)
  starting transfers between devices  47.3 us (8%)
  blocking collectives  18.9 us (3%)
  between operations  14.6 us (3%)
    all_to_all x7, waiting for transfers between devices, scatter_packed(): got = lax.all_to_all(blocks, axis, 0, 0, tiled=True)  111 us
    all_gather x1, waiting for transfers between devices, gather_packed(): full = lax.all_gather(packed, AXES, axis=0, tiled=True)  110 us
    reduce_scatter x4, waiting for transfers between devices, scatter_packed(): blocks = lax.psum_scatter(blocks, axis, scatter_dimension=0, tiled=True)  32.2 us
    all_to_all x7, starting transfers between devices, scatter_packed(): got = lax.all_to_all(blocks, axis, 0, 0, tiled=True)  31.5 us
    reduce_sum x8, other arithmetic, scatter_packed(): blocks = jnp.sum(got.astype(jnp.float32), axis=0).astype(jnp.bfloat16)  29.2 us
    convert_element_type x2, local copies, waits for them, and re-layouts, scatter_packed(): packed = jnp.concatenate(pieces, axis=1).astype(jnp.bfloat16)  26.4 us
    all_to_all x1, blocking collectives, scatter_packed(): got = lax.all_to_all(blocks, axis, 0, 0, tiled=True)  18.9 us
    reshape x1, local copies, waits for them, and re-layouts, per_device(): w_down = w_down_packed.reshape(n * down_rows, width)  17.9 us
  transfers between devices with their start and end apart: 16, of which 9 were waited for; matrix products, arithmetic and copies ran while one was open for 29% of the time, Pallas kernels for 0%

profile of v6, /device:TPU:0, one launch (start us, length us, event | category | flops | bytes accessed | tf_op | source)
XLA Modules:
  0.0 560.7 jit_solution(1354817071812724549)
XLA Ops:
  19.2 110.3 %all-gather.2.cloned.1.call-done = bf16[1024,18176]{1,0:T(8,128)(2,1)} async-done(((bf16[8,18176]{1,0:T(8,128)(2,1)}), bf16[1024,18176]{1,0:T(8,128)(2,1)}) %all-gather.2.cloned.1.call-update) | async-done | bytes 37224464 | tf_op jit(solution)/shard_map/all_gather | solution.py:29
  137.1 7.8 %slice.148 = bf16[1024,4608]{1,0:T(8,128)(2,1)} slice(bf16[1024,18176]{1,0:T(8,128)(2,1)} %all-gather.2.cloned.1.call-done), slice={[0:1024], [13568:18176]} | slice | bytes 18874368 | tf_op jit(solution)/shard_map/slice | solution.py:32
  145.0 17.9 %reshape.145 = bf16[4608,1024]{1,0:T(8,128)(2,1)} reshape(bf16[1024,4608]{1,0:T(8,128)(2,1)} %slice.148) | data formatting | bytes 18874368 | tf_op jit(solution)/shard_map/reshape | solution.py:112
  162.9 6.9 %convolution_bitcast_fusion = f32[128,4608]{1,0:T(8,128)S(1)} fusion(bf16[4608,1024]{1,0:T(8,128)(2,1)} %reshape.145, bf16[128,1024]{1,0:T(8,128)(2,1)S(1)} %copy-done.6), kind=kOutput, calls=%fused_computation.13 | convolution fusion | flops 1207959552 | bytes 12058624 | tf_op jit(solution)/shard_map/dot_general | solution.py:152
  175.3 5.1 fusion.2
  180.4 5.8 %multiply_convert_fusion.1 = (bf16[128,4608]{1,0:T(8,128)(2,1)S(1)}, bf16[128,4608]{1,0:T(8,128)(2,1)S(1)}, bf16[128,4608]{1,0:T(8,128)(2,1)S(1)}) fusion(f32[128,4608]{1,0:T(8,128)S(1)} %convolution_bitcast_fusion, f32[128,4608]{1,0:T(8,128)S(1)} %fusion.2, bf16[128,1024]{1,0:T(8,128)(2,1)S(1)} %multiply_convert_fusion.6, ...), kind=kOutput, calls=%fused_computation.20 | convolution fusion | flops 1216806912 | bytes 17956864 | tf_op jit(solution)/shard_map/dot_general | solution.py:143
  192.0 10.4 %maximum_bitcast_fusion = bf16[2,4,4,4,8,9216]{5,4,0,1,2,3:T(8,128)(2,1)S(1)} fusion(bf16[4,4,4,2,8,4608]{5,4,3,2,1,0:T(8,128)(2,1)S(1)} %bitcast.47, bf16[4,4,4,2,8,4608]{5,4,3,2,1,0:T(8,128)(2,1)S(1)} %bitcast.48), kind=kLoop, calls=%fused_computation | loop fusion | flops 37748736 | bytes 37748736 | tf_op jit(solution)/shard_map/transpose | solution.py:62
  202.4 6.7 %copy.70 = bf16[2,4,4,4,8,9216]{5,4,3,2,1,0:T(8,128)(2,1)} copy(bf16[2,4,4,4,8,9216]{5,4,0,1,2,3:T(8,128)(2,1)S(1)} %maximum_bitcast_fusion) | data formatting | bytes 37748736 | tf_op jit(solution)/shard_map/transpose | solution.py:62
  209.4 32.2 %reduce-scatter.5.cloned.1.call-done = bf16[512,9216]{1,0:T(8,128)(2,1)} async-done(((bf16[1024,9216]{1,0:T(8,128)(2,1)}), bf16[512,9216]{1,0:T(8,128)(2,1)}) %reduce-scatter.5.cloned.1.call-update) | async-done | bytes 9437200 | tf_op jit(solution)/shard_map/reduce_scatter | solution.py:71
  242.8 6.9 %fusion = f32[128,1024]{1,0:T(8,128)S(1)} fusion(bf16[128,4608]{1,0:T(8,128)(2,1)S(1)} %copy-done.13, bf16[1024,18176]{1,0:T(8,128)(2,1)} %all-gather.2.cloned.1.call-done), kind=kOutput, calls=%fused_computation.5 | convolution fusion | flops 1207959552 | bytes 11141120 | tf_op jit(solution)/shard_map/dot_general | solution.py:167
  249.7 5.9 %multiply_reduce_fusion.3 = (f32[1024]{0:T(1024)S(1)}, f32[128]{0:T(128)S(1)}, f32[128,1024]{1,0:T(8,128)S(1)}) fusion(f32[128,1024]{1,0:T(8,128)S(1)} %get-tuple-element.75, f32[128]{0:T(128)S(1)} %get-tuple-element.73, f32[1024]{0:T(1024)S(1)} %get-tuple-element.40, f32[128,1024]{1,0:T(8,128)S(1)} %fusion, bf16[128,4608]{1,0:T(8,128)(2,1)S(1)} %copy-done.11, ...), kind=kOutput, calls=%fused_computation.58 | convolution fusion | flops 1208875904 | bytes 12198912 | tf_op jit(solution)/shard_map/dot_general | solution.py:166
  264.0 5.0 convolution_convert_fusion
  270.0 17.5 %convert_element_type.140 = bf16[4,4,4,2,8,4608]{5,4,3,2,1,0:T(8,128)(2,1)} reshape(bf16[4608,1024]{1,0:T(8,128)(2,1)} %convolution_convert_fusion) | data formatting | bytes 18874368 | tf_op jit(solution)/shard_map/convert_element_type | solution.py:57
  287.5 8.9 %copy.71 = bf16[4,4,4,2,8,4608]{5,4,2,0,1,3:T(8,128)(2,1)} copy(bf16[4,4,4,2,8,4608]{5,4,3,2,1,0:T(8,128)(2,1)} %convert_element_type.140) | data formatting | bytes 18874368 | tf_op jit(solution)/shard_map/convert_element_type | solution.py:57
  296.4 7.7 %all-to-all-start.5 = ((bf16[2,512,4608]{2,1,0:T(8,128)(2,1)}), bf16[2,512,4608]{2,1,0:T(8,128)(2,1)}, u32[]{:S(2)}, u32[]{:S(2)}) async-start(bf16[2,512,4608]{2,1,0:T(8,128)(2,1)} %bitcast.49), calls=%async_computation.9 | async-start | bytes 18874368 | tf_op jit(solution)/shard_map/all_to_all | solution.py:67
  305.6 6.1 %fusion.31 = (f32[1024]{0:T(1024)S(1)}, f32[128]{0:T(128)S(1)}, f32[128,1024]{1,0:T(8,128)}) fusion(bf16[128,1024]{1,0:T(8,128)(2,1)S(1)} %copy-done.5, f32[128]{0:T(128)S(1)} %get-tuple-element.71, f32[1024]{0:T(1024)S(1)} %get-tuple-element.41, bf16[1024,18176]{1,0:T(8,128)(2,1)} %all-gather.2.cloned.1.call-done, ...), kind=kOutput, calls=%fused_computation.48 | convolution fusion | flops 808582016 | bytes 7873536 | tf_op jit(solution)/shard_map/dot_general | solution.py:193
  311.9 5.6 %convolution_convert_fusion.3 = bf16[1024,3072]{1,0:T(8,128)(2,1)} fusion(bf16[128,1024]{1,0:T(8,128)(2,1)} %copy-done.16, bf16[128,1024]{1,0:T(8,128)(2,1)S(1)} %copy-done.14, bf16[128,1024]{1,0:T(8,128)(2,1)} %copy-done.15, bf16[128,1024]{1,0:T(8,128)(2,1)S(1)} %copy-done.5, f32[1024]{0:T(1024)S(1)} %get-tuple-element.41, f32[128]{0:T(128)S(1)} %get-tuple-element.71), kind=kOutput, calls=%fused_computation.14 | convolution fusion | flops 811335680 | bytes 7344640 | tf_op jit(solution)/shard_map/dot_general | solution.py:192
  317.5 7.8 %pad_maximum_fusion = bf16[4,4,4,2,8,4096]{5,4,3,2,1,0:T(8,128)(2,1)} fusion(bf16[4,4,4,2,8,1024]{5,4,3,2,1,0:T(8,128)(2,1)} %bitcast.54, bf16[4,4,4,2,8,3072]{5,4,3,2,1,0:T(8,128)(2,1)} %bitcast.51), kind=kLoop, calls=%fused_computation.4 | loop fusion | flops 16777216 | bytes 16777216 | tf_op jit(solution)/shard_map/concatenate | solution.py:57
  325.4 7.8 %copy.74 = bf16[4,4,4,2,8,4096]{5,4,1,2,0,3:T(8,128)(2,1)} copy(bf16[4,4,4,2,8,4096]{5,4,3,2,1,0:T(8,128)(2,1)} %pad_maximum_fusion) | data formatting | bytes 16777216 | tf_op jit(solution)/shard_map/concatenate | solution.py:57
  334.3 18.9 %all_to_all.81 = bf16[2,512,4096]{2,1,0:T(8,128)(2,1)} all-to-all(bf16[2,512,4096]{2,1,0:T(8,128)(2,1)} %bitcast.50), channel_id=1, replica_groups=mesh['y'=4,'z'=4,'x'=4,'core'=2] {'core'}, dimensions={0} | all-to-all | bytes 16777216 | tf_op jit(solution)/shard_map/all_to_all | solution.py:67
  353.2 10.4 %all-to-all-start = ((f32[128,8,256]{2,1,0:T(8,128)}), f32[128,8,256]{2,1,0:T(8,128)S(1)}, u32[]{:S(2)}, u32[]{:S(2)}) async-start(f32[128,8,256]{2,1,0:T(8,128)} %pad_bitcast_fusion), calls=%async_computation | async-start | bytes 2097152 | tf_op jit(solution)/shard_map/all_to_all | solution.py:45
  363.6 8.5 %reduce_sum.196 = bf16[512,4096]{1,0:T(8,128)(2,1)} reduce(bf16[2,512,4096]{2,1,0:T(8,128)(2,1)} %all_to_all.81, bf16[]{:T(256)} %constant.22.clone.1), dimensions={0}, to_apply=%region_10.11 | reduce | flops 2097152 | bytes 12582914 | tf_op jit(solution)/shard_map/reduce_sum | solution.py:69
  372.1 10.6 %all-to-all-done = f32[128,8,256]{2,1,0:T(8,128)S(1)} async-done(((f32[128,8,256]{2,1,0:T(8,128)}), f32[128,8,256]{2,1,0:T(8,128)S(1)}, u32[]{:S(2)}, u32[]{:S(2)}) %all-to-all-start) | async-done | bytes 1048608 | tf_op jit(solution)/shard_map/all_to_all | solution.py:45
  382.8 4.8 all-to-all-start.2
  388.2 8.8 %reduce_sum.200 = bf16[512,4608]{1,0:T(8,128)(2,1)} reduce(bf16[2,512,4608]{2,1,0:T(8,128)(2,1)} %all-to-all-done.5, bf16[]{:T(256)} %constant.22.clone.1), dimensions={0}, to_apply=%region_18.19 | reduce | flops 2359296 | bytes 14155778 | tf_op jit(solution)/shard_map/reduce_sum | solution.py:69
  397.0 39.5 %all-to-all-done.2 = bf16[4,128,4096]{2,1,0:T(8,128)(2,1)} async-done(((bf16[4,128,4096]{2,1,0:T(8,128)(2,1)}), bf16[4,128,4096]{2,1,0:T(8,128)(2,1)}, u32[]{:S(2)}, u32[]{:S(2)}) %all-to-all-start.2) | async-done | bytes 4194336 | tf_op jit(solution)/shard_map/all_to_all | solution.py:67
  436.6 5.0 all-to-all-start.6
  445.8 49.4 %all-to-all-done.6 = bf16[4,128,4608]{2,1,0:T(8,128)(2,1)} async-done(((bf16[4,128,4608]{2,1,0:T(8,128)(2,1)}), bf16[4,128,4608]{2,1,0:T(8,128)(2,1)}, u32[]{:S(2)}, u32[]{:S(2)}) %all-to-all-start.6) | async-done | bytes 4718624 | tf_op jit(solution)/shard_map/all_to_all | solution.py:67
  503.1 8.9 %all-to-all-done.3 = bf16[4,32,4096]{2,1,0:T(8,128)(2,1)S(1)} async-done(((bf16[4,32,4096]{2,1,0:T(8,128)(2,1)}), bf16[4,32,4096]{2,1,0:T(8,128)(2,1)S(1)}, u32[]{:S(2)}, u32[]{:S(2)}) %all-to-all-start.3) | async-done | bytes 1048608 | tf_op jit(solution)/shard_map/all_to_all | solution.py:67
  517.2 5.8 %fusion.23 = bf16[128,1024]{1,0:T(8,128)(2,1)} fusion(f32[128,1024]{1,0:T(8,128)S(1)} %get-tuple-element.75, bf16[128,4608]{1,0:T(8,128)(2,1)S(1)} %get-tuple-element.59, bf16[4608,1024]{1,0:T(8,128)(2,1)} %reshape.145), kind=kOutput, calls=%fused_computation.32 | convolution fusion | flops 1208221696 | bytes 11403264 | tf_op jit(solution)/shard_map/dot_general | solution.py:148
  525.2 6.0 %all-to-all-done.7 = bf16[4,32,4608]{2,1,0:T(8,128)(2,1)S(1)} async-done(((bf16[4,32,4608]{2,1,0:T(8,128)(2,1)}), bf16[4,32,4608]{2,1,0:T(8,128)(2,1)S(1)}, u32[]{:S(2)}, u32[]{:S(2)}) %all-to-all-start.7) | async-done | bytes 1179680 | tf_op jit(solution)/shard_map/all_to_all | solution.py:67
  535.5 5.7 %all-to-all-done.4 = bf16[4,8,4096]{2,1,0:T(8,128)(2,1)S(1)} async-done(((bf16[4,8,4096]{2,1,0:T(8,128)(2,1)}), bf16[4,8,4096]{2,1,0:T(8,128)(2,1)S(1)}, u32[]{:S(2)}, u32[]{:S(2)}) %all-to-all-start.4) | async-done | bytes 262176 | tf_op jit(solution)/shard_map/all_to_all | solution.py:67
  (123 shorter events, 81.3 us)
Async XLA Ops:
  7.2 122.4 %all-gather.2.cloned.1.call-start = ((), (), s32[]{:S(2)}) async-start(), calls=%async_computation.13 | async-start | bytes 37515264 | tf_op jit(solution)/shard_map/all_gather | solution.py:29
  14.6 227.0 %reduce-scatter.5.cloned.1.call-start = ((), (), s32[]{:S(2)}) async-start(), calls=%async_computation.14 | async-start | bytes 28311552 | tf_op jit(solution)/shard_map/reduce_scatter | solution.py:71
  15.4 2.4 collective-permute-start.1
  134.9 36.9 %copy-start = (f32[128,3072]{1,0:T(8,128)}, f32[128,3072]{1,0:T(8,128)S(1)}, u32[]{:S(2)}) copy-start(f32[128,3072]{1,0:T(8,128)S(1)} %fusion.10) | copy-start | bytes 4718596
  135.0 36.7 %collective-permute-start = (bf16[2,1024]{1,0:T(2,128)(2,1)S(1)}, bf16[2,1024]{1,0:T(2,128)(2,1)S(1)}, u32[]{:S(2)}, u32[]{:S(2)}) collective-permute-start(bf16[2,1024]{1,0:T(2,128)(2,1)S(1)} %slice.138), channel_id=1, source_target_pairs={{0,1},{1,2},{2,3},{3,4},{4,5},{5,6},{6,7},{7,8},{8,9},{9,10},{10,1... | collective-permute-start | bytes 12296 | tf_op jit(solution)/shard_map/ppermute | solution.py:14
  145.0 17.9 %copy-start.6 = (bf16[128,1024]{1,0:T(8,128)(2,1)S(1)}, bf16[128,1024]{1,0:T(8,128)(2,1)}, u32[]{:S(2)}) copy-start(bf16[128,1024]{1,0:T(8,128)(2,1)} %param.21) | copy-start | bytes 786436
  169.8 3.1 copy-start.4
  186.2 2.9 copy-start.12
  186.2 2.9 copy-start.10
  209.2 178.8 %reduce-scatter.7.cloned.1.call-start = ((), (), s32[]{:S(2)}) async-start(), calls=%async_computation.15 | async-start | bytes 11796480 | tf_op jit(solution)/shard_map/reduce_scatter | solution.py:71
  242.8 6.9 %copy-start.11 = (bf16[128,4608]{1,0:T(8,128)(2,1)S(1)}, bf16[128,4608]{1,0:T(8,128)(2,1)}, u32[]{:S(2)}) copy-start(bf16[128,4608]{1,0:T(8,128)(2,1)} %copy-done.10) | copy-start | bytes 3538948
  249.7 5.9 %copy-start.7 = (bf16[128,1024]{1,0:T(8,128)(2,1)S(1)}, bf16[128,1024]{1,0:T(8,128)(2,1)}, u32[]{:S(2)}) copy-start(bf16[128,1024]{1,0:T(8,128)(2,1)} %param.21) | copy-start | bytes 786436
  255.6 2.7 copy-start.9
  255.9 6.0 %copy-start.18 = (bf16[128,1024]{1,0:T(8,128)(2,1)S(1)}, bf16[128,1024]{1,0:T(8,128)(2,1)}, u32[]{:S(2)}) copy-start(bf16[128,1024]{1,0:T(8,128)(2,1)} %copy-done.17) | copy-start | bytes 786436
  260.6 43.6 %collective-permute-start.2 = (f32[2,1024]{1,0:T(2,128)S(1)}, f32[2,1024]{1,0:T(2,128)S(1)}, u32[]{:S(2)}, u32[]{:S(2)}) collective-permute-start(f32[2,1024]{1,0:T(2,128)S(1)} %pad_add_fusion.1), channel_id=1, source_target_pairs={{1,0},{2,1},{3,2},{4,3},{5,4},{6,5},{7,6},{8,7},{9,8},{10,9},{11,1... | collective-permute-start | bytes 24584 | tf_op jit(solution)/shard_map/ppermute | solution.py:14
  296.4 7.8 %copy-start.8 = (f32[130,1024]{1,0:T(8,128)S(1)}, f32[130,1024]{1,0:T(8,128)}, u32[]{:S(2)}) copy-start(f32[130,1024]{1,0:T(8,128)} %pad_add_fusion) | copy-start | bytes 1597444
  296.4 9.1 %copy-start.5 = (bf16[128,1024]{1,0:T(8,128)(2,1)S(1)}, bf16[128,1024]{1,0:T(8,128)(2,1)}, u32[]{:S(2)}) copy-start(bf16[128,1024]{1,0:T(8,128)(2,1)} %param.11) | copy-start | bytes 786436
  296.4 9.1 %copy-start.14 = (bf16[128,1024]{1,0:T(8,128)(2,1)S(1)}, bf16[128,1024]{1,0:T(8,128)(2,1)}, u32[]{:S(2)}) copy-start(bf16[128,1024]{1,0:T(8,128)(2,1)} %get-tuple-element.62) | copy-start | bytes 786436
  296.4 37.8 %all-to-all-start.5 = ((bf16[2,512,4608]{2,1,0:T(8,128)(2,1)}), bf16[2,512,4608]{2,1,0:T(8,128)(2,1)}, u32[]{:S(2)}, u32[]{:S(2)}) async-start(bf16[2,512,4608]{2,1,0:T(8,128)(2,1)} %bitcast.49), calls=%async_computation.9 | async-start | bytes 18874368 | tf_op jit(solution)/shard_map/all_to_all | solution.py:67
  305.5 6.1 %copy-start.15 = (bf16[128,1024]{1,0:T(8,128)(2,1)}, bf16[128,1024]{1,0:T(8,128)(2,1)S(1)}, u32[]{:S(2)}) copy-start(bf16[128,1024]{1,0:T(8,128)(2,1)S(1)} %get-tuple-element.60) | copy-start | bytes 786436
  305.5 6.1 %copy-start.16 = (bf16[128,1024]{1,0:T(8,128)(2,1)}, bf16[128,1024]{1,0:T(8,128)(2,1)S(1)}, u32[]{:S(2)}) copy-start(bf16[128,1024]{1,0:T(8,128)(2,1)S(1)} %get-tuple-element.61) | copy-start | bytes 786436
  353.2 29.6 %all-to-all-start = ((f32[128,8,256]{2,1,0:T(8,128)}), f32[128,8,256]{2,1,0:T(8,128)S(1)}, u32[]{:S(2)}, u32[]{:S(2)}) async-start(f32[128,8,256]{2,1,0:T(8,128)} %pad_bitcast_fusion), calls=%async_computation | async-start | bytes 2097152 | tf_op jit(solution)/shard_map/all_to_all | solution.py:45
  382.8 5.4 copy-start.1
  382.8 53.8 %all-to-all-start.2 = ((bf16[4,128,4096]{2,1,0:T(8,128)(2,1)}), bf16[4,128,4096]{2,1,0:T(8,128)(2,1)}, u32[]{:S(2)}, u32[]{:S(2)}) async-start(bf16[4,128,4096]{2,1,0:T(8,128)(2,1)} %bitcast.53), calls=%async_computation.2 | async-start | bytes 8388608 | tf_op jit(solution)/shard_map/all_to_all | solution.py:67
  387.6 129.0 %reduce-scatter.9.cloned.1.call-start = ((), (), s32[]{:S(2)}) async-start(), calls=%async_computation.16 | async-start | bytes 2949120 | tf_op jit(solution)/shard_map/reduce_scatter | solution.py:71
  436.6 58.7 %all-to-all-start.6 = ((bf16[4,128,4608]{2,1,0:T(8,128)(2,1)}), bf16[4,128,4608]{2,1,0:T(8,128)(2,1)}, u32[]{:S(2)}, u32[]{:S(2)}) async-start(bf16[4,128,4608]{2,1,0:T(8,128)(2,1)} %bitcast.52), calls=%async_computation.10 | async-start | bytes 9437184 | tf_op jit(solution)/shard_map/all_to_all | solution.py:67
  495.2 16.8 %all-to-all-start.3 = ((bf16[4,32,4096]{2,1,0:T(8,128)(2,1)}), bf16[4,32,4096]{2,1,0:T(8,128)(2,1)S(1)}, u32[]{:S(2)}, u32[]{:S(2)}) async-start(bf16[4,32,4096]{2,1,0:T(8,128)(2,1)} %bitcast.56), calls=%async_computation.3 | async-start | bytes 2097152 | tf_op jit(solution)/shard_map/all_to_all | solution.py:67
  513.0 18.1 %all-to-all-start.7 = ((bf16[4,32,4608]{2,1,0:T(8,128)(2,1)}), bf16[4,32,4608]{2,1,0:T(8,128)(2,1)S(1)}, u32[]{:S(2)}, u32[]{:S(2)}) async-start(bf16[4,32,4608]{2,1,0:T(8,128)(2,1)} %bitcast.55), calls=%async_computation.11 | async-start | bytes 2359296 | tf_op jit(solution)/shard_map/all_to_all | solution.py:67
  516.6 35.7 %reduce-scatter.11.cloned.1.call-start = ((), (), s32[]{:S(2)}) async-start(), calls=%async_computation.17 | async-start | bytes 737280 | tf_op jit(solution)/shard_map/reduce_scatter | solution.py:71
  522.9 23.8 %copy-start.2 = (f32[128,8,256]{2,1,0:T(8,128)S(1)}, f32[128,8,256]{2,1,0:T(8,128)}, u32[]{:S(2)}) copy-start(f32[128,8,256]{2,1,0:T(8,128)} %copy-done.1) | copy-start | bytes 3145732
  531.1 10.1 %all-to-all-start.4 = ((bf16[4,8,4096]{2,1,0:T(8,128)(2,1)}), bf16[4,8,4096]{2,1,0:T(8,128)(2,1)S(1)}, u32[]{:S(2)}, u32[]{:S(2)}) async-start(bf16[4,8,4096]{2,1,0:T(8,128)(2,1)} %bitcast.15), calls=%async_computation.4 | async-start | bytes 524288 | tf_op jit(solution)/shard_map/all_to_all | solution.py:67
  541.2 10.3 %all-to-all-start.8 = ((bf16[4,8,4608]{2,1,0:T(8,128)(2,1)}), bf16[4,8,4608]{2,1,0:T(8,128)(2,1)S(1)}, u32[]{:S(2)}, u32[]{:S(2)}) async-start(bf16[4,8,4608]{2,1,0:T(8,128)(2,1)} %bitcast.24), calls=%async_computation.12 | async-start | bytes 589824 | tf_op jit(solution)/shard_map/all_to_all | solution.py:67
  (4 other events, 5.3 us)
Sparse Core Ops, SparseCore 0:
  14.7 114.7 all-gather.1
  209.3 32.2 reduce-scatter.4
  244.0 90.2 reduce-scatter.6
  390.6 30.2 reduce-scatter.8
  519.5 20.2 reduce-scatter.10

commit v7 on v6

--- a/solution.py
+++ b/solution.py
@@ -159,9 +159,8 @@
     )
     g_gate = lax.dot_general(h2, da, (((0,), (0,)), ((), ())), preferred_element_type=jnp.float32)
     g_up = lax.dot_general(h2, db, (((0,), (0,)), ((), ())), preferred_element_type=jnp.float32)
-    own_gate, own_up = scatter_packed([g_gate, g_up])
-    (own_down,) = scatter_packed(
-        [g_down.reshape(n * per, -1)], order=("core", "z", "y", "x"), direct=True
+    own_gate, own_up, own_down = scatter_packed(
+        [g_gate, g_up, g_down.reshape(n * per, -1)]
     )
     dh2 = lax.dot_general(da, w_gate, (((1,), (1,)), ((), ())), preferred_element_type=jnp.float32)
     dh2 = dh2 + lax.dot_general(

time: 566 us -> 625 us (1.10)
  blocking collectives: 18.9 us -> 76.8 us
  waiting for transfers between devices: 265 us -> 298 us
  starting transfers between devices: 47.3 us -> 18.8 us
  other arithmetic: 61.6 us -> 52.8 us
  matrix products: 69.5 us -> 77.9 us
    all_to_all x7 -> x2, waiting for transfers between devices: 111 us -> 10.2 us  [scatter_packed(): got = lax.all_to_all(blocks, axis, 0, 0, tiled=True)]
    reduce_scatter x4 -> x3, waiting for transfers between devices: 32.2 us -> 123 us  [scatter_packed(): blocks = lax.psum_scatter(blocks, axis, scatter_dimension=0, tiled=True)]
    all_to_all x1 -> x2, blocking collectives: 18.9 us -> 76.8 us  [scatter_packed(): got = lax.all_to_all(blocks, axis, 0, 0, tiled=True)]
    unnamed x5 -> x6, waiting for transfers between devices: 0.8 us -> 43.5 us
    convert_element_type x2 -> x0, local copies, waits for them, and re-layouts: 26.4 us -> none  [scatter_packed(): packed = jnp.concatenate(pieces, axis=1).astype(jnp.bfloat16)]
    all_to_all x7 -> x2, starting transfers between devices: 31.5 us -> 7.65 us  [scatter_packed(): got = lax.all_to_all(blocks, axis, 0, 0, tiled=True)]
    concatenate x1 -> x2, local copies, waits for them, and re-layouts: 7.78 us -> 25.3 us  [scatter_packed(): packed = jnp.concatenate(pieces, axis=1).astype(jnp.bfloat16)]
    reduce_sum x8 -> x4, other arithmetic: 29.2 us -> 15.1 us  [scatter_packed(): blocks = jnp.sum(got.astype(jnp.float32), axis=0).astype(jnp.bfloat16)]
  transfers between devices with their start and end apart: 16 -> 11, of which waited for: 9 -> 6; matrix products, arithmetic and copies ran while one was open for 29% -> 18% of each run, Pallas kernels for 0% -> 0%
where the time goes in v7:
time: 625 us; the launch traced here: 623 us
  waiting for transfers between devices  298 us (48%)
  local copies, waits for them, and re-layouts  84.7 us (14%)
  matrix products  77.9 us (12%)
  blocking collectives  76.8 us (12%)
  other arithmetic  52.8 us (8%)
  starting transfers between devices  18.8 us (3%)
  between operations  14.1 us (2%)
    reduce_scatter x3, waiting for transfers between devices, scatter_packed(): blocks = lax.psum_scatter(blocks, axis, scatter_dimension=0, tiled=True)  123 us
    all_gather x1, waiting for transfers between devices, gather_packed(): full = lax.all_gather(packed, AXES, axis=0, tiled=True)  110 us
    all_to_all x2, blocking collectives, scatter_packed(): got = lax.all_to_all(blocks, axis, 0, 0, tiled=True)  76.8 us
    unnamed x6, waiting for transfers between devices  43.5 us
    concatenate x2, local copies, waits for them, and re-layouts, scatter_packed(): packed = jnp.concatenate(pieces, axis=1).astype(jnp.bfloat16)  25.3 us
    transpose x1, local copies, waits for them, and re-layouts, scatter_packed(): blocks = blocks.transpose([AXES.index(a) for a in order] + [4, 5])  19.5 us
    transpose x1, other arithmetic, scatter_packed(): blocks = blocks.transpose([AXES.index(a) for a in order] + [4, 5])  19.5 us
    reshape x1, local copies, waits for them, and re-layouts, per_device(): w_down = w_down_packed.reshape(n * down_rows, width)  17.5 us
  transfers between devices with their start and end apart: 11, of which 6 were waited for; matrix products, arithmetic and copies ran while one was open for 18% of the time, Pallas kernels for 0%

profile of v7, /device:TPU:0, one launch (start us, length us, event | category | flops | bytes accessed | tf_op | source)
XLA Modules:
  0.0 623.0 jit_solution(18330075969767772169)
XLA Ops:
  19.2 110.3 %all-gather.2.cloned.1.call-done = bf16[1024,18176]{1,0:T(8,128)(2,1)} async-done(((bf16[8,18176]{1,0:T(8,128)(2,1)}), bf16[1024,18176]{1,0:T(8,128)(2,1)}) %all-gather.2.cloned.1.call-update) | async-done | bytes 37224464 | tf_op jit(solution)/shard_map/all_gather | solution.py:29
  130.9 3.9 fusion.10
  137.1 7.8 %slice.152 = bf16[1024,4608]{1,0:T(8,128)(2,1)} slice(bf16[1024,18176]{1,0:T(8,128)(2,1)} %all-gather.2.cloned.1.call-done), slice={[0:1024], [13568:18176]} | slice | bytes 18874368 | tf_op jit(solution)/shard_map/slice | solution.py:32
  145.0 17.5 %reshape.124 = bf16[4608,1024]{1,0:T(8,128)(2,1)} reshape(bf16[1024,4608]{1,0:T(8,128)(2,1)} %slice.152) | data formatting | bytes 18874368 | tf_op jit(solution)/shard_map/reshape | solution.py:112
  162.4 6.9 %convolution_bitcast_fusion = f32[128,4608]{1,0:T(8,128)S(1)} fusion(bf16[4608,1024]{1,0:T(8,128)(2,1)} %reshape.124, bf16[128,1024]{1,0:T(8,128)(2,1)S(1)} %copy-done.3), kind=kOutput, calls=%fused_computation.13 | convolution fusion | flops 1207959552 | bytes 12058624 | tf_op jit(solution)/shard_map/dot_general | solution.py:152
  174.8 5.1 fusion.2
  179.9 7.2 %multiply_convert_fusion.1 = (bf16[128,4608]{1,0:T(8,128)(2,1)}, bf16[128,4608]{1,0:T(8,128)(2,1)}, bf16[128,4608]{1,0:T(8,128)(2,1)S(1)}) fusion(f32[128,4608]{1,0:T(8,128)S(1)} %convolution_bitcast_fusion, f32[128,4608]{1,0:T(8,128)S(1)} %fusion.2, bf16[128,1024]{1,0:T(8,128)(2,1)S(1)} %multiply_convert_fusion.6, ...), kind=kOutput, calls=%fused_computation.20 | convolution fusion | flops 1216806912 | bytes 17956864 | tf_op jit(solution)/shard_map/dot_general | solution.py:143
  187.1 5.0 convolution_convert_fusion
  192.1 17.5 %concatenate.50 = bf16[4,4,4,2,8,4608]{5,4,3,2,1,0:T(8,128)(2,1)} reshape(bf16[4608,1024]{1,0:T(8,128)(2,1)} %convolution_convert_fusion) | data formatting | bytes 18874368 | tf_op jit(solution)/shard_map/concatenate | solution.py:57
  209.6 6.4 %convolution_convert_fusion.1 = bf16[1024,4608]{1,0:T(8,128)(2,1)} fusion(bf16[128,1024]{1,0:T(8,128)(2,1)S(1)} %multiply_convert_fusion.6, bf16[128,4608]{1,0:T(8,128)(2,1)} %get-tuple-element.58), kind=kOutput, calls=%fused_computation.2 | convolution fusion | flops 1212678144 | bytes 10878976 | tf_op jit(solution)/shard_map/dot_general | solution.py:161
  216.0 5.0 convolution_convert_fusion.2
  221.0 19.5 %maximum_bitcast_fusion = bf16[2,4,4,4,8,13824]{5,4,0,1,2,3:T(8,128)(2,1)} fusion(bf16[4,4,4,2,8,4608]{5,4,3,2,1,0:T(8,128)(2,1)} %concatenate.50, bf16[4,4,4,2,8,4608]{5,4,3,2,1,0:T(8,128)(2,1)} %bitcast.42, bf16[4,4,4,2,8,4608]{5,4,3,2,1,0:T(8,128)(2,1)} %bitcast.43), kind=kLoop, calls=%fused_computation | loop fusion | flops 84934656 | bytes 56623104 | tf_op jit(solution)/shard_map/transpose | solution.py:62
  240.5 19.5 %copy.66 = bf16[2,4,4,4,8,13824]{5,4,3,2,1,0:T(8,128)(2,1)} copy(bf16[2,4,4,4,8,13824]{5,4,0,1,2,3:T(8,128)(2,1)} %maximum_bitcast_fusion) | data formatting | bytes 56623104 | tf_op jit(solution)/shard_map/transpose | solution.py:62
  260.1 42.9 %reduce-scatter.14.cloned.1.call-done = bf16[512,13824]{1,0:T(8,128)(2,1)} async-done(((bf16[1024,13824]{1,0:T(8,128)(2,1)}), bf16[512,13824]{1,0:T(8,128)(2,1)}) %reduce-scatter.14.cloned.1.call-update) | async-done | bytes 14155792
  303.1 7.9 %fusion = f32[128,1024]{1,0:T(8,128)} fusion(bf16[128,4608]{1,0:T(8,128)(2,1)} %get-tuple-element.58, bf16[1024,18176]{1,0:T(8,128)(2,1)} %all-gather.2.cloned.1.call-done), kind=kOutput, calls=%fused_computation.5 | convolution fusion | flops 1207959552 | bytes 11141120 | tf_op jit(solution)/shard_map/dot_general | solution.py:166
  311.1 123.1 %reduce-scatter.8.cloned.1.call-done = bf16[128,13824]{1,0:T(8,128)(2,1)} async-done(((bf16[512,13824]{1,0:T(8,128)(2,1)}), bf16[128,13824]{1,0:T(8,128)(2,1)}) %reduce-scatter.8.cloned.1.call-update) | async-done | bytes 3538960 | tf_op jit(solution)/shard_map/reduce_scatter | solution.py:71
  434.2 7.4 %multiply_reduce_fusion.3 = (f32[1024]{0:T(1024)S(1)}, f32[128]{0:T(128)S(1)}, f32[128,1024]{1,0:T(8,128)S(1)}) fusion(f32[128,1024]{1,0:T(8,128)S(1)} %get-tuple-element.76, f32[128]{0:T(128)S(1)} %get-tuple-element.74, f32[1024]{0:T(1024)S(1)} %get-tuple-element.40, f32[128,1024]{1,0:T(8,128)} %fusion, bf16[128,4608]{1,0:T(8,128)(2,1)} %get-tuple-element.57, ...), kind=kOutput, calls=%fused_computation.58 | convolution fusion | flops 1208875904 | bytes 12198912 | tf_op jit(solution)/shard_map/dot_general | solution.py:165
  448.4 4.6 convolution_convert_fusion.3
  453.0 7.8 %pad_maximum_fusion = bf16[4,4,4,2,8,4096]{5,4,3,2,1,0:T(8,128)(2,1)} fusion(bf16[4,4,4,2,8,1024]{5,4,3,2,1,0:T(8,128)(2,1)} %bitcast.47, bf16[4,4,4,2,8,3072]{5,4,3,2,1,0:T(8,128)(2,1)} %bitcast.45), kind=kLoop, calls=%fused_computation.4 | loop fusion | flops 16777216 | bytes 16777216 | tf_op jit(solution)/shard_map/concatenate | solution.py:57
  460.8 7.8 %copy.69 = bf16[4,4,4,2,8,4096]{5,4,1,2,0,3:T(8,128)(2,1)} copy(bf16[4,4,4,2,8,4096]{5,4,3,2,1,0:T(8,128)(2,1)} %pad_maximum_fusion) | data formatting | bytes 16777216 | tf_op jit(solution)/shard_map/concatenate | solution.py:57
  468.6 20.0 %all_to_all.45 = bf16[2,512,4096]{2,1,0:T(8,128)(2,1)} all-to-all(bf16[2,512,4096]{2,1,0:T(8,128)(2,1)} %bitcast.44), channel_id=1, replica_groups=mesh['y'=4,'z'=4,'x'=4,'core'=2] {'core'}, dimensions={0} | all-to-all | bytes 16777216 | tf_op jit(solution)/shard_map/all_to_all | solution.py:67
  488.6 8.6 %reduce_sum.148 = bf16[512,4096]{1,0:T(8,128)(2,1)} reduce(bf16[2,512,4096]{2,1,0:T(8,128)(2,1)} %all_to_all.45, bf16[]{:T(256)} %constant.18.clone.1), dimensions={0}, to_apply=%region_10.11 | reduce | flops 2097152 | bytes 12582914 | tf_op jit(solution)/shard_map/reduce_sum | solution.py:69
  497.2 56.9 %all_to_all.46 = bf16[4,128,4096]{2,1,0:T(8,128)(2,1)} all-to-all(bf16[4,128,4096]{2,1,0:T(8,128)(2,1)} %bitcast.46), channel_id=1, replica_groups=mesh['y'=4,'z'=4,'x'=4,'core'=2] {'y'}, dimensions={0} | all-to-all | bytes 8388608 | tf_op jit(solution)/shard_map/all_to_all | solution.py:67
  554.0 4.3 reduce_sum.149
  558.3 4.2 all-to-all-start.3
  563.2 5.8 fusion.31
  570.3 7.3 %all-to-all-done.3 = bf16[4,32,4096]{2,1,0:T(8,128)(2,1)} async-done(((bf16[4,32,4096]{2,1,0:T(8,128)(2,1)}), bf16[4,32,4096]{2,1,0:T(8,128)(2,1)}, u32[]{:S(2)}, u32[]{:S(2)}) %all-to-all-start.3) | async-done | bytes 1048608 | tf_op jit(solution)/shard_map/all_to_all | solution.py:67
  577.6 6.2 all-to-all-start
  583.9 5.9 fusion.23
  591.9 10.7 %all-to-all-done = f32[128,8,256]{2,1,0:T(8,128)} async-done(((f32[128,8,256]{2,1,0:T(8,128)}), f32[128,8,256]{2,1,0:T(8,128)}, u32[]{:S(2)}, u32[]{:S(2)}) %all-to-all-start) | async-done | bytes 1048608 | tf_op jit(solution)/shard_map/all_to_all | solution.py:45
  602.6 3.4 all-to-all-start.4
  609.8 2.9 all-to-all-done.4
  (89 shorter events, 39.4 us)
Async XLA Ops:
  7.2 122.4 %all-gather.2.cloned.1.call-start = ((), (), s32[]{:S(2)}) async-start(), calls=%async_computation.9 | async-start | bytes 37515264 | tf_op jit(solution)/shard_map/all_gather | solution.py:29
  13.9 0.7 copy-start.9
  14.6 288.5 %reduce-scatter.14.cloned.1.call-start = ((), (), s32[]{:S(2)}) async-start(), calls=%async_computation.13 | async-start | bytes 42467328
  15.4 2.4 collective-permute-start.1
  134.9 36.4 %copy-start = (f32[128,3072]{1,0:T(8,128)}, f32[128,3072]{1,0:T(8,128)S(1)}, u32[]{:S(2)}) copy-start(f32[128,3072]{1,0:T(8,128)S(1)} %fusion.10) | copy-start | bytes 4718596
  135.0 36.3 %collective-permute-start = (bf16[2,1024]{1,0:T(2,128)(2,1)S(1)}, bf16[2,1024]{1,0:T(2,128)(2,1)S(1)}, u32[]{:S(2)}, u32[]{:S(2)}) collective-permute-start(bf16[2,1024]{1,0:T(2,128)(2,1)S(1)} %slice.142), channel_id=1, source_target_pairs={{0,1},{1,2},{2,3},{3,4},{4,5},{5,6},{6,7},{7,8},{8,9},{9,10},{10,1... | collective-permute-start | bytes 12296 | tf_op jit(solution)/shard_map/ppermute | solution.py:14
  145.0 17.5 %copy-start.3 = (bf16[128,1024]{1,0:T(8,128)(2,1)S(1)}, bf16[128,1024]{1,0:T(8,128)(2,1)}, u32[]{:S(2)}) copy-start(bf16[128,1024]{1,0:T(8,128)(2,1)} %param.21) | copy-start | bytes 786436
  162.4 10.0 %copy-start.2 = (bf16[128,1024]{1,0:T(8,128)(2,1)S(1)}, bf16[128,1024]{1,0:T(8,128)(2,1)}, u32[]{:S(2)}) copy-start(bf16[128,1024]{1,0:T(8,128)(2,1)} %param.11) | copy-start | bytes 786436
  172.4 7.5 %copy-start.6 = (bf16[128,1024]{1,0:T(8,128)(2,1)}, bf16[128,1024]{1,0:T(8,128)(2,1)S(1)}, u32[]{:S(2)}) copy-start(bf16[128,1024]{1,0:T(8,128)(2,1)S(1)} %get-tuple-element.55) | copy-start | bytes 786436
  209.6 6.4 %copy-start.5 = (bf16[128,4608]{1,0:T(8,128)(2,1)S(1)}, bf16[128,4608]{1,0:T(8,128)(2,1)}, u32[]{:S(2)}) copy-start(bf16[128,4608]{1,0:T(8,128)(2,1)} %get-tuple-element.57) | copy-start | bytes 3538948
  260.1 174.1 %reduce-scatter.8.cloned.1.call-start = ((), (), s32[]{:S(2)}) async-start(), calls=%async_computation.10 | async-start | bytes 17694720 | tf_op jit(solution)/shard_map/reduce_scatter | solution.py:71
  303.1 259.6 %reduce-scatter.10.cloned.1.call-start = ((), (), s32[]{:S(2)}) async-start(), calls=%async_computation.11 | async-start | bytes 4423680 | tf_op jit(solution)/shard_map/reduce_scatter | solution.py:71
  434.2 10.1 %copy-start.1 = (f32[128,3072]{1,0:T(8,128)S(1)}, f32[128,3072]{1,0:T(8,128)}, u32[]{:S(2)}) copy-start(f32[128,3072]{1,0:T(8,128)} %copy-done) | copy-start | bytes 4718596
  434.2 10.1 %copy-start.4 = (f32[128,1024]{1,0:T(8,128)S(1)}, f32[128,1024]{1,0:T(8,128)}, u32[]{:S(2)}) copy-start(f32[128,1024]{1,0:T(8,128)} %get-tuple-element.56) | copy-start | bytes 1572868
  441.6 4.5 copy-start.7
  444.8 3.5 collective-permute-start.2
  558.3 19.3 %all-to-all-start.3 = ((bf16[4,32,4096]{2,1,0:T(8,128)(2,1)}), bf16[4,32,4096]{2,1,0:T(8,128)(2,1)}, u32[]{:S(2)}, u32[]{:S(2)}) async-start(bf16[4,32,4096]{2,1,0:T(8,128)(2,1)} %bitcast.48), calls=%async_computation.3 | async-start | bytes 2097152 | tf_op jit(solution)/shard_map/all_to_all | solution.py:67
  562.6 51.4 %reduce-scatter.12.cloned.1.call-start = ((), (), s32[]{:S(2)}) async-start(), calls=%async_computation.12 | async-start | bytes 1105920 | tf_op jit(solution)/shard_map/reduce_scatter | solution.py:71
  577.6 24.9 %all-to-all-start = ((f32[128,8,256]{2,1,0:T(8,128)}), f32[128,8,256]{2,1,0:T(8,128)}, u32[]{:S(2)}, u32[]{:S(2)}) async-start(f32[128,8,256]{2,1,0:T(8,128)} %pad_bitcast_fusion), calls=%async_computation | async-start | bytes 2097152 | tf_op jit(solution)/shard_map/all_to_all | solution.py:45
  583.9 22.1 %copy-start.8 = (f32[128,1024]{1,0:T(8,128)S(1)}, f32[128,1024]{1,0:T(8,128)}, u32[]{:S(2)}) copy-start(f32[128,1024]{1,0:T(8,128)} %get-tuple-element.78) | copy-start | bytes 1572868
  602.6 10.1 %all-to-all-start.4 = ((bf16[4,8,4096]{2,1,0:T(8,128)(2,1)}), bf16[4,8,4096]{2,1,0:T(8,128)(2,1)S(1)}, u32[]{:S(2)}, u32[]{:S(2)}) async-start(bf16[4,8,4096]{2,1,0:T(8,128)(2,1)} %bitcast.15), calls=%async_computation.4 | async-start | bytes 524288 | tf_op jit(solution)/shard_map/all_to_all | solution.py:67
Sparse Core Ops, SparseCore 0:
  14.7 114.7 all-gather.1
  260.2 42.8 reduce-scatter.13
  305.5 128.5 reduce-scatter.7
  436.4 41.4 reduce-scatter.9
  565.5 29.4 reduce-scatter.11

commit v8 on v6

--- a/solution.py
+++ b/solution.py
@@ -1,6 +1,8 @@
 import jax
 import jax.numpy as jnp
 from jax import lax
+from jax.experimental import pallas as pl
+from jax.experimental.pallas import tpu as pltpu
 from jax.sharding import PartitionSpec as P
 
 CONV = 3
@@ -52,7 +54,43 @@
     return out
 
 
-def scatter_packed(pieces, order=("core", "x", "z", "y"), direct=False):
+def pair_kernel(x_ref, o_ref, send_sem, recv_sem):
+    other = 1 - lax.axis_index("core")
+    partner = (lax.axis_index("y"), lax.axis_index("z"), lax.axis_index("x"), other)
+    barrier = pltpu.get_barrier_semaphore()
+    pl.semaphore_signal(
+        barrier, inc=1, device_id=partner, device_id_type=pl.DeviceIdType.MESH
+    )
+    pl.semaphore_wait(barrier, 1)
+    copy = pltpu.make_async_remote_copy(
+        src_ref=x_ref.at[other],
+        dst_ref=o_ref,
+        send_sem=send_sem,
+        recv_sem=recv_sem,
+        device_id=partner,
+        device_id_type=pl.DeviceIdType.MESH,
+    )
+    copy.start()
+    copy.wait()
+
+
+def pair_exchange(blocks, collective_id):
+    halves = blocks.reshape(2, blocks.shape[0] // 2, blocks.shape[1])
+    received = pl.pallas_call(
+        pair_kernel,
+        out_shape=jax.ShapeDtypeStruct(halves.shape[1:], halves.dtype),
+        in_specs=[pl.BlockSpec(memory_space=pl.ANY)],
+        out_specs=pl.BlockSpec(memory_space=pl.ANY),
+        scratch_shapes=[pltpu.SemaphoreType.DMA(()), pltpu.SemaphoreType.DMA(())],
+        compiler_params=pltpu.CompilerParams(
+            collective_id=collective_id, has_side_effects=True
+        ),
+    )(halves)
+    own = lax.dynamic_index_in_dim(halves, lax.axis_index("core"), 0, keepdims=False)
+    return (own.astype(jnp.float32) + received.astype(jnp.float32)).astype(jnp.bfloat16)
+
+
+def scatter_packed(pieces, order=("core", "x", "z", "y"), direct=False, collective_id=0):
     widths = [p.shape[1] for p in pieces]
     packed = jnp.concatenate(pieces, axis=1).astype(jnp.bfloat16)
     sizes = [lax.axis_size(a) for a in AXES]
@@ -62,7 +100,9 @@
     blocks = blocks.transpose([AXES.index(a) for a in order] + [4, 5])
     blocks = blocks.reshape(packed.shape)
     for axis in order:
-        if direct:
+        if direct and axis == "core":
+            blocks = pair_exchange(blocks, collective_id)
+        elif direct:
             size = lax.axis_size(axis)
             got = lax.all_to_all(blocks, axis, 0, 0, tiled=True)
             got = got.reshape(size, got.shape[0] // size, got.shape[1])
@@ -161,7 +201,10 @@
     g_up = lax.dot_general(h2, db, (((0,), (0,)), ((), ())), preferred_element_type=jnp.float32)
     own_gate, own_up = scatter_packed([g_gate, g_up])
     (own_down,) = scatter_packed(
-        [g_down.reshape(n * per, -1)], order=("core", "z", "y", "x"), direct=True
+        [g_down.reshape(n * per, -1)],
+        order=("core", "z", "y", "x"),
+        direct=True,
+        collective_id=1,
     )
     dh2 = lax.dot_general(da, w_gate, (((1,), (1,)), ((), ())), preferred_element_type=jnp.float32)
     dh2 = dh2 + lax.dot_general(
@@ -198,7 +241,7 @@
     )
     g_small = jnp.concatenate([g_gain1[:, None], g_gain2[:, None], g_conv], axis=1)
     own_in, own_out = scatter_packed(
-        [g_in, g_out], order=("core", "y", "x", "z"), direct=True
+        [g_in, g_out], order=("core", "y", "x", "z"), direct=True, collective_id=2
     )
     (own_small,) = exchange_packed([pad_cols(g_small)])
     return (

time: 566 us -> 528 us (0.933)
  waiting for transfers between devices: 265 us -> 238 us
  blocking collectives: 18.9 us -> 0 us
  Pallas kernels: 0 us -> 15.8 us
  other arithmetic: 61.6 us -> 55 us
    all_to_all x1 -> x0, blocking collectives: 18.9 us -> none  [scatter_packed(): got = lax.all_to_all(blocks, axis, 0, 0, tiled=True)]
    reduce_sum x8 -> x6, other arithmetic: 29.2 us -> 12 us  [scatter_packed(): blocks = jnp.sum(got.astype(jnp.float32), axis=0).astype(jnp.bfloat16)]
    all_to_all x7 -> x6, waiting for transfers between devices: 111 us -> 94.5 us  [scatter_packed(): got = lax.all_to_all(blocks, axis, 0, 0, tiled=True)]
    pallas_call x0 -> x2, Pallas kernels: none -> 15.8 us  [pair_exchange(): pl.pallas_call(pair_kernel, out_shape=jax.ShapeDtypeStruct(halves.shape[1...]
    convert_element_type x0 -> x2, other arithmetic: none -> 14.5 us  [pair_exchange(): (own.astype(jnp.float32) + received.astype(jnp.float32)).astype(jnp.bfloa...]
    all_to_all x1, waiting for transfers between devices: 10.6 us -> 0.01 us  [exchange_packed(): blocks = lax.all_to_all(packed.astype(dtype), AXES, 0, 0, tiled=True)]
    all_to_all x7 -> x6, starting transfers between devices: 31.5 us -> 25.5 us  [scatter_packed(): got = lax.all_to_all(blocks, axis, 0, 0, tiled=True)]
  transfers between devices with their start and end apart: 16 -> 15, of which waited for: 9 -> 8; matrix products, arithmetic and copies ran while one was open for 29% -> 30% of each run, Pallas kernels for 0% -> 3%
where the time goes in v8:
time: 528 us; the launch traced here: 523 us
  waiting for transfers between devices  238 us (45%)
  local copies, waits for them, and re-layouts  83.2 us (16%)
  matrix products  70.6 us (13%)
  other arithmetic  55 us (10%)
  starting transfers between devices  46.3 us (9%)
  Pallas kernels  15.8 us (3%)
  between operations  14.5 us (3%)
    all_gather x1, waiting for transfers between devices, gather_packed(): full = lax.all_gather(packed, AXES, axis=0, tiled=True)  110 us
    all_to_all x6, waiting for transfers between devices, scatter_packed(): got = lax.all_to_all(blocks, axis, 0, 0, tiled=True)  94.5 us
    reduce_scatter x4, waiting for transfers between devices, scatter_packed(): blocks = lax.psum_scatter(blocks, axis, scatter_dimension=0, tiled=True)  32.2 us
    convert_element_type x2, local copies, waits for them, and re-layouts, scatter_packed(): packed = jnp.concatenate(pieces, axis=1).astype(jnp.bfloat16)  26.2 us
    all_to_all x6, starting transfers between devices, scatter_packed(): got = lax.all_to_all(blocks, axis, 0, 0, tiled=True)  25.5 us
    reshape x1, local copies, waits for them, and re-layouts, per_device(): w_down = w_down_packed.reshape(n * down_rows, width)  17.9 us
    pallas_call x2, Pallas kernels, pair_exchange(): pl.pallas_call(pair_kernel, out_shape=jax.ShapeDtypeStruct(halves.shape[1...  15.8 us
    all_to_all x1, starting transfers between devices, exchange_packed(): blocks = lax.all_to_all(packed.astype(dtype), AXES, 0, 0, tiled=True)  15.4 us
  transfers between devices with their start and end apart: 15, of which 8 were waited for; matrix products, arithmetic and copies ran while one was open for 30% of the time, Pallas kernels for 3%

profile of v8, /device:TPU:0, one launch (start us, length us, event | category | flops | bytes accessed | tf_op | source)
XLA Modules:
  0.0 523.1 jit_solution(9422111549333430655)
XLA Ops:
  19.2 110.3 %all-gather.2.cloned.1.call-done = bf16[1024,18176]{1,0:T(8,128)(2,1)} async-done(((bf16[8,18176]{1,0:T(8,128)(2,1)}), bf16[1024,18176]{1,0:T(8,128)(2,1)}) %all-gather.2.cloned.1.call-update) | async-done | bytes 37224464 | tf_op jit(solution)/shard_map/all_gather | solution.py:31
  137.1 7.8 %slice.148 = bf16[1024,4608]{1,0:T(8,128)(2,1)} slice(bf16[1024,18176]{1,0:T(8,128)(2,1)} %all-gather.2.cloned.1.call-done), slice={[0:1024], [13568:18176]} | slice | bytes 18874368 | tf_op jit(solution)/shard_map/slice | solution.py:34
  145.0 17.9 %reshape.137 = bf16[4608,1024]{1,0:T(8,128)(2,1)} reshape(bf16[1024,4608]{1,0:T(8,128)(2,1)} %slice.148) | data formatting | bytes 18874368 | tf_op jit(solution)/shard_map/reshape | solution.py:152
  162.8 6.9 %convolution_bitcast_fusion = f32[128,4608]{1,0:T(8,128)S(1)} fusion(bf16[4608,1024]{1,0:T(8,128)(2,1)} %reshape.137, bf16[128,1024]{1,0:T(8,128)(2,1)S(1)} %copy-done.7), kind=kOutput, calls=%fused_computation.17 | convolution fusion | flops 1207959552 | bytes 12058624 | tf_op jit(solution)/shard_map/dot_general | solution.py:192
  175.2 5.1 fusion.4
  180.3 5.8 %multiply_convert_fusion.1 = (bf16[128,4608]{1,0:T(8,128)(2,1)S(1)}, bf16[128,4608]{1,0:T(8,128)(2,1)S(1)}, bf16[128,4608]{1,0:T(8,128)(2,1)S(1)}) fusion(f32[128,4608]{1,0:T(8,128)S(1)} %convolution_bitcast_fusion, f32[128,4608]{1,0:T(8,128)S(1)} %fusion.4, bf16[128,1024]{1,0:T(8,128)(2,1)S(1)} %multiply_convert_fusion.6, ...), kind=kOutput, calls=%fused_computation.24 | convolution fusion | flops 1216806912 | bytes 17956864 | tf_op jit(solution)/shard_map/dot_general | solution.py:183
  191.9 10.4 %maximum_bitcast_fusion = bf16[2,4,4,4,8,9216]{5,4,0,1,2,3:T(8,128)(2,1)S(1)} fusion(bf16[4,4,4,2,8,4608]{5,4,3,2,1,0:T(8,128)(2,1)S(1)} %bitcast.57, bf16[4,4,4,2,8,4608]{5,4,3,2,1,0:T(8,128)(2,1)S(1)} %bitcast.58), kind=kLoop, calls=%fused_computation | loop fusion | flops 37748736 | bytes 37748736 | tf_op jit(solution)/shard_map/transpose | solution.py:100
  202.4 6.7 %copy.73 = bf16[2,4,4,4,8,9216]{5,4,3,2,1,0:T(8,128)(2,1)} copy(bf16[2,4,4,4,8,9216]{5,4,0,1,2,3:T(8,128)(2,1)S(1)} %maximum_bitcast_fusion) | data formatting | bytes 37748736 | tf_op jit(solution)/shard_map/transpose | solution.py:100
  209.3 32.2 %reduce-scatter.5.cloned.1.call-done = bf16[512,9216]{1,0:T(8,128)(2,1)} async-done(((bf16[1024,9216]{1,0:T(8,128)(2,1)}), bf16[512,9216]{1,0:T(8,128)(2,1)}) %reduce-scatter.5.cloned.1.call-update) | async-done | bytes 9437200 | tf_op jit(solution)/shard_map/reduce_scatter | solution.py:111
  242.8 6.8 %fusion.2 = f32[128,1024]{1,0:T(8,128)S(1)} fusion(bf16[128,4608]{1,0:T(8,128)(2,1)S(1)} %copy-done.13, bf16[1024,18176]{1,0:T(8,128)(2,1)} %all-gather.2.cloned.1.call-done), kind=kOutput, calls=%fused_computation.9 | convolution fusion | flops 1207959552 | bytes 11141120 | tf_op jit(solution)/shard_map/dot_general | solution.py:210
  249.7 5.9 %multiply_reduce_fusion.3 = (f32[1024]{0:T(1024)S(1)}, f32[128]{0:T(128)S(1)}, f32[128,1024]{1,0:T(8,128)S(1)}) fusion(f32[128,1024]{1,0:T(8,128)S(1)} %get-tuple-element.75, f32[128]{0:T(128)S(1)} %get-tuple-element.73, f32[1024]{0:T(1024)S(1)} %get-tuple-element.40, f32[128,1024]{1,0:T(8,128)S(1)} %fusion.2, bf16[128,4608]{1,0:T(8,128)(2,1)S(1)} %copy-done.11, ...), kind=kOutput, calls=%fused_computation.62 | convolution fusion | flops 1208875904 | bytes 12198912 | tf_op jit(solution)/shard_map/dot_general | solution.py:209
  262.8 6.1 %fusion.33 = (f32[1024]{0:T(1024)S(1)}, f32[128]{0:T(128)S(1)}, f32[128,1024]{1,0:T(8,128)}) fusion(bf16[128,1024]{1,0:T(8,128)(2,1)S(1)} %copy-done.6, f32[128]{0:T(128)S(1)} %get-tuple-element.71, f32[1024]{0:T(1024)S(1)} %get-tuple-element.41, bf16[1024,18176]{1,0:T(8,128)(2,1)} %all-gather.2.cloned.1.call-done, ...), kind=kOutput, calls=%fused_computation.52 | convolution fusion | flops 808582016 | bytes 7873536 | tf_op jit(solution)/shard_map/dot_general | solution.py:236
  270.2 15.4 %all-to-all-start = ((f32[128,8,256]{2,1,0:T(8,128)}), f32[128,8,256]{2,1,0:T(8,128)S(1)}, u32[]{:S(2)}, u32[]{:S(2)}) async-start(f32[128,8,256]{2,1,0:T(8,128)} %pad_bitcast_fusion), calls=%async_computation | async-start | bytes 2097152 | tf_op jit(solution)/shard_map/all_to_all | solution.py:47
  285.6 5.8 %convolution_convert_fusion.3 = bf16[1024,3072]{1,0:T(8,128)(2,1)} fusion(bf16[128,1024]{1,0:T(8,128)(2,1)} %copy-done.16, bf16[128,1024]{1,0:T(8,128)(2,1)} %copy-done.14, bf16[128,1024]{1,0:T(8,128)(2,1)} %copy-done.15, bf16[128,1024]{1,0:T(8,128)(2,1)} %param.11, f32[1024]{0:T(1024)S(1)} %get-tuple-element.41, f32[128]{0:T(128)S(1)} %get-tuple-element.71), kind=kOutput, calls=%fused_computation.18 | convolution fusion | flops 811335680 | bytes 7344640 | tf_op jit(solution)/shard_map/dot_general | solution.py:235
  291.3 7.7 %pad_maximum_fusion = bf16[4,4,4,2,8,4096]{5,4,3,2,1,0:T(8,128)(2,1)} fusion(bf16[4,4,4,2,8,1024]{5,4,3,2,1,0:T(8,128)(2,1)} %bitcast.62, bf16[4,4,4,2,8,3072]{5,4,3,2,1,0:T(8,128)(2,1)} %bitcast.59), kind=kLoop, calls=%fused_computation.6 | loop fusion | flops 16777216 | bytes 16777216 | tf_op jit(solution)/shard_map/concatenate | solution.py:95
  299.1 7.8 %copy.77 = bf16[4,4,4,2,8,4096]{5,4,1,2,0,3:T(8,128)(2,1)} copy(bf16[4,4,4,2,8,4096]{5,4,3,2,1,0:T(8,128)(2,1)} %pad_maximum_fusion) | data formatting | bytes 16777216 | tf_op jit(solution)/shard_map/concatenate | solution.py:95
  306.9 7.5 %shard_map.186 = bf16[512,4096]{1,0:T(8,128)(2,1)} custom-call(bf16[2,512,4096]{2,1,0:T(8,128)(2,1)} %bitcast.55), custom_call_target="tpu_custom_call" | custom-call | tf_op jit(solution)/shard_map/pallas_call | solution.py:79
  314.4 7.3 %fusion.1 = bf16[512,4096]{1,0:T(8,128)(2,1)} fusion(bf16[512,4096]{1,0:T(8,128)(2,1)} %shard_map.186, bf16[2,512,4096]{2,1,0:T(8,128)(2,1)} %bitcast.56, s32[]{:T(128)S(6)} %select_n.6), kind=kLoop, calls=%fused_computation.8 | loop fusion | flops 8388608 | bytes 12582916 | tf_op jit(solution)/shard_map/convert_element_type | solution.py:90
  321.7 4.9 all-to-all-start.1
  326.9 6.0 %convolution_convert_fusion = bf16[4608,1024]{1,0:T(8,128)(2,1)} fusion(bf16[128,4608]{1,0:T(8,128)(2,1)S(1)} %get-tuple-element.59, bf16[128,1024]{1,0:T(8,128)(2,1)} %param.21), kind=kOutput, calls=%fused_computation.1 | convolution fusion | flops 1212678144 | bytes 10878976 | tf_op jit(solution)/shard_map/dot_general | solution.py:197
  332.9 17.6 %convert_element_type.164 = bf16[4,4,4,2,8,4608]{5,4,3,2,1,0:T(8,128)(2,1)} reshape(bf16[4608,1024]{1,0:T(8,128)(2,1)} %convolution_convert_fusion) | data formatting | bytes 18874368 | tf_op jit(solution)/shard_map/convert_element_type | solution.py:95
  350.4 8.6 %copy.74 = bf16[4,4,4,2,8,4608]{5,4,2,0,1,3:T(8,128)(2,1)} copy(bf16[4,4,4,2,8,4608]{5,4,3,2,1,0:T(8,128)(2,1)} %convert_element_type.164) | data formatting | bytes 18874368 | tf_op jit(solution)/shard_map/convert_element_type | solution.py:95
  359.1 8.3 %shard_map.187 = bf16[512,4608]{1,0:T(8,128)(2,1)} custom-call(bf16[2,512,4608]{2,1,0:T(8,128)(2,1)} %bitcast.53), custom_call_target="tpu_custom_call" | custom-call | tf_op jit(solution)/shard_map/pallas_call | solution.py:79
  367.4 7.1 %fusion = bf16[512,4608]{1,0:T(8,128)(2,1)} fusion(bf16[512,4608]{1,0:T(8,128)(2,1)} %shard_map.187, bf16[2,512,4608]{2,1,0:T(8,128)(2,1)} %bitcast.54, s32[]{:T(128)S(6)} %select_n.6), kind=kLoop, calls=%fused_computation.5 | loop fusion | flops 9437184 | bytes 14155780 | tf_op jit(solution)/shard_map/convert_element_type | solution.py:90
  376.1 5.0 all-to-all-start.4
  385.3 65.4 %all-to-all-done.4 = bf16[4,128,4608]{2,1,0:T(8,128)(2,1)} async-done(((bf16[4,128,4608]{2,1,0:T(8,128)(2,1)}), bf16[4,128,4608]{2,1,0:T(8,128)(2,1)}, u32[]{:S(2)}, u32[]{:S(2)}) %all-to-all-start.4) | async-done | bytes 4718624 | tf_op jit(solution)/shard_map/all_to_all | solution.py:107
  455.0 4.4 reduce_sum.175
  459.4 10.5 %all-to-all-done.2 = bf16[4,32,4096]{2,1,0:T(8,128)(2,1)S(1)} async-done(((bf16[4,32,4096]{2,1,0:T(8,128)(2,1)}), bf16[4,32,4096]{2,1,0:T(8,128)(2,1)S(1)}, u32[]{:S(2)}, u32[]{:S(2)}) %all-to-all-start.2) | async-done | bytes 1048608 | tf_op jit(solution)/shard_map/all_to_all | solution.py:107
  470.9 4.5 all-to-all-start.5
  476.0 5.8 %fusion.25 = bf16[128,1024]{1,0:T(8,128)(2,1)} fusion(f32[128,1024]{1,0:T(8,128)S(1)} %get-tuple-element.75, bf16[128,4608]{1,0:T(8,128)(2,1)S(1)} %get-tuple-element.59, bf16[4608,1024]{1,0:T(8,128)(2,1)} %reshape.137), kind=kOutput, calls=%fused_computation.36 | convolution fusion | flops 1208221696 | bytes 11403264 | tf_op jit(solution)/shard_map/dot_general | solution.py:188
  484.0 9.5 %all-to-all-done.5 = bf16[4,32,4608]{2,1,0:T(8,128)(2,1)S(1)} async-done(((bf16[4,32,4608]{2,1,0:T(8,128)(2,1)}), bf16[4,32,4608]{2,1,0:T(8,128)(2,1)S(1)}, u32[]{:S(2)}, u32[]{:S(2)}) %all-to-all-start.5) | async-done | bytes 1179680 | tf_op jit(solution)/shard_map/all_to_all | solution.py:107
  497.9 5.7 %all-to-all-done.3 = bf16[4,8,4096]{2,1,0:T(8,128)(2,1)S(1)} async-done(((bf16[4,8,4096]{2,1,0:T(8,128)(2,1)}), bf16[4,8,4096]{2,1,0:T(8,128)(2,1)S(1)}, u32[]{:S(2)}, u32[]{:S(2)}) %all-to-all-start.3) | async-done | bytes 262176 | tf_op jit(solution)/shard_map/all_to_all | solution.py:107
  (122 shorter events, 71.9 us)
Async XLA Ops:
  7.2 122.4 %all-gather.2.cloned.1.call-start = ((), (), s32[]{:S(2)}) async-start(), calls=%async_computation.11 | async-start | bytes 37515264 | tf_op jit(solution)/shard_map/all_gather | solution.py:31
  14.6 226.9 %reduce-scatter.5.cloned.1.call-start = ((), (), s32[]{:S(2)}) async-start(), calls=%async_computation.12 | async-start | bytes 28311552 | tf_op jit(solution)/shard_map/reduce_scatter | solution.py:111
  15.4 2.4 collective-permute-start.1
  134.9 36.8 %copy-start = (f32[128,3072]{1,0:T(8,128)}, f32[128,3072]{1,0:T(8,128)S(1)}, u32[]{:S(2)}) copy-start(f32[128,3072]{1,0:T(8,128)S(1)} %fusion.12) | copy-start | bytes 4718596
  135.0 36.7 %collective-permute-start = (bf16[2,1024]{1,0:T(2,128)(2,1)S(1)}, bf16[2,1024]{1,0:T(2,128)(2,1)S(1)}, u32[]{:S(2)}, u32[]{:S(2)}) collective-permute-start(bf16[2,1024]{1,0:T(2,128)(2,1)S(1)} %slice.138), channel_id=1, source_target_pairs={{0,1},{1,2},{2,3},{3,4},{4,5},{5,6},{6,7},{7,8},{8,9},{9,10},{10,1... | collective-permute-start | bytes 12296 | tf_op jit(solution)/shard_map/ppermute | solution.py:16
  145.0 17.9 %copy-start.7 = (bf16[128,1024]{1,0:T(8,128)(2,1)S(1)}, bf16[128,1024]{1,0:T(8,128)(2,1)}, u32[]{:S(2)}) copy-start(bf16[128,1024]{1,0:T(8,128)(2,1)} %param.21) | copy-start | bytes 786436
  169.7 3.1 copy-start.5
  172.8 2.4 copy-start.17
  186.1 2.9 copy-start.12
  186.1 2.9 copy-start.10
  209.1 158.3 %reduce-scatter.7.cloned.1.call-start = ((), (), s32[]{:S(2)}) async-start(), calls=%async_computation.13 | async-start | bytes 11796480 | tf_op jit(solution)/shard_map/reduce_scatter | solution.py:111
  242.8 6.9 %copy-start.11 = (bf16[128,4608]{1,0:T(8,128)(2,1)S(1)}, bf16[128,4608]{1,0:T(8,128)(2,1)}, u32[]{:S(2)}) copy-start(bf16[128,4608]{1,0:T(8,128)(2,1)} %copy-done.10) | copy-start | bytes 3538948
  249.6 6.0 %copy-start.8 = (bf16[128,1024]{1,0:T(8,128)(2,1)S(1)}, bf16[128,1024]{1,0:T(8,128)(2,1)}, u32[]{:S(2)}) copy-start(bf16[128,1024]{1,0:T(8,128)(2,1)} %param.21) | copy-start | bytes 786436
  255.6 2.8 copy-start.1
  255.6 2.8 copy-start.9
  255.8 4.5 copy-start.18
  258.7 4.0 copy-start.14
  258.9 3.9 copy-start.6
  258.9 3.6 collective-permute-start.2
  262.7 6.1 %copy-start.15 = (bf16[128,1024]{1,0:T(8,128)(2,1)}, bf16[128,1024]{1,0:T(8,128)(2,1)S(1)}, u32[]{:S(2)}) copy-start(bf16[128,1024]{1,0:T(8,128)(2,1)S(1)} %get-tuple-element.60) | copy-start | bytes 786436
  262.7 6.1 %copy-start.16 = (bf16[128,1024]{1,0:T(8,128)(2,1)}, bf16[128,1024]{1,0:T(8,128)(2,1)S(1)}, u32[]{:S(2)}) copy-start(bf16[128,1024]{1,0:T(8,128)(2,1)S(1)} %get-tuple-element.61) | copy-start | bytes 786436
  270.2 51.5 %all-to-all-start = ((f32[128,8,256]{2,1,0:T(8,128)}), f32[128,8,256]{2,1,0:T(8,128)S(1)}, u32[]{:S(2)}, u32[]{:S(2)}) async-start(f32[128,8,256]{2,1,0:T(8,128)} %pad_bitcast_fusion), calls=%async_computation | async-start | bytes 2097152 | tf_op jit(solution)/shard_map/all_to_all | solution.py:47
  321.7 11.1 %copy-start.2 = (f32[128,8,256]{2,1,0:T(8,128)}, f32[128,8,256]{2,1,0:T(8,128)S(1)}, u32[]{:S(2)}) copy-start(f32[128,8,256]{2,1,0:T(8,128)S(1)} %all-to-all-done) | copy-start | bytes 3145732
  321.7 54.4 %all-to-all-start.1 = ((bf16[4,128,4096]{2,1,0:T(8,128)(2,1)}), bf16[4,128,4096]{2,1,0:T(8,128)(2,1)}, u32[]{:S(2)}, u32[]{:S(2)}) async-start(bf16[4,128,4096]{2,1,0:T(8,128)(2,1)} %bitcast.61), calls=%async_computation.1 | async-start | bytes 8388608 | tf_op jit(solution)/shard_map/all_to_all | solution.py:107
  326.6 148.8 %reduce-scatter.9.cloned.1.call-start = ((), (), s32[]{:S(2)}) async-start(), calls=%async_computation.14 | async-start | bytes 2949120 | tf_op jit(solution)/shard_map/reduce_scatter | solution.py:111
  376.1 74.7 %all-to-all-start.4 = ((bf16[4,128,4608]{2,1,0:T(8,128)(2,1)}), bf16[4,128,4608]{2,1,0:T(8,128)(2,1)}, u32[]{:S(2)}, u32[]{:S(2)}) async-start(bf16[4,128,4608]{2,1,0:T(8,128)(2,1)} %bitcast.60), calls=%async_computation.8 | async-start | bytes 9437184 | tf_op jit(solution)/shard_map/all_to_all | solution.py:107
  450.8 19.1 %all-to-all-start.2 = ((bf16[4,32,4096]{2,1,0:T(8,128)(2,1)}), bf16[4,32,4096]{2,1,0:T(8,128)(2,1)S(1)}, u32[]{:S(2)}, u32[]{:S(2)}) async-start(bf16[4,32,4096]{2,1,0:T(8,128)(2,1)} %bitcast.64), calls=%async_computation.2 | async-start | bytes 2097152 | tf_op jit(solution)/shard_map/all_to_all | solution.py:107
  470.9 22.7 %all-to-all-start.5 = ((bf16[4,32,4608]{2,1,0:T(8,128)(2,1)}), bf16[4,32,4608]{2,1,0:T(8,128)(2,1)S(1)}, u32[]{:S(2)}, u32[]{:S(2)}) async-start(bf16[4,32,4608]{2,1,0:T(8,128)(2,1)} %bitcast.63), calls=%async_computation.9 | async-start | bytes 2359296 | tf_op jit(solution)/shard_map/all_to_all | solution.py:107
  475.4 39.3 %reduce-scatter.11.cloned.1.call-start = ((), (), s32[]{:S(2)}) async-start(), calls=%async_computation.15 | async-start | bytes 737280 | tf_op jit(solution)/shard_map/reduce_scatter | solution.py:111
  481.8 27.4 %copy-start.3 = (f32[128,8,256]{2,1,0:T(8,128)S(1)}, f32[128,8,256]{2,1,0:T(8,128)}, u32[]{:S(2)}) copy-start(f32[128,8,256]{2,1,0:T(8,128)} %copy-done.2) | copy-start | bytes 3145732
  493.5 10.1 %all-to-all-start.3 = ((bf16[4,8,4096]{2,1,0:T(8,128)(2,1)}), bf16[4,8,4096]{2,1,0:T(8,128)(2,1)S(1)}, u32[]{:S(2)}, u32[]{:S(2)}) async-start(bf16[4,8,4096]{2,1,0:T(8,128)(2,1)} %bitcast.17), calls=%async_computation.3 | async-start | bytes 524288 | tf_op jit(solution)/shard_map/all_to_all | solution.py:107
  503.6 10.3 %all-to-all-start.6 = ((bf16[4,8,4608]{2,1,0:T(8,128)(2,1)}), bf16[4,8,4608]{2,1,0:T(8,128)(2,1)S(1)}, u32[]{:S(2)}, u32[]{:S(2)}) async-start(bf16[4,8,4608]{2,1,0:T(8,128)(2,1)} %bitcast.28), calls=%async_computation.10 | async-start | bytes 589824 | tf_op jit(solution)/shard_map/all_to_all | solution.py:107
  (3 other events, 3.0 us)
Sparse Core Ops, SparseCore 0:
  14.7 114.7 all-gather.1
  209.2 32.2 reduce-scatter.4
  244.0 101.5 reduce-scatter.6
  367.5 48.5 reduce-scatter.8
  478.3 20.2 reduce-scatter.10

commit v9 on v8

--- a/solution.py
+++ b/solution.py
@@ -100,7 +100,7 @@
     blocks = blocks.transpose([AXES.index(a) for a in order] + [4, 5])
     blocks = blocks.reshape(packed.shape)
     for axis in order:
-        if direct and axis == "core":
+        if axis == "core":
             blocks = pair_exchange(blocks, collective_id)
         elif direct:
             size = lax.axis_size(axis)

time: 528 us -> 524 us (level)
  waiting for transfers between devices: 238 us -> 205 us
  Pallas kernels: 15.8 us -> 31.8 us
  other arithmetic: 55 us -> 67.5 us
    reduce_scatter x4 -> x3, waiting for transfers between devices: 32.2 us -> 0.04 us  [scatter_packed(): blocks = lax.psum_scatter(blocks, axis, scatter_dimension=0, tiled=True)]
    pallas_call x2 -> x3, Pallas kernels: 15.8 us -> 31.8 us  [pair_exchange(): pl.pallas_call(pair_kernel, out_shape=jax.ShapeDtypeStruct(halves.shape[1...]
    convert_element_type x2 -> x3, other arithmetic: 14.5 us -> 26.6 us  [pair_exchange(): (own.astype(jnp.float32) + received.astype(jnp.float32)).astype(jnp.bfloa...]
    transpose x1 -> x0, other arithmetic: 10.4 us -> none  [scatter_packed(): blocks = blocks.transpose([AXES.index(a) for a in order] + [4, 5])]
    concatenate x1 -> x2, other arithmetic: 7.74 us -> 18.1 us  [scatter_packed(): packed = jnp.concatenate(pieces, axis=1).astype(jnp.bfloat16)]
    transpose x1 -> x0, local copies, waits for them, and re-layouts: 6.7 us -> none  [scatter_packed(): blocks = blocks.transpose([AXES.index(a) for a in order] + [4, 5])]
    concatenate x1 -> x2, local copies, waits for them, and re-layouts: 7.81 us -> 14.4 us  [scatter_packed(): packed = jnp.concatenate(pieces, axis=1).astype(jnp.bfloat16)]
  transfers between devices with their start and end apart: 15 -> 14, of which waited for: 8 -> 7; matrix products, arithmetic and copies ran while one was open for 30% -> 30% of each run, Pallas kernels for 3% -> 3%
where the time goes in v9:
time: 524 us; the launch traced here: 519 us
  waiting for transfers between devices  205 us (39%)
  local copies, waits for them, and re-layouts  83.2 us (16%)
  matrix products  71.7 us (14%)
  other arithmetic  67.5 us (13%)
  starting transfers between devices  45.6 us (9%)
  Pallas kernels  31.8 us (6%)
  between operations  14.6 us (3%)
    all_gather x1, waiting for transfers between devices, gather_packed(): full = lax.all_gather(packed, AXES, axis=0, tiled=True)  110 us
    all_to_all x6, waiting for transfers between devices, scatter_packed(): got = lax.all_to_all(blocks, axis, 0, 0, tiled=True)  94.8 us
    pallas_call x3, Pallas kernels, pair_exchange(): pl.pallas_call(pair_kernel, out_shape=jax.ShapeDtypeStruct(halves.shape[1...  31.8 us
    convert_element_type x3, other arithmetic, pair_exchange(): (own.astype(jnp.float32) + received.astype(jnp.float32)).astype(jnp.bfloa...  26.6 us
    convert_element_type x2, local copies, waits for them, and re-layouts, scatter_packed(): packed = jnp.concatenate(pieces, axis=1).astype(jnp.bfloat16)  26.1 us
    all_to_all x6, starting transfers between devices, scatter_packed(): got = lax.all_to_all(blocks, axis, 0, 0, tiled=True)  25.3 us
    concatenate x2, other arithmetic, scatter_packed(): packed = jnp.concatenate(pieces, axis=1).astype(jnp.bfloat16)  18.1 us
    reshape x1, local copies, waits for them, and re-layouts, per_device(): w_down = w_down_packed.reshape(n * down_rows, width)  17.9 us
  transfers between devices with their start and end apart: 14, of which 7 were waited for; matrix products, arithmetic and copies ran while one was open for 30% of the time, Pallas kernels for 3%

profile of v9, /device:TPU:0, one launch (start us, length us, event | category | flops | bytes accessed | tf_op | source)
XLA Modules:
  0.0 519.3 jit_solution(15028902110042747447)
XLA Ops:
  19.8 109.8 %all-gather.2.cloned.1.call-done = bf16[1024,18176]{1,0:T(8,128)(2,1)} async-done(((bf16[8,18176]{1,0:T(8,128)(2,1)}), bf16[1024,18176]{1,0:T(8,128)(2,1)}) %all-gather.2.cloned.1.call-update) | async-done | bytes 37224464 | tf_op jit(solution)/shard_map/all_gather | solution.py:31
  137.1 7.8 %slice.148 = bf16[1024,4608]{1,0:T(8,128)(2,1)} slice(bf16[1024,18176]{1,0:T(8,128)(2,1)} %all-gather.2.cloned.1.call-done), slice={[0:1024], [13568:18176]} | slice | bytes 18874368 | tf_op jit(solution)/shard_map/slice | solution.py:34
  145.0 17.9 %reshape.136 = bf16[4608,1024]{1,0:T(8,128)(2,1)} reshape(bf16[1024,4608]{1,0:T(8,128)(2,1)} %slice.148) | data formatting | bytes 18874368 | tf_op jit(solution)/shard_map/reshape | solution.py:152
  162.9 6.9 %convolution_bitcast_fusion = f32[128,4608]{1,0:T(8,128)S(1)} fusion(bf16[4608,1024]{1,0:T(8,128)(2,1)} %reshape.136, bf16[128,1024]{1,0:T(8,128)(2,1)S(1)} %copy-done.7), kind=kOutput, calls=%fused_computation.19 | convolution fusion | flops 1207959552 | bytes 12058624 | tf_op jit(solution)/shard_map/dot_general | solution.py:192
  175.2 5.1 fusion.5
  180.3 5.8 %multiply_convert_fusion.1 = (bf16[128,4608]{1,0:T(8,128)(2,1)S(1)}, bf16[128,4608]{1,0:T(8,128)(2,1)S(1)}, bf16[128,4608]{1,0:T(8,128)(2,1)S(1)}) fusion(f32[128,4608]{1,0:T(8,128)S(1)} %convolution_bitcast_fusion, f32[128,4608]{1,0:T(8,128)S(1)} %fusion.5, bf16[128,1024]{1,0:T(8,128)(2,1)S(1)} %multiply_convert_fusion.6, ...), kind=kOutput, calls=%fused_computation.26 | convolution fusion | flops 1216806912 | bytes 17956864 | tf_op jit(solution)/shard_map/dot_general | solution.py:183
  192.0 10.4 %pad_maximum_fusion = bf16[4,4,4,2,8,9216]{5,4,3,2,1,0:T(8,128)(2,1)S(1)} fusion(bf16[4,4,4,2,8,4608]{5,4,3,2,1,0:T(8,128)(2,1)S(1)} %bitcast.61, bf16[4,4,4,2,8,4608]{5,4,3,2,1,0:T(8,128)(2,1)S(1)} %bitcast.62), kind=kLoop, calls=%fused_computation | loop fusion | flops 37748736 | bytes 37748736 | tf_op jit(solution)/shard_map/concatenate | solution.py:95
  202.4 6.7 %copy.84 = bf16[4,4,4,2,8,9216]{5,4,0,1,2,3:T(8,128)(2,1)} copy(bf16[4,4,4,2,8,9216]{5,4,3,2,1,0:T(8,128)(2,1)S(1)} %pad_maximum_fusion) | data formatting | bytes 37748736 | tf_op jit(solution)/shard_map/concatenate | solution.py:95
  209.1 16.0 %shard_map.187 = bf16[512,9216]{1,0:T(8,128)(2,1)} custom-call(bf16[2,512,9216]{2,1,0:T(8,128)(2,1)} %bitcast.55), custom_call_target="tpu_custom_call" | custom-call | tf_op jit(solution)/shard_map/pallas_call | solution.py:79
  225.1 12.1 %fusion = bf16[512,9216]{1,0:T(8,128)(2,1)} fusion(bf16[512,9216]{1,0:T(8,128)(2,1)} %shard_map.187, bf16[2,512,9216]{2,1,0:T(8,128)(2,1)} %bitcast.56, s32[]{:T(128)S(6)} %select_n.8), kind=kLoop, calls=%fused_computation.2 | loop fusion | flops 18874368 | bytes 28311556 | tf_op jit(solution)/shard_map/convert_element_type | solution.py:90
  238.4 6.9 %fusion.3 = f32[128,1024]{1,0:T(8,128)S(1)} fusion(bf16[128,4608]{1,0:T(8,128)(2,1)S(1)} %copy-done.13, bf16[1024,18176]{1,0:T(8,128)(2,1)} %all-gather.2.cloned.1.call-done), kind=kOutput, calls=%fused_computation.11 | convolution fusion | flops 1207959552 | bytes 11141120 | tf_op jit(solution)/shard_map/dot_general | solution.py:210
  245.3 6.8 %multiply_reduce_fusion.3 = (f32[1024]{0:T(1024)S(1)}, f32[128]{0:T(128)S(1)}, f32[128,1024]{1,0:T(8,128)S(1)}) fusion(f32[128,1024]{1,0:T(8,128)S(1)} %get-tuple-element.75, f32[128]{0:T(128)S(1)} %get-tuple-element.73, f32[1024]{0:T(1024)S(1)} %get-tuple-element.40, f32[128,1024]{1,0:T(8,128)S(1)} %fusion.3, bf16[128,4608]{1,0:T(8,128)(2,1)S(1)} %copy-done.11, ...), kind=kOutput, calls=%fused_computation.64 | convolution fusion | flops 1208875904 | bytes 12198912 | tf_op jit(solution)/shard_map/dot_general | solution.py:209
  259.0 6.1 %fusion.34 = (f32[1024]{0:T(1024)S(1)}, f32[128]{0:T(128)S(1)}, f32[128,1024]{1,0:T(8,128)}) fusion(bf16[128,1024]{1,0:T(8,128)(2,1)S(1)} %copy-done.6, f32[128]{0:T(128)S(1)} %get-tuple-element.71, f32[1024]{0:T(1024)S(1)} %get-tuple-element.41, bf16[1024,18176]{1,0:T(8,128)(2,1)} %all-gather.2.cloned.1.call-done, ...), kind=kOutput, calls=%fused_computation.54 | convolution fusion | flops 808582016 | bytes 7873536 | tf_op jit(solution)/shard_map/dot_general | solution.py:236
  266.5 15.2 %all-to-all-start = ((f32[128,8,256]{2,1,0:T(8,128)}), f32[128,8,256]{2,1,0:T(8,128)S(1)}, u32[]{:S(2)}, u32[]{:S(2)}) async-start(f32[128,8,256]{2,1,0:T(8,128)} %pad_bitcast_fusion), calls=%async_computation | async-start | bytes 2097152 | tf_op jit(solution)/shard_map/all_to_all | solution.py:47
  281.7 5.9 %convolution_convert_fusion.3 = bf16[1024,3072]{1,0:T(8,128)(2,1)} fusion(bf16[128,1024]{1,0:T(8,128)(2,1)} %copy-done.16, bf16[128,1024]{1,0:T(8,128)(2,1)} %copy-done.14, bf16[128,1024]{1,0:T(8,128)(2,1)} %copy-done.15, bf16[128,1024]{1,0:T(8,128)(2,1)} %param.11, f32[1024]{0:T(1024)S(1)} %get-tuple-element.41, f32[128]{0:T(128)S(1)} %get-tuple-element.71), kind=kOutput, calls=%fused_computation.20 | convolution fusion | flops 811335680 | bytes 7344640 | tf_op jit(solution)/shard_map/dot_general | solution.py:235
  287.5 7.7 %pad_maximum_fusion.1 = bf16[4,4,4,2,8,4096]{5,4,3,2,1,0:T(8,128)(2,1)} fusion(bf16[4,4,4,2,8,1024]{5,4,3,2,1,0:T(8,128)(2,1)} %bitcast.66, bf16[4,4,4,2,8,3072]{5,4,3,2,1,0:T(8,128)(2,1)} %bitcast.63), kind=kLoop, calls=%fused_computation.8 | loop fusion | flops 16777216 | bytes 16777216 | tf_op jit(solution)/shard_map/concatenate | solution.py:95
  295.2 7.7 %copy.83 = bf16[4,4,4,2,8,4096]{5,4,1,2,0,3:T(8,128)(2,1)} copy(bf16[4,4,4,2,8,4096]{5,4,3,2,1,0:T(8,128)(2,1)} %pad_maximum_fusion.1) | data formatting | bytes 16777216 | tf_op jit(solution)/shard_map/concatenate | solution.py:95
  303.0 7.5 %shard_map.186 = bf16[512,4096]{1,0:T(8,128)(2,1)} custom-call(bf16[2,512,4096]{2,1,0:T(8,128)(2,1)} %bitcast.59), custom_call_target="tpu_custom_call" | custom-call | tf_op jit(solution)/shard_map/pallas_call | solution.py:79
  310.5 7.4 %fusion.2 = bf16[512,4096]{1,0:T(8,128)(2,1)} fusion(bf16[512,4096]{1,0:T(8,128)(2,1)} %shard_map.186, bf16[2,512,4096]{2,1,0:T(8,128)(2,1)} %bitcast.60, s32[]{:T(128)S(6)} %select_n.8), kind=kLoop, calls=%fused_computation.10 | loop fusion | flops 8388608 | bytes 12582916 | tf_op jit(solution)/shard_map/convert_element_type | solution.py:90
  317.9 4.9 all-to-all-start.1
  322.8 6.1 %convolution_convert_fusion = bf16[4608,1024]{1,0:T(8,128)(2,1)} fusion(bf16[128,4608]{1,0:T(8,128)(2,1)S(1)} %get-tuple-element.59, bf16[128,1024]{1,0:T(8,128)(2,1)} %param.21), kind=kOutput, calls=%fused_computation.3 | convolution fusion | flops 1212678144 | bytes 10878976 | tf_op jit(solution)/shard_map/dot_general | solution.py:197
  328.9 17.5 %convert_element_type.180 = bf16[4,4,4,2,8,4608]{5,4,3,2,1,0:T(8,128)(2,1)} reshape(bf16[4608,1024]{1,0:T(8,128)(2,1)} %convolution_convert_fusion) | data formatting | bytes 18874368 | tf_op jit(solution)/shard_map/convert_element_type | solution.py:95
  346.4 8.6 %copy.80 = bf16[4,4,4,2,8,4608]{5,4,2,0,1,3:T(8,128)(2,1)} copy(bf16[4,4,4,2,8,4608]{5,4,3,2,1,0:T(8,128)(2,1)} %convert_element_type.180) | data formatting | bytes 18874368 | tf_op jit(solution)/shard_map/convert_element_type | solution.py:95
  355.0 8.3 %shard_map.188 = bf16[512,4608]{1,0:T(8,128)(2,1)} custom-call(bf16[2,512,4608]{2,1,0:T(8,128)(2,1)} %bitcast.57), custom_call_target="tpu_custom_call" | custom-call | tf_op jit(solution)/shard_map/pallas_call | solution.py:79
  363.4 7.1 %fusion.1 = bf16[512,4608]{1,0:T(8,128)(2,1)} fusion(bf16[512,4608]{1,0:T(8,128)(2,1)} %shard_map.188, bf16[2,512,4608]{2,1,0:T(8,128)(2,1)} %bitcast.58, s32[]{:T(128)S(6)} %select_n.8), kind=kLoop, calls=%fused_computation.7 | loop fusion | flops 9437184 | bytes 14155780 | tf_op jit(solution)/shard_map/convert_element_type | solution.py:90
  372.2 5.0 all-to-all-start.4
  381.4 65.5 %all-to-all-done.4 = bf16[4,128,4608]{2,1,0:T(8,128)(2,1)} async-done(((bf16[4,128,4608]{2,1,0:T(8,128)(2,1)}), bf16[4,128,4608]{2,1,0:T(8,128)(2,1)}, u32[]{:S(2)}, u32[]{:S(2)}) %all-to-all-start.4) | async-done | bytes 4718624 | tf_op jit(solution)/shard_map/all_to_all | solution.py:107
  455.5 10.6 %all-to-all-done.2 = bf16[4,32,4096]{2,1,0:T(8,128)(2,1)S(1)} async-done(((bf16[4,32,4096]{2,1,0:T(8,128)(2,1)}), bf16[4,32,4096]{2,1,0:T(8,128)(2,1)S(1)}, u32[]{:S(2)}, u32[]{:S(2)}) %all-to-all-start.2) | async-done | bytes 1048608 | tf_op jit(solution)/shard_map/all_to_all | solution.py:107
  467.1 4.4 all-to-all-start.5
  472.1 5.8 %fusion.26 = bf16[128,1024]{1,0:T(8,128)(2,1)} fusion(f32[128,1024]{1,0:T(8,128)S(1)} %get-tuple-element.75, bf16[128,4608]{1,0:T(8,128)(2,1)S(1)} %get-tuple-element.59, bf16[4608,1024]{1,0:T(8,128)(2,1)} %reshape.136), kind=kOutput, calls=%fused_computation.38 | convolution fusion | flops 1208221696 | bytes 11403264 | tf_op jit(solution)/shard_map/dot_general | solution.py:188
  480.1 9.6 %all-to-all-done.5 = bf16[4,32,4608]{2,1,0:T(8,128)(2,1)S(1)} async-done(((bf16[4,32,4608]{2,1,0:T(8,128)(2,1)}), bf16[4,32,4608]{2,1,0:T(8,128)(2,1)S(1)}, u32[]{:S(2)}, u32[]{:S(2)}) %all-to-all-start.5) | async-done | bytes 1179680 | tf_op jit(solution)/shard_map/all_to_all | solution.py:107
  494.1 5.7 %all-to-all-done.3 = bf16[4,8,4096]{2,1,0:T(8,128)(2,1)S(1)} async-done(((bf16[4,8,4096]{2,1,0:T(8,128)(2,1)}), bf16[4,8,4096]{2,1,0:T(8,128)(2,1)S(1)}, u32[]{:S(2)}, u32[]{:S(2)}) %all-to-all-start.3) | async-done | bytes 262176 | tf_op jit(solution)/shard_map/all_to_all | solution.py:107
  (123 shorter events, 76.1 us)
Async XLA Ops:
  7.2 122.4 %all-gather.2.cloned.1.call-start = ((), (), s32[]{:S(2)}) async-start(), calls=%async_computation.10 | async-start | bytes 37515264 | tf_op jit(solution)/shard_map/all_gather | solution.py:31
  14.6 348.7 %reduce-scatter.4.cloned.1.call-start = ((), (), s32[]{:S(2)}) async-start(), calls=%async_computation.11 | async-start | bytes 11796480 | tf_op jit(solution)/shard_map/reduce_scatter | solution.py:111
  15.4 2.9 collective-permute-start.1
  134.9 36.9 %copy-start = (f32[128,3072]{1,0:T(8,128)}, f32[128,3072]{1,0:T(8,128)S(1)}, u32[]{:S(2)}) copy-start(f32[128,3072]{1,0:T(8,128)S(1)} %fusion.13) | copy-start | bytes 4718596
  135.0 36.7 %collective-permute-start = (bf16[2,1024]{1,0:T(2,128)(2,1)S(1)}, bf16[2,1024]{1,0:T(2,128)(2,1)S(1)}, u32[]{:S(2)}, u32[]{:S(2)}) collective-permute-start(bf16[2,1024]{1,0:T(2,128)(2,1)S(1)} %slice.138), channel_id=1, source_target_pairs={{0,1},{1,2},{2,3},{3,4},{4,5},{5,6},{6,7},{7,8},{8,9},{9,10},{10,1... | collective-permute-start | bytes 12296 | tf_op jit(solution)/shard_map/ppermute | solution.py:16
  145.0 17.9 %copy-start.7 = (bf16[128,1024]{1,0:T(8,128)(2,1)S(1)}, bf16[128,1024]{1,0:T(8,128)(2,1)}, u32[]{:S(2)}) copy-start(bf16[128,1024]{1,0:T(8,128)(2,1)} %param.21) | copy-start | bytes 786436
  162.9 10.0 %copy-start.5 = (bf16[128,1024]{1,0:T(8,128)(2,1)S(1)}, bf16[128,1024]{1,0:T(8,128)(2,1)}, u32[]{:S(2)}) copy-start(bf16[128,1024]{1,0:T(8,128)(2,1)} %param.11) | copy-start | bytes 786436
  172.9 2.2 copy-start.17
  186.2 2.9 copy-start.12
  186.2 2.9 copy-start.10
  238.4 6.9 %copy-start.11 = (bf16[128,4608]{1,0:T(8,128)(2,1)S(1)}, bf16[128,4608]{1,0:T(8,128)(2,1)}, u32[]{:S(2)}) copy-start(bf16[128,4608]{1,0:T(8,128)(2,1)} %copy-done.10) | copy-start | bytes 3538948
  245.3 6.9 %copy-start.8 = (bf16[128,1024]{1,0:T(8,128)(2,1)S(1)}, bf16[128,1024]{1,0:T(8,128)(2,1)}, u32[]{:S(2)}) copy-start(bf16[128,1024]{1,0:T(8,128)(2,1)} %param.21) | copy-start | bytes 786436
  245.3 9.5 %copy-start.1 = (f32[128,3072]{1,0:T(8,128)S(1)}, f32[128,3072]{1,0:T(8,128)}, u32[]{:S(2)}) copy-start(f32[128,3072]{1,0:T(8,128)} %copy-done) | copy-start | bytes 4718596
  245.3 9.5 %copy-start.9 = (f32[128,1024]{1,0:T(8,128)S(1)}, f32[128,1024]{1,0:T(8,128)}, u32[]{:S(2)}) copy-start(f32[128,1024]{1,0:T(8,128)} %get-tuple-element.56) | copy-start | bytes 1572868
  252.2 4.5 copy-start.18
  255.1 10.0 %copy-start.14 = (bf16[128,1024]{1,0:T(8,128)(2,1)}, bf16[128,1024]{1,0:T(8,128)(2,1)S(1)}, u32[]{:S(2)}) copy-start(bf16[128,1024]{1,0:T(8,128)(2,1)S(1)} %get-tuple-element.62) | copy-start | bytes 786436
  255.2 3.8 copy-start.6
  255.3 3.5 collective-permute-start.2
  259.0 6.2 %copy-start.15 = (bf16[128,1024]{1,0:T(8,128)(2,1)}, bf16[128,1024]{1,0:T(8,128)(2,1)S(1)}, u32[]{:S(2)}) copy-start(bf16[128,1024]{1,0:T(8,128)(2,1)S(1)} %get-tuple-element.60) | copy-start | bytes 786436
  259.0 6.1 %copy-start.16 = (bf16[128,1024]{1,0:T(8,128)(2,1)}, bf16[128,1024]{1,0:T(8,128)(2,1)S(1)}, u32[]{:S(2)}) copy-start(bf16[128,1024]{1,0:T(8,128)(2,1)S(1)} %get-tuple-element.61) | copy-start | bytes 786436
  266.5 51.4 %all-to-all-start = ((f32[128,8,256]{2,1,0:T(8,128)}), f32[128,8,256]{2,1,0:T(8,128)S(1)}, u32[]{:S(2)}, u32[]{:S(2)}) async-start(f32[128,8,256]{2,1,0:T(8,128)} %pad_bitcast_fusion), calls=%async_computation | async-start | bytes 2097152 | tf_op jit(solution)/shard_map/all_to_all | solution.py:47
  317.9 11.0 %copy-start.2 = (f32[128,8,256]{2,1,0:T(8,128)}, f32[128,8,256]{2,1,0:T(8,128)S(1)}, u32[]{:S(2)}) copy-start(f32[128,8,256]{2,1,0:T(8,128)S(1)} %all-to-all-done) | copy-start | bytes 3145732
  317.9 54.3 %all-to-all-start.1 = ((bf16[4,128,4096]{2,1,0:T(8,128)(2,1)}), bf16[4,128,4096]{2,1,0:T(8,128)(2,1)}, u32[]{:S(2)}, u32[]{:S(2)}) async-start(bf16[4,128,4096]{2,1,0:T(8,128)(2,1)} %bitcast.65), calls=%async_computation.1 | async-start | bytes 8388608 | tf_op jit(solution)/shard_map/all_to_all | solution.py:107
  322.7 149.1 %reduce-scatter.6.cloned.1.call-start = ((), (), s32[]{:S(2)}) async-start(), calls=%async_computation.12 | async-start | bytes 2949120 | tf_op jit(solution)/shard_map/reduce_scatter | solution.py:111
  372.2 74.7 %all-to-all-start.4 = ((bf16[4,128,4608]{2,1,0:T(8,128)(2,1)}), bf16[4,128,4608]{2,1,0:T(8,128)(2,1)}, u32[]{:S(2)}, u32[]{:S(2)}) async-start(bf16[4,128,4608]{2,1,0:T(8,128)(2,1)} %bitcast.64), calls=%async_computation.7 | async-start | bytes 9437184 | tf_op jit(solution)/shard_map/all_to_all | solution.py:107
  446.9 19.3 %all-to-all-start.2 = ((bf16[4,32,4096]{2,1,0:T(8,128)(2,1)}), bf16[4,32,4096]{2,1,0:T(8,128)(2,1)S(1)}, u32[]{:S(2)}, u32[]{:S(2)}) async-start(bf16[4,32,4096]{2,1,0:T(8,128)(2,1)} %bitcast.68), calls=%async_computation.2 | async-start | bytes 2097152 | tf_op jit(solution)/shard_map/all_to_all | solution.py:107
  467.1 22.6 %all-to-all-start.5 = ((bf16[4,32,4608]{2,1,0:T(8,128)(2,1)}), bf16[4,32,4608]{2,1,0:T(8,128)(2,1)S(1)}, u32[]{:S(2)}, u32[]{:S(2)}) async-start(bf16[4,32,4608]{2,1,0:T(8,128)(2,1)} %bitcast.67), calls=%async_computation.8 | async-start | bytes 2359296 | tf_op jit(solution)/shard_map/all_to_all | solution.py:107
  471.5 39.3 %reduce-scatter.8.cloned.1.call-start = ((), (), s32[]{:S(2)}) async-start(), calls=%async_computation.13 | async-start | bytes 737280 | tf_op jit(solution)/shard_map/reduce_scatter | solution.py:111
  472.1 31.1 %copy-start.20 = (f32[128]{0:T(128)S(1)}, f32[128]{0:T(128)}, u32[]{:S(2)}) copy-start(f32[128]{0:T(128)} %get-tuple-element.70) | copy-start | bytes 1540
  477.9 27.5 %copy-start.3 = (f32[128,8,256]{2,1,0:T(8,128)S(1)}, f32[128,8,256]{2,1,0:T(8,128)}, u32[]{:S(2)}) copy-start(f32[128,8,256]{2,1,0:T(8,128)} %copy-done.2) | copy-start | bytes 3145732
  489.7 10.1 %all-to-all-start.3 = ((bf16[4,8,4096]{2,1,0:T(8,128)(2,1)}), bf16[4,8,4096]{2,1,0:T(8,128)(2,1)S(1)}, u32[]{:S(2)}, u32[]{:S(2)}) async-start(bf16[4,8,4096]{2,1,0:T(8,128)(2,1)} %bitcast.17), calls=%async_computation.3 | async-start | bytes 524288 | tf_op jit(solution)/shard_map/all_to_all | solution.py:107
  499.8 10.3 %all-to-all-start.6 = ((bf16[4,8,4608]{2,1,0:T(8,128)(2,1)}), bf16[4,8,4608]{2,1,0:T(8,128)(2,1)S(1)}, u32[]{:S(2)}, u32[]{:S(2)}) async-start(bf16[4,8,4608]{2,1,0:T(8,128)(2,1)} %bitcast.30), calls=%async_computation.9 | async-start | bytes 589824 | tf_op jit(solution)/shard_map/all_to_all | solution.py:107
  (3 other events, 3.0 us)
Sparse Core Ops, SparseCore 0:
  14.7 114.7 all-gather.1
  237.3 100.4 reduce-scatter.3
  363.5 48.6 reduce-scatter.5
  474.4 20.2 reduce-scatter.7

commit v10 on v9

--- a/solution.py
+++ b/solution.py
@@ -38,6 +38,9 @@
 
 AXES = ("y", "z", "x", "core")
 FSDP = AXES
+ORDER_UP = ("core", "x", "z", "y")
+ORDER_DOWN = ("core", "z", "y", "x")
+ORDER_IN = ("core", "y", "x", "z")
 
 
 def exchange_packed(pieces, dtype=jnp.float32):
@@ -90,15 +93,21 @@
     return (own.astype(jnp.float32) + received.astype(jnp.float32)).astype(jnp.bfloat16)
 
 
+def in_stage_order(values, order):
+    sizes = [lax.axis_size(a) for a in AXES]
+    group = values.shape[1] // (sizes[0] * sizes[1] * sizes[2] * sizes[3])
+    grid = values.reshape([values.shape[0]] + sizes + [group])
+    grid = grid.transpose([0] + [1 + AXES.index(a) for a in order] + [5])
+    return grid.reshape(values.shape)
+
+
 def scatter_packed(pieces, order=("core", "x", "z", "y"), direct=False, collective_id=0):
     widths = [p.shape[1] for p in pieces]
     packed = jnp.concatenate(pieces, axis=1).astype(jnp.bfloat16)
     sizes = [lax.axis_size(a) for a in AXES]
     count = sizes[0] * sizes[1] * sizes[2] * sizes[3]
     per = packed.shape[0] // count
-    blocks = packed.reshape(sizes + [per, packed.shape[1]])
-    blocks = blocks.transpose([AXES.index(a) for a in order] + [4, 5])
-    blocks = blocks.reshape(packed.shape)
+    blocks = packed
     for axis in order:
         if axis == "core":
             blocks = pair_exchange(blocks, collective_id)
@@ -194,15 +203,23 @@
     )
     da = (dz * b * sig * (1.0 + a * (1.0 - sig))).astype(jnp.bfloat16)
     db = (dz * act).astype(jnp.bfloat16)
+    h2_up = in_stage_order(h2, ORDER_UP)
     g_down = lax.dot_general(
-        z, cotangent, (((0,), (0,)), ((), ())), preferred_element_type=jnp.float32
-    )
-    g_gate = lax.dot_general(h2, da, (((0,), (0,)), ((), ())), preferred_element_type=jnp.float32)
-    g_up = lax.dot_general(h2, db, (((0,), (0,)), ((), ())), preferred_element_type=jnp.float32)
-    own_gate, own_up = scatter_packed([g_gate, g_up])
+        in_stage_order(z, ORDER_DOWN),
+        cotangent,
+        (((0,), (0,)), ((), ())),
+        preferred_element_type=jnp.bfloat16,
+    )
+    g_gate = lax.dot_general(
+        h2_up, da, (((0,), (0,)), ((), ())), preferred_element_type=jnp.bfloat16
+    )
+    g_up = lax.dot_general(
+        h2_up, db, (((0,), (0,)), ((), ())), preferred_element_type=jnp.bfloat16
+    )
+    own_gate, own_up = scatter_packed([g_gate, g_up], order=ORDER_UP)
     (own_down,) = scatter_packed(
         [g_down.reshape(n * per, -1)],
-        order=("core", "z", "y", "x"),
+        order=ORDER_DOWN,
         direct=True,
         collective_id=1,
     )
@@ -218,7 +235,12 @@
         - resid * (s2 * s2 * s2) * jnp.mean(dn2 * resid, axis=-1, keepdims=True)
     )
     d_out = d_resid.astype(jnp.bfloat16)
-    g_out = lax.dot_general(y, d_out, (((0,), (0,)), ((), ())), preferred_element_type=jnp.float32)
+    g_out = lax.dot_general(
+        in_stage_order(y, ORDER_IN),
+        d_out,
+        (((0,), (0,)), ((), ())),
+        preferred_element_type=jnp.bfloat16,
+    )
     dy = lax.dot_general(d_out, w_out, (((1,), (1,)), ((), ())), preferred_element_type=jnp.float32)
     d_cgate = dy * conv_out
     d_conv = dy * cgate
@@ -232,7 +254,12 @@
     returned = shifted(d_ext[:2], AXES, -1)
     d_bx = d_ext[2:] + jnp.pad(returned, ((rows - 2, 0), (0, 0)))
     d_proj = jnp.concatenate([d_bx * xv, d_cgate, d_bx * bgate], axis=1).astype(jnp.bfloat16)
-    g_in = lax.dot_general(h, d_proj, (((0,), (0,)), ((), ())), preferred_element_type=jnp.float32)
+    g_in = lax.dot_general(
+        in_stage_order(h, ORDER_IN),
+        d_proj,
+        (((0,), (0,)), ((), ())),
+        preferred_element_type=jnp.bfloat16,
+    )
     dh = lax.dot_general(d_proj, w_in, (((1,), (1,)), ((), ())), preferred_element_type=jnp.float32)
     g_gain1 = jnp.sum(dh * xf * s1, axis=0)
     dn1 = dh * gain1.astype(jnp.float32)
@@ -241,7 +268,7 @@
     )
     g_small = jnp.concatenate([g_gain1[:, None], g_gain2[:, None], g_conv], axis=1)
     own_in, own_out = scatter_packed(
-        [g_in, g_out], order=("core", "y", "x", "z"), direct=True, collective_id=2
+        [g_in, g_out], order=ORDER_IN, direct=True, collective_id=2
     )
     (own_small,) = exchange_packed([pad_cols(g_small)])
     return (

time: 524 us -> 508 us (0.969)
  local copies, waits for them, and re-layouts: 83.2 us -> 69.9 us
    convert_element_type x2 -> x4, local copies, waits for them, and re-layouts: 26.1 us -> 3.11 us  [the longest x1 1.79 us: per_device(): y = (cgate * conv_out).astype(jnp.bfloat16)]
    another operation x0 -> x1, local copies, waits for them, and re-layouts: none -> 17.6 us  [pair_exchange(): halves = blocks.reshape(2, blocks.shape[0] // 2, blocks.shape[1])]
    concatenate x2 -> x0, local copies, waits for them, and re-layouts: 14.4 us -> none  [scatter_packed(): packed = jnp.concatenate(pieces, axis=1).astype(jnp.bfloat16)]
  transfers between devices with their start and end apart: 14 -> 14, of which waited for: 7 -> 8; matrix products, arithmetic and copies ran while one was open for 30% -> 29% of each run, Pallas kernels for 3% -> 3%
where the time goes in v10:
time: 508 us; the launch traced here: 506 us
  waiting for transfers between devices  205 us (40%)
  matrix products  71.3 us (14%)
  local copies, waits for them, and re-layouts  69.9 us (14%)
  other arithmetic  68.7 us (14%)
  starting transfers between devices  45.1 us (9%)
  Pallas kernels  31.8 us (6%)
  between operations  14.4 us (3%)
    all_gather x1, waiting for transfers between devices, gather_packed(): full = lax.all_gather(packed, AXES, axis=0, tiled=True)  110 us
    all_to_all x6, waiting for transfers between devices, scatter_packed(): got = lax.all_to_all(blocks, axis, 0, 0, tiled=True)  91.5 us
    pallas_call x3, Pallas kernels, pair_exchange(): pl.pallas_call(pair_kernel, out_shape=jax.ShapeDtypeStruct(halves.shape[1...  31.8 us
    convert_element_type x3, other arithmetic, pair_exchange(): (own.astype(jnp.float32) + received.astype(jnp.float32)).astype(jnp.bfloa...  26.3 us
    all_to_all x6, starting transfers between devices, scatter_packed(): got = lax.all_to_all(blocks, axis, 0, 0, tiled=True)  25.3 us
    concatenate x2, other arithmetic, scatter_packed(): packed = jnp.concatenate(pieces, axis=1).astype(jnp.bfloat16)  18.8 us
    another operation x1, local copies, waits for them, and re-layouts, pair_exchange(): halves = blocks.reshape(2, blocks.shape[0] // 2, blocks.shape[1])  17.6 us
    reshape x1, local copies, waits for them, and re-layouts, per_device(): w_down = w_down_packed.reshape(n * down_rows, width)  17.5 us
  transfers between devices with their start and end apart: 14, of which 8 were waited for; matrix products, arithmetic and copies ran while one was open for 29% of the time, Pallas kernels for 3%

profile of v10, /device:TPU:0, one launch (start us, length us, event | category | flops | bytes accessed | tf_op | source)
XLA Modules:
  0.0 505.8 jit_solution(1592263216700957920)
XLA Ops:
  19.3 110.3 %all-gather.2.cloned.1.call-done = bf16[1024,18176]{1,0:T(8,128)(2,1)} async-done(((bf16[8,18176]{1,0:T(8,128)(2,1)}), bf16[1024,18176]{1,0:T(8,128)(2,1)}) %all-gather.2.cloned.1.call-update) | async-done | bytes 37224464 | tf_op jit(solution)/shard_map/all_gather | solution.py:31
  138.2 7.8 %slice.148 = bf16[1024,4608]{1,0:T(8,128)(2,1)} slice(bf16[1024,18176]{1,0:T(8,128)(2,1)} %all-gather.2.cloned.1.call-done), slice={[0:1024], [13568:18176]} | slice | bytes 18874368 | tf_op jit(solution)/shard_map/slice | solution.py:34
  146.0 17.5 %reshape.152 = bf16[4608,1024]{1,0:T(8,128)(2,1)} reshape(bf16[1024,4608]{1,0:T(8,128)(2,1)} %slice.148) | data formatting | bytes 18874368 | tf_op jit(solution)/shard_map/reshape | solution.py:161
  163.5 8.2 %convolution_bitcast_fusion = f32[128,4608]{1,0:T(8,128)} fusion(bf16[4608,1024]{1,0:T(8,128)(2,1)} %reshape.152, bf16[128,1024]{1,0:T(8,128)(2,1)S(1)} %copy-done.8), kind=kOutput, calls=%fused_computation.16 | convolution fusion | flops 1207959552 | bytes 12058624 | tf_op jit(solution)/shard_map/dot_general | solution.py:201
  177.9 5.2 %fusion.5 = f32[128,4608]{1,0:T(8,128)S(1)} fusion(bf16[128,1024]{1,0:T(8,128)(2,1)S(1)} %multiply_convert_fusion.6, bf16[1024,18176]{1,0:T(8,128)(2,1)} %all-gather.2.cloned.1.call-done), kind=kOutput, calls=%fused_computation.10 | convolution fusion | flops 1207959552 | bytes 12058624 | tf_op jit(solution)/shard_map/dot_general | solution.py:193
  183.2 5.9 %multiply_convert_fusion.1 = (bf16[128,4608]{1,0:T(8,128)(2,1)S(1)}, bf16[128,4608]{1,0:T(8,128)(2,1)S(1)}, bf16[128,4608]{1,0:T(8,128)(2,1)S(1)}) fusion(f32[128,4608]{1,0:T(8,128)S(1)} %copy-done.7, f32[128,4608]{1,0:T(8,128)S(1)} %fusion.5, bf16[128,1024]{1,0:T(8,128)(2,1)} %copy-done.19, bf16[1024,18176]{1,0:T(8,128)(2,1)} %all-gather.2.cloned.1.call-done), kind=kOutput, calls=%fused_computation.22 | convolution fusion | flops 1216806912 | bytes 17956864 | tf_op jit(solution)/shard_map/dot_general | solution.py:192
  194.8 10.8 %pad_maximum_fusion = bf16[1024,9216]{1,0:T(8,128)(2,1)} fusion(bf16[1024,4608]{1,0:T(8,128)(2,1)S(1)} %fusion.48, bf16[1024,4608]{1,0:T(8,128)(2,1)S(1)} %fusion.47), kind=kLoop, calls=%fused_computation | loop fusion | flops 37748736 | bytes 37748736 | tf_op jit(solution)/shard_map/concatenate | solution.py:106
  205.6 16.0 %shard_map.187 = bf16[512,9216]{1,0:T(8,128)(2,1)} custom-call(bf16[2,512,9216]{2,1,0:T(8,128)(2,1)} %bitcast.63), custom_call_target="tpu_custom_call" | custom-call | tf_op jit(solution)/shard_map/pallas_call | solution.py:82
  221.6 11.9 %fusion = bf16[512,9216]{1,0:T(8,128)(2,1)} fusion(bf16[512,9216]{1,0:T(8,128)(2,1)} %shard_map.187, bf16[2,512,9216]{2,1,0:T(8,128)(2,1)} %bitcast.64, s32[]{:T(128)S(6)} %select_n.8), kind=kLoop, calls=%fused_computation.2 | loop fusion | flops 18874368 | bytes 28311556 | tf_op jit(solution)/shard_map/convert_element_type | solution.py:93
  237.1 7.2 %fusion.3 = f32[128,1024]{1,0:T(8,128)S(1)} fusion(bf16[128,4608]{1,0:T(8,128)(2,1)} %copy-done.14, bf16[1024,18176]{1,0:T(8,128)(2,1)} %all-gather.2.cloned.1.call-done), kind=kOutput, calls=%fused_computation.8 | convolution fusion | flops 1207959552 | bytes 11141120 | tf_op jit(solution)/shard_map/dot_general | solution.py:227
  244.4 5.9 %multiply_reduce_fusion.3 = (f32[1024]{0:T(1024)S(1)}, f32[128]{0:T(128)S(1)}, f32[128,1024]{1,0:T(8,128)S(1)}) fusion(f32[128,1024]{1,0:T(8,128)S(1)} %get-tuple-element.75, f32[128]{0:T(128)S(1)} %get-tuple-element.73, f32[1024]{0:T(1024)S(1)} %get-tuple-element.40, f32[128,1024]{1,0:T(8,128)S(1)} %fusion.3, bf16[128,4608]{1,0:T(8,128)(2,1)S(1)} %copy-done.13, ...), kind=kOutput, calls=%fused_computation.59 | convolution fusion | flops 1208875904 | bytes 12198912 | tf_op jit(solution)/shard_map/dot_general | solution.py:226
  257.3 6.1 %fusion.34 = (f32[1024]{0:T(1024)S(1)}, f32[128]{0:T(128)S(1)}, f32[128,1024]{1,0:T(8,128)}) fusion(bf16[128,1024]{1,0:T(8,128)(2,1)S(1)} %copy-done.10, f32[128]{0:T(128)S(1)} %get-tuple-element.71, f32[1024]{0:T(1024)S(1)} %get-tuple-element.41, bf16[1024,18176]{1,0:T(8,128)(2,1)} %all-gather.2.cloned.1.call-done, ...), kind=kOutput, calls=%fused_computation.49 | convolution fusion | flops 808582016 | bytes 7873536 | tf_op jit(solution)/shard_map/dot_general | solution.py:263
  264.7 15.0 %all-to-all-start = ((f32[128,8,256]{2,1,0:T(8,128)}), f32[128,8,256]{2,1,0:T(8,128)S(1)}, u32[]{:S(2)}, u32[]{:S(2)}) async-start(f32[128,8,256]{2,1,0:T(8,128)} %pad_bitcast_fusion), calls=%async_computation | async-start | bytes 2097152 | tf_op jit(solution)/shard_map/all_to_all | solution.py:50
  279.7 5.7 %fusion.35 = bf16[1024,3072]{1,0:T(8,128)(2,1)} fusion(bf16[128,1024]{0,1:T(8,128)(2,1)} %bitcast.74, bf16[128,1024]{1,0:T(8,128)(2,1)} %copy-done.21, bf16[128,1024]{1,0:T(8,128)(2,1)} %copy-done.15, bf16[128,1024]{1,0:T(8,128)(2,1)} %copy-done.20), kind=kOutput, calls=%fused_computation.73 | convolution fusion | flops 807665664 | bytes 7340032 | tf_op jit(solution)/shard_map/dot_general | solution.py:257
  285.4 8.0 %pad_maximum_fusion.1 = bf16[1024,4096]{1,0:T(8,128)(2,1)} fusion(bf16[1024,1024]{1,0:T(8,128)(2,1)} %fusion.36, bf16[1024,3072]{1,0:T(8,128)(2,1)} %fusion.35), kind=kLoop, calls=%fused_computation.5 | loop fusion | flops 16777216 | bytes 16777216 | tf_op jit(solution)/shard_map/concatenate | solution.py:106
  293.4 7.5 %shard_map.186 = bf16[512,4096]{1,0:T(8,128)(2,1)} custom-call(bf16[2,512,4096]{2,1,0:T(8,128)(2,1)} %bitcast.65), custom_call_target="tpu_custom_call" | custom-call | tf_op jit(solution)/shard_map/pallas_call | solution.py:82
  300.9 7.3 %fusion.2 = bf16[512,4096]{1,0:T(8,128)(2,1)} fusion(bf16[512,4096]{1,0:T(8,128)(2,1)} %shard_map.186, bf16[2,512,4096]{2,1,0:T(8,128)(2,1)} %bitcast.66, s32[]{:T(128)S(6)} %select_n.8), kind=kLoop, calls=%fused_computation.7 | loop fusion | flops 8388608 | bytes 12582916 | tf_op jit(solution)/shard_map/convert_element_type | solution.py:93
  310.5 4.9 all-to-all-start.1
  322.4 5.0 fusion.49
  327.5 17.6 %reshape_reshape.3.x_ref = bf16[2,512,4608]{2,1,0:T(8,128)(2,1)} reshape(bf16[4608,1024]{1,0:T(8,128)(2,1)} %fusion.49) | data formatting | bytes 18874368 | tf_op jit(solution)/shard_map/reshape;reshape | solution.py:81
  345.1 8.3 %shard_map.188 = bf16[512,4608]{1,0:T(8,128)(2,1)} custom-call(bf16[2,512,4608]{2,1,0:T(8,128)(2,1)} %reshape_reshape.3.x_ref), custom_call_target="tpu_custom_call" | custom-call | tf_op jit(solution)/shard_map/pallas_call | solution.py:82
  353.4 7.1 %fusion.1 = bf16[512,4608]{1,0:T(8,128)(2,1)} fusion(bf16[512,4608]{1,0:T(8,128)(2,1)} %shard_map.188, bf16[2,512,4608]{2,1,0:T(8,128)(2,1)} %reshape_reshape.3.x_ref, s32[]{:T(128)S(6)} %select_n.8), kind=kLoop, calls=%fused_computation.4 | loop fusion | flops 9437184 | bytes 14155780 | tf_op jit(solution)/shard_map/convert_element_type | solution.py:93
  364.1 4.9 all-to-all-start.4
  369.0 4.3 reduce_sum.172
  373.4 60.7 %all-to-all-done.4 = bf16[4,128,4608]{2,1,0:T(8,128)(2,1)} async-done(((bf16[4,128,4608]{2,1,0:T(8,128)(2,1)}), bf16[4,128,4608]{2,1,0:T(8,128)(2,1)}, u32[]{:S(2)}, u32[]{:S(2)}) %all-to-all-start.4) | async-done | bytes 4718624 | tf_op jit(solution)/shard_map/all_to_all | solution.py:116
  434.1 4.2 all-to-all-start.2
  438.4 4.4 reduce_sum.175
  442.8 10.4 %all-to-all-done.2 = bf16[4,32,4096]{2,1,0:T(8,128)(2,1)S(1)} async-done(((bf16[4,32,4096]{2,1,0:T(8,128)(2,1)}), bf16[4,32,4096]{2,1,0:T(8,128)(2,1)S(1)}, u32[]{:S(2)}, u32[]{:S(2)}) %all-to-all-start.2) | async-done | bytes 1048608 | tf_op jit(solution)/shard_map/all_to_all | solution.py:116
  454.2 4.4 all-to-all-start.5
  459.2 5.8 %fusion.26 = bf16[128,1024]{1,0:T(8,128)(2,1)} fusion(f32[128,1024]{1,0:T(8,128)S(1)} %copy-done.3, bf16[128,4608]{1,0:T(8,128)(2,1)S(1)} %get-tuple-element.59, bf16[4608,1024]{1,0:T(8,128)(2,1)} %reshape.152), kind=kOutput, calls=%fused_computation.33 | convolution fusion | flops 1208221696 | bytes 11403264 | tf_op jit(solution)/shard_map/dot_general | solution.py:197
  467.2 9.3 %all-to-all-done.5 = bf16[4,32,4608]{2,1,0:T(8,128)(2,1)S(1)} async-done(((bf16[4,32,4608]{2,1,0:T(8,128)(2,1)}), bf16[4,32,4608]{2,1,0:T(8,128)(2,1)S(1)}, u32[]{:S(2)}, u32[]{:S(2)}) %all-to-all-start.5) | async-done | bytes 1179680 | tf_op jit(solution)/shard_map/all_to_all | solution.py:116
  480.9 5.7 %all-to-all-done.3 = bf16[4,8,4096]{2,1,0:T(8,128)(2,1)S(1)} async-done(((bf16[4,8,4096]{2,1,0:T(8,128)(2,1)}), bf16[4,8,4096]{2,1,0:T(8,128)(2,1)S(1)}, u32[]{:S(2)}, u32[]{:S(2)}) %all-to-all-start.3) | async-done | bytes 262176 | tf_op jit(solution)/shard_map/all_to_all | solution.py:116
  (137 shorter events, 78.0 us)
Async XLA Ops:
  7.2 122.4 %all-gather.2.cloned.1.call-start = ((), (), s32[]{:S(2)}) async-start(), calls=%async_computation.10 | async-start | bytes 37515264 | tf_op jit(solution)/shard_map/all_gather | solution.py:31
  14.6 338.8 %reduce-scatter.4.cloned.1.call-start = ((), (), s32[]{:S(2)}) async-start(), calls=%async_computation.11 | async-start | bytes 11796480 | tf_op jit(solution)/shard_map/reduce_scatter | solution.py:120
  15.4 2.4 collective-permute-start.1
  132.0 4.0 copy-start.16
  135.9 37.8 %copy-start = (f32[128,3072]{1,0:T(8,128)}, f32[128,3072]{1,0:T(8,128)S(1)}, u32[]{:S(2)}) copy-start(f32[128,3072]{1,0:T(8,128)S(1)} %fusion.13) | copy-start | bytes 4718596
  136.0 37.6 %collective-permute-start = (bf16[2,1024]{1,0:T(2,128)(2,1)S(1)}, bf16[2,1024]{1,0:T(2,128)(2,1)S(1)}, u32[]{:S(2)}, u32[]{:S(2)}) collective-permute-start(bf16[2,1024]{1,0:T(2,128)(2,1)S(1)} %slice.138), channel_id=1, source_target_pairs={{0,1},{1,2},{2,3},{3,4},{4,5},{5,6},{6,7},{7,8},{8,9},{9,10},{10,1... | collective-permute-start | bytes 12296 | tf_op jit(solution)/shard_map/ppermute | solution.py:16
  146.0 17.5 %copy-start.8 = (bf16[128,1024]{1,0:T(8,128)(2,1)S(1)}, bf16[128,1024]{1,0:T(8,128)(2,1)}, u32[]{:S(2)}) copy-start(bf16[128,1024]{1,0:T(8,128)(2,1)} %param.21) | copy-start | bytes 786436
  171.7 3.1 copy-start.10
  177.1 73.2 %copy-start.2 = (f32[128,1024]{1,0:T(8,128)}, f32[128,1024]{1,0:T(8,128)S(1)}, u32[]{:S(2)}) copy-start(f32[128,1024]{1,0:T(8,128)S(1)} %get-tuple-element.75) | copy-start | bytes 1572868
  177.9 5.2 %copy-start.7 = (f32[128,4608]{1,0:T(8,128)S(1)}, f32[128,4608]{1,0:T(8,128)}, u32[]{:S(2)}) copy-start(f32[128,4608]{1,0:T(8,128)} %convolution_bitcast_fusion) | copy-start | bytes 7077892
  189.1 2.8 copy-start.14
  237.1 7.2 %copy-start.13 = (bf16[128,4608]{1,0:T(8,128)(2,1)S(1)}, bf16[128,4608]{1,0:T(8,128)(2,1)}, u32[]{:S(2)}) copy-start(bf16[128,4608]{1,0:T(8,128)(2,1)} %copy-done.12) | copy-start | bytes 3538948
  250.2 2.9 copy-start.1
  250.2 2.9 copy-start.11
  250.5 4.4 copy-start.18
  253.4 3.9 copy-start.15
  253.6 3.5 collective-permute-start.2
  257.3 6.1 %copy-start.20 = (bf16[128,1024]{1,0:T(8,128)(2,1)}, bf16[128,1024]{1,0:T(8,128)(2,1)S(1)}, u32[]{:S(2)}) copy-start(bf16[128,1024]{1,0:T(8,128)(2,1)S(1)} %get-tuple-element.60) | copy-start | bytes 786436
  257.3 6.1 %copy-start.21 = (bf16[128,1024]{1,0:T(8,128)(2,1)}, bf16[128,1024]{1,0:T(8,128)(2,1)S(1)}, u32[]{:S(2)}) copy-start(bf16[128,1024]{1,0:T(8,128)(2,1)S(1)} %get-tuple-element.61) | copy-start | bytes 786436
  264.7 45.8 %all-to-all-start = ((f32[128,8,256]{2,1,0:T(8,128)}), f32[128,8,256]{2,1,0:T(8,128)S(1)}, u32[]{:S(2)}, u32[]{:S(2)}) async-start(f32[128,8,256]{2,1,0:T(8,128)} %pad_bitcast_fusion), calls=%async_computation | async-start | bytes 2097152 | tf_op jit(solution)/shard_map/all_to_all | solution.py:50
  310.5 4.9 copy-start.4
  310.5 53.6 %all-to-all-start.1 = ((bf16[4,128,4096]{2,1,0:T(8,128)(2,1)}), bf16[4,128,4096]{2,1,0:T(8,128)(2,1)}, u32[]{:S(2)}, u32[]{:S(2)}) async-start(bf16[4,128,4096]{2,1,0:T(8,128)(2,1)} %bitcast.68), calls=%async_computation.1 | async-start | bytes 8388608 | tf_op jit(solution)/shard_map/all_to_all | solution.py:116
  315.4 143.3 %reduce-scatter.6.cloned.1.call-start = ((), (), s32[]{:S(2)}) async-start(), calls=%async_computation.12 | async-start | bytes 2949120 | tf_op jit(solution)/shard_map/reduce_scatter | solution.py:120
  315.4 7.0 %copy-start.9 = (bf16[128,1024]{1,0:T(8,128)(2,1)S(1)}, bf16[128,1024]{1,0:T(8,128)(2,1)}, u32[]{:S(2)}) copy-start(bf16[128,1024]{1,0:T(8,128)(2,1)} %param.21) | copy-start | bytes 786436
  364.1 70.0 %all-to-all-start.4 = ((bf16[4,128,4608]{2,1,0:T(8,128)(2,1)}), bf16[4,128,4608]{2,1,0:T(8,128)(2,1)}, u32[]{:S(2)}, u32[]{:S(2)}) async-start(bf16[4,128,4608]{2,1,0:T(8,128)(2,1)} %bitcast.67), calls=%async_computation.7 | async-start | bytes 9437184 | tf_op jit(solution)/shard_map/all_to_all | solution.py:116
  434.1 19.1 %all-to-all-start.2 = ((bf16[4,32,4096]{2,1,0:T(8,128)(2,1)}), bf16[4,32,4096]{2,1,0:T(8,128)(2,1)S(1)}, u32[]{:S(2)}, u32[]{:S(2)}) async-start(bf16[4,32,4096]{2,1,0:T(8,128)(2,1)} %bitcast.71), calls=%async_computation.2 | async-start | bytes 2097152 | tf_op jit(solution)/shard_map/all_to_all | solution.py:116
  438.4 20.8 %copy-start.3 = (f32[128,1024]{1,0:T(8,128)S(1)}, f32[128,1024]{1,0:T(8,128)}, u32[]{:S(2)}) copy-start(f32[128,1024]{1,0:T(8,128)} %copy-done.2) | copy-start | bytes 1572868
  454.2 22.3 %all-to-all-start.5 = ((bf16[4,32,4608]{2,1,0:T(8,128)(2,1)}), bf16[4,32,4608]{2,1,0:T(8,128)(2,1)S(1)}, u32[]{:S(2)}, u32[]{:S(2)}) async-start(bf16[4,32,4608]{2,1,0:T(8,128)(2,1)} %bitcast.70), calls=%async_computation.8 | async-start | bytes 2359296 | tf_op jit(solution)/shard_map/all_to_all | solution.py:116
  458.6 39.0 %reduce-scatter.8.cloned.1.call-start = ((), (), s32[]{:S(2)}) async-start(), calls=%async_computation.13 | async-start | bytes 737280 | tf_op jit(solution)/shard_map/reduce_scatter | solution.py:120
  465.0 27.2 %copy-start.5 = (f32[128,8,256]{2,1,0:T(8,128)S(1)}, f32[128,8,256]{2,1,0:T(8,128)}, u32[]{:S(2)}) copy-start(f32[128,8,256]{2,1,0:T(8,128)} %copy-done.4) | copy-start | bytes 3145732
  476.5 10.1 %all-to-all-start.3 = ((bf16[4,8,4096]{2,1,0:T(8,128)(2,1)}), bf16[4,8,4096]{2,1,0:T(8,128)(2,1)S(1)}, u32[]{:S(2)}, u32[]{:S(2)}) async-start(bf16[4,8,4096]{2,1,0:T(8,128)(2,1)} %bitcast.19), calls=%async_computation.3 | async-start | bytes 524288 | tf_op jit(solution)/shard_map/all_to_all | solution.py:116
  486.5 10.3 %all-to-all-start.6 = ((bf16[4,8,4608]{2,1,0:T(8,128)(2,1)}), bf16[4,8,4608]{2,1,0:T(8,128)(2,1)S(1)}, u32[]{:S(2)}, u32[]{:S(2)}) async-start(bf16[4,8,4608]{2,1,0:T(8,128)(2,1)} %bitcast.29), calls=%async_computation.9 | async-start | bytes 589824 | tf_op jit(solution)/shard_map/all_to_all | solution.py:116
  (6 other events, 8.4 us)
Sparse Core Ops, SparseCore 0:
  14.7 114.7 all-gather.1
  233.6 100.4 reduce-scatter.3
  353.5 41.7 reduce-scatter.5
  461.5 20.2 reduce-scatter.7

commit v11 on v10

--- a/solution.py
+++ b/solution.py
@@ -218,7 +218,7 @@
     )
     own_gate, own_up = scatter_packed([g_gate, g_up], order=ORDER_UP)
     (own_down,) = scatter_packed(
-        [g_down.reshape(n * per, -1)],
+        [g_down],
         order=ORDER_DOWN,
         direct=True,
         collective_id=1,

time: 508 us -> 495 us (0.974)
  local copies, waits for them, and re-layouts: 69.9 us -> 52.3 us
    another operation x1 -> x0, local copies, waits for them, and re-layouts: 17.6 us -> none  [pair_exchange(): halves = blocks.reshape(2, blocks.shape[0] // 2, blocks.shape[1])]
  transfers between devices with their start and end apart: 14 -> 14, of which waited for: 8 -> 8; matrix products, arithmetic and copies ran while one was open for 29% -> 27% of each run, Pallas kernels for 3% -> 3%
where the time goes in v11:
time: 495 us; the launch traced here: 490 us
  waiting for transfers between devices  204 us (41%)
  matrix products  71.3 us (14%)
  other arithmetic  71.2 us (14%)
  local copies, waits for them, and re-layouts  52.3 us (11%)
  starting transfers between devices  44.2 us (9%)
  Pallas kernels  31.8 us (6%)
  between operations  14.9 us (3%)
    all_gather x1, waiting for transfers between devices, gather_packed(): full = lax.all_gather(packed, AXES, axis=0, tiled=True)  110 us
    all_to_all x6, waiting for transfers between devices, scatter_packed(): got = lax.all_to_all(blocks, axis, 0, 0, tiled=True)  90.9 us
    pallas_call x3, Pallas kernels, pair_exchange(): pl.pallas_call(pair_kernel, out_shape=jax.ShapeDtypeStruct(halves.shape[1...  31.8 us
    convert_element_type x3, other arithmetic, pair_exchange(): (own.astype(jnp.float32) + received.astype(jnp.float32)).astype(jnp.bfloa...  27.8 us
    all_to_all x6, starting transfers between devices, scatter_packed(): got = lax.all_to_all(blocks, axis, 0, 0, tiled=True)  24.3 us
    concatenate x2, other arithmetic, scatter_packed(): packed = jnp.concatenate(pieces, axis=1).astype(jnp.bfloat16)  18.8 us
    reshape x1, local copies, waits for them, and re-layouts, per_device(): w_down = w_down_packed.reshape(n * down_rows, width)  17.6 us
    all_to_all x1, starting transfers between devices, exchange_packed(): blocks = lax.all_to_all(packed.astype(dtype), AXES, 0, 0, tiled=True)  15 us
  transfers between devices with their start and end apart: 14, of which 8 were waited for; matrix products, arithmetic and copies ran while one was open for 27% of the time, Pallas kernels for 3%

profile of v11, /device:TPU:0, one launch (start us, length us, event | category | flops | bytes accessed | tf_op | source)
XLA Modules:
  0.0 489.8 jit_solution(10587142110253765782)
XLA Ops:
  19.3 110.3 %all-gather.2.cloned.1.call-done = bf16[1024,18176]{1,0:T(8,128)(2,1)} async-done(((bf16[8,18176]{1,0:T(8,128)(2,1)}), bf16[1024,18176]{1,0:T(8,128)(2,1)}) %all-gather.2.cloned.1.call-update) | async-done | bytes 37224464 | tf_op jit(solution)/shard_map/all_gather | solution.py:31
  132.0 3.9 fusion.13
  138.2 7.8 %slice.148 = bf16[1024,4608]{1,0:T(8,128)(2,1)} slice(bf16[1024,18176]{1,0:T(8,128)(2,1)} %all-gather.2.cloned.1.call-done), slice={[0:1024], [13568:18176]} | slice | bytes 18874368 | tf_op jit(solution)/shard_map/slice | solution.py:34
  146.0 17.6 %reshape.148 = bf16[4608,1024]{1,0:T(8,128)(2,1)} reshape(bf16[1024,4608]{1,0:T(8,128)(2,1)} %slice.148) | data formatting | bytes 18874368 | tf_op jit(solution)/shard_map/reshape | solution.py:161
  163.6 8.2 %convolution_bitcast_fusion = f32[128,4608]{1,0:T(8,128)} fusion(bf16[4608,1024]{1,0:T(8,128)(2,1)} %reshape.148, bf16[128,1024]{1,0:T(8,128)(2,1)S(1)} %copy-done.8), kind=kOutput, calls=%fused_computation.16 | convolution fusion | flops 1207959552 | bytes 12058624 | tf_op jit(solution)/shard_map/dot_general | solution.py:201
  178.1 5.2 %fusion.5 = f32[128,4608]{1,0:T(8,128)S(1)} fusion(bf16[128,1024]{1,0:T(8,128)(2,1)S(1)} %multiply_convert_fusion.6, bf16[1024,18176]{1,0:T(8,128)(2,1)} %all-gather.2.cloned.1.call-done), kind=kOutput, calls=%fused_computation.10 | convolution fusion | flops 1207959552 | bytes 12058624 | tf_op jit(solution)/shard_map/dot_general | solution.py:193
  183.3 5.9 %multiply_convert_fusion.1 = (bf16[128,4608]{1,0:T(8,128)(2,1)S(1)}, bf16[128,4608]{1,0:T(8,128)(2,1)S(1)}, bf16[128,4608]{1,0:T(8,128)(2,1)S(1)}) fusion(f32[128,4608]{1,0:T(8,128)S(1)} %copy-done.7, f32[128,4608]{1,0:T(8,128)S(1)} %fusion.5, bf16[128,1024]{1,0:T(8,128)(2,1)} %copy-done.20, bf16[1024,18176]{1,0:T(8,128)(2,1)} %all-gather.2.cloned.1.call-done), kind=kOutput, calls=%fused_computation.22 | convolution fusion | flops 1216806912 | bytes 17956864 | tf_op jit(solution)/shard_map/dot_general | solution.py:192
  194.9 10.8 %pad_maximum_fusion = bf16[1024,9216]{1,0:T(8,128)(2,1)} fusion(bf16[1024,4608]{1,0:T(8,128)(2,1)S(1)} %fusion.50, bf16[1024,4608]{1,0:T(8,128)(2,1)S(1)} %fusion.49), kind=kLoop, calls=%fused_computation | loop fusion | flops 37748736 | bytes 37748736 | tf_op jit(solution)/shard_map/concatenate | solution.py:106
  205.7 16.0 %shard_map.187 = bf16[512,9216]{1,0:T(8,128)(2,1)} custom-call(bf16[2,512,9216]{2,1,0:T(8,128)(2,1)} %bitcast.67), custom_call_target="tpu_custom_call" | custom-call | tf_op jit(solution)/shard_map/pallas_call | solution.py:82
  221.7 12.1 %fusion = bf16[512,9216]{1,0:T(8,128)(2,1)} fusion(bf16[512,9216]{1,0:T(8,128)(2,1)} %shard_map.187, bf16[2,512,9216]{2,1,0:T(8,128)(2,1)} %bitcast.68, s32[]{:T(128)S(6)} %select_n.8), kind=kLoop, calls=%fused_computation.2 | loop fusion | flops 18874368 | bytes 28311556 | tf_op jit(solution)/shard_map/convert_element_type | solution.py:93
  237.4 7.2 %fusion.3 = f32[128,1024]{1,0:T(8,128)S(1)} fusion(bf16[128,4608]{1,0:T(8,128)(2,1)} %copy-done.15, bf16[1024,18176]{1,0:T(8,128)(2,1)} %all-gather.2.cloned.1.call-done), kind=kOutput, calls=%fused_computation.8 | convolution fusion | flops 1207959552 | bytes 11141120 | tf_op jit(solution)/shard_map/dot_general | solution.py:227
  244.7 5.9 %multiply_reduce_fusion.3 = (f32[1024]{0:T(1024)S(1)}, f32[128]{0:T(128)S(1)}, f32[128,1024]{1,0:T(8,128)S(1)}) fusion(f32[128,1024]{1,0:T(8,128)S(1)} %get-tuple-element.75, f32[128]{0:T(128)S(1)} %get-tuple-element.73, f32[1024]{0:T(1024)S(1)} %get-tuple-element.40, f32[128,1024]{1,0:T(8,128)S(1)} %fusion.3, bf16[128,4608]{1,0:T(8,128)(2,1)S(1)} %copy-done.14, ...), kind=kOutput, calls=%fused_computation.59 | convolution fusion | flops 1208875904 | bytes 12198912 | tf_op jit(solution)/shard_map/dot_general | solution.py:226
  257.6 6.1 %fusion.34 = (f32[1024]{0:T(1024)S(1)}, f32[128]{0:T(128)S(1)}, f32[128,1024]{1,0:T(8,128)}) fusion(bf16[128,1024]{1,0:T(8,128)(2,1)S(1)} %copy-done.10, f32[128]{0:T(128)S(1)} %get-tuple-element.71, f32[1024]{0:T(1024)S(1)} %get-tuple-element.41, bf16[1024,18176]{1,0:T(8,128)(2,1)} %all-gather.2.cloned.1.call-done, ...), kind=kOutput, calls=%fused_computation.49 | convolution fusion | flops 808582016 | bytes 7873536 | tf_op jit(solution)/shard_map/dot_general | solution.py:263
  265.0 15.0 %all-to-all-start = ((f32[128,8,256]{2,1,0:T(8,128)}), f32[128,8,256]{2,1,0:T(8,128)S(1)}, u32[]{:S(2)}, u32[]{:S(2)}) async-start(f32[128,8,256]{2,1,0:T(8,128)} %pad_bitcast_fusion), calls=%async_computation | async-start | bytes 2097152 | tf_op jit(solution)/shard_map/all_to_all | solution.py:50
  280.0 5.7 %fusion.35 = bf16[1024,3072]{1,0:T(8,128)(2,1)} fusion(bf16[128,1024]{0,1:T(8,128)(2,1)} %bitcast.79, bf16[128,1024]{1,0:T(8,128)(2,1)} %copy-done.22, bf16[128,1024]{1,0:T(8,128)(2,1)} %copy-done.16, bf16[128,1024]{1,0:T(8,128)(2,1)} %copy-done.21), kind=kOutput, calls=%fused_computation.73 | convolution fusion | flops 807665664 | bytes 7340032 | tf_op jit(solution)/shard_map/dot_general | solution.py:257
  285.7 8.0 %pad_maximum_fusion.1 = bf16[1024,4096]{1,0:T(8,128)(2,1)} fusion(bf16[1024,1024]{1,0:T(8,128)(2,1)} %fusion.38, bf16[1024,3072]{1,0:T(8,128)(2,1)} %fusion.35), kind=kLoop, calls=%fused_computation.5 | loop fusion | flops 16777216 | bytes 16777216 | tf_op jit(solution)/shard_map/concatenate | solution.py:106
  293.6 7.5 %shard_map.186 = bf16[512,4096]{1,0:T(8,128)(2,1)} custom-call(bf16[2,512,4096]{2,1,0:T(8,128)(2,1)} %bitcast.69), custom_call_target="tpu_custom_call" | custom-call | tf_op jit(solution)/shard_map/pallas_call | solution.py:82
  301.2 7.3 %fusion.2 = bf16[512,4096]{1,0:T(8,128)(2,1)} fusion(bf16[512,4096]{1,0:T(8,128)(2,1)} %shard_map.186, bf16[2,512,4096]{2,1,0:T(8,128)(2,1)} %bitcast.70, s32[]{:T(128)S(6)} %select_n.8), kind=kLoop, calls=%fused_computation.7 | loop fusion | flops 8388608 | bytes 12582916 | tf_op jit(solution)/shard_map/convert_element_type | solution.py:93
  310.8 4.8 all-to-all-start.1
  322.7 5.0 %fusion.36.x_ref = bf16[2,2304,1024]{2,1,0:T(8,128)(2,1)} fusion(bf16[2,2304,128]{2,1,0:T(8,128)(2,1)S(1)} %bitcast.75, bf16[128,1024]{1,0:T(8,128)(2,1)S(1)} %copy-done.9), kind=kOutput, calls=%fused_computation.76 | convolution fusion | flops 1207959552 | bytes 10878976 | tf_op jit(solution)/shard_map/dot_general | solution.py:207
  327.7 8.3 %shard_map.188 = bf16[2304,1024]{1,0:T(8,128)(2,1)} custom-call(bf16[2,2304,1024]{2,1,0:T(8,128)(2,1)} %fusion.36.x_ref), custom_call_target="tpu_custom_call" | custom-call | tf_op jit(solution)/shard_map/pallas_call | solution.py:82
  336.0 8.4 %fusion.1 = bf16[2304,1024]{1,0:T(8,128)(2,1)} fusion(bf16[2304,1024]{1,0:T(8,128)(2,1)} %shard_map.188, bf16[2,2304,1024]{2,1,0:T(8,128)(2,1)} %fusion.36.x_ref, s32[]{:T(128)S(6)} %select_n.8), kind=kLoop, calls=%fused_computation.4 | loop fusion | flops 9437184 | bytes 14155780 | tf_op jit(solution)/shard_map/convert_element_type | solution.py:93
  344.4 20.0 %all-to-all-done.1 = bf16[4,128,4096]{2,1,0:T(8,128)(2,1)} async-done(((bf16[4,128,4096]{2,1,0:T(8,128)(2,1)}), bf16[4,128,4096]{2,1,0:T(8,128)(2,1)}, u32[]{:S(2)}, u32[]{:S(2)}) %all-to-all-start.1) | async-done | bytes 4194336 | tf_op jit(solution)/shard_map/all_to_all | solution.py:116
  364.4 4.9 %all-to-all-start.4 = ((bf16[4,576,1024]{2,1,0:T(8,128)(2,1)}), bf16[4,576,1024]{2,1,0:T(8,128)(2,1)}, u32[]{:S(2)}, u32[]{:S(2)}) async-start(bf16[4,576,1024]{2,1,0:T(8,128)(2,1)} %bitcast.71), calls=%async_computation.7 | async-start | bytes 9437184 | tf_op jit(solution)/shard_map/all_to_all | solution.py:116
  369.3 4.2 reduce_sum.172
  373.6 49.3 %all-to-all-done.4 = bf16[4,576,1024]{2,1,0:T(8,128)(2,1)} async-done(((bf16[4,576,1024]{2,1,0:T(8,128)(2,1)}), bf16[4,576,1024]{2,1,0:T(8,128)(2,1)}, u32[]{:S(2)}, u32[]{:S(2)}) %all-to-all-start.4) | async-done | bytes 4718624 | tf_op jit(solution)/shard_map/all_to_all | solution.py:116
  426.4 4.8 reduce_sum.175
  431.2 8.5 %all-to-all-done.2 = bf16[4,32,4096]{2,1,0:T(8,128)(2,1)S(1)} async-done(((bf16[4,32,4096]{2,1,0:T(8,128)(2,1)}), bf16[4,32,4096]{2,1,0:T(8,128)(2,1)S(1)}, u32[]{:S(2)}, u32[]{:S(2)}) %all-to-all-start.2) | async-done | bytes 1048608 | tf_op jit(solution)/shard_map/all_to_all | solution.py:116
  444.8 5.8 %fusion.26 = bf16[128,1024]{1,0:T(8,128)(2,1)} fusion(f32[128,1024]{1,0:T(8,128)S(1)} %copy-done.3, bf16[128,4608]{1,0:T(8,128)(2,1)S(1)} %get-tuple-element.59, bf16[4608,1024]{1,0:T(8,128)(2,1)} %reshape.148), kind=kOutput, calls=%fused_computation.33 | convolution fusion | flops 1208221696 | bytes 11403264 | tf_op jit(solution)/shard_map/dot_general | solution.py:197
  452.8 6.3 %all-to-all-done.5 = bf16[4,144,1024]{2,1,0:T(8,128)(2,1)S(1)} async-done(((bf16[4,144,1024]{2,1,0:T(8,128)(2,1)}), bf16[4,144,1024]{2,1,0:T(8,128)(2,1)S(1)}, u32[]{:S(2)}, u32[]{:S(2)}) %all-to-all-start.5) | async-done | bytes 1179680 | tf_op jit(solution)/shard_map/all_to_all | solution.py:116
  459.2 4.0 all-to-all-start.3
  464.2 5.7 %all-to-all-done.3 = bf16[4,8,4096]{2,1,0:T(8,128)(2,1)} async-done(((bf16[4,8,4096]{2,1,0:T(8,128)(2,1)}), bf16[4,8,4096]{2,1,0:T(8,128)(2,1)}, u32[]{:S(2)}, u32[]{:S(2)}) %all-to-all-start.3) | async-done | bytes 262176 | tf_op jit(solution)/shard_map/all_to_all | solution.py:116
  (139 shorter events, 74.3 us)
Async XLA Ops:
  7.2 122.4 %all-gather.2.cloned.1.call-start = ((), (), s32[]{:S(2)}) async-start(), calls=%async_computation.10 | async-start | bytes 37515264 | tf_op jit(solution)/shard_map/all_gather | solution.py:31
  14.6 321.4 %reduce-scatter.4.cloned.1.call-start = ((), (), s32[]{:S(2)}) async-start(), calls=%async_computation.11 | async-start | bytes 11796480 | tf_op jit(solution)/shard_map/reduce_scatter | solution.py:120
  15.4 2.4 collective-permute-start.1
  132.0 4.0 copy-start.17
  135.9 37.9 %copy-start = (f32[128,3072]{1,0:T(8,128)}, f32[128,3072]{1,0:T(8,128)S(1)}, u32[]{:S(2)}) copy-start(f32[128,3072]{1,0:T(8,128)S(1)} %fusion.13) | copy-start | bytes 4718596
  136.0 37.7 %collective-permute-start = (bf16[2,1024]{1,0:T(2,128)(2,1)S(1)}, bf16[2,1024]{1,0:T(2,128)(2,1)S(1)}, u32[]{:S(2)}, u32[]{:S(2)}) collective-permute-start(bf16[2,1024]{1,0:T(2,128)(2,1)S(1)} %slice.138), channel_id=1, source_target_pairs={{0,1},{1,2},{2,3},{3,4},{4,5},{5,6},{6,7},{7,8},{8,9},{9,10},{10,1... | collective-permute-start | bytes 12296 | tf_op jit(solution)/shard_map/ppermute | solution.py:16
  146.0 17.6 %copy-start.8 = (bf16[128,1024]{1,0:T(8,128)(2,1)S(1)}, bf16[128,1024]{1,0:T(8,128)(2,1)}, u32[]{:S(2)}) copy-start(bf16[128,1024]{1,0:T(8,128)(2,1)} %param.21) | copy-start | bytes 786436
  171.8 3.1 copy-start.10
  177.2 73.4 %copy-start.2 = (f32[128,1024]{1,0:T(8,128)}, f32[128,1024]{1,0:T(8,128)S(1)}, u32[]{:S(2)}) copy-start(f32[128,1024]{1,0:T(8,128)S(1)} %get-tuple-element.75) | copy-start | bytes 1572868
  178.0 5.2 %copy-start.7 = (f32[128,4608]{1,0:T(8,128)S(1)}, f32[128,4608]{1,0:T(8,128)}, u32[]{:S(2)}) copy-start(f32[128,4608]{1,0:T(8,128)} %convolution_bitcast_fusion) | copy-start | bytes 7077892
  237.4 7.2 %copy-start.14 = (bf16[128,4608]{1,0:T(8,128)(2,1)S(1)}, bf16[128,4608]{1,0:T(8,128)(2,1)}, u32[]{:S(2)}) copy-start(bf16[128,4608]{1,0:T(8,128)(2,1)} %copy-done.13) | copy-start | bytes 3538948
  250.6 2.9 copy-start.1
  250.6 2.9 copy-start.12
  250.8 4.4 copy-start.19
  253.7 3.9 copy-start.16
  253.9 3.5 collective-permute-start.2
  257.6 6.1 %copy-start.21 = (bf16[128,1024]{1,0:T(8,128)(2,1)}, bf16[128,1024]{1,0:T(8,128)(2,1)S(1)}, u32[]{:S(2)}) copy-start(bf16[128,1024]{1,0:T(8,128)(2,1)S(1)} %get-tuple-element.60) | copy-start | bytes 786436
  257.6 6.1 %copy-start.22 = (bf16[128,1024]{1,0:T(8,128)(2,1)}, bf16[128,1024]{1,0:T(8,128)(2,1)S(1)}, u32[]{:S(2)}) copy-start(bf16[128,1024]{1,0:T(8,128)(2,1)S(1)} %get-tuple-element.61) | copy-start | bytes 786436
  265.0 45.8 %all-to-all-start = ((f32[128,8,256]{2,1,0:T(8,128)}), f32[128,8,256]{2,1,0:T(8,128)S(1)}, u32[]{:S(2)}, u32[]{:S(2)}) async-start(f32[128,8,256]{2,1,0:T(8,128)} %pad_bitcast_fusion), calls=%async_computation | async-start | bytes 2097152 | tf_op jit(solution)/shard_map/all_to_all | solution.py:50
  310.8 4.9 %copy-start.4 = (f32[128,8,256]{2,1,0:T(8,128)}, f32[128,8,256]{2,1,0:T(8,128)S(1)}, u32[]{:S(2)}) copy-start(f32[128,8,256]{2,1,0:T(8,128)S(1)} %all-to-all-done) | copy-start | bytes 3145732
  310.8 53.6 %all-to-all-start.1 = ((bf16[4,128,4096]{2,1,0:T(8,128)(2,1)}), bf16[4,128,4096]{2,1,0:T(8,128)(2,1)}, u32[]{:S(2)}, u32[]{:S(2)}) async-start(bf16[4,128,4096]{2,1,0:T(8,128)(2,1)} %bitcast.72), calls=%async_computation.1 | async-start | bytes 8388608 | tf_op jit(solution)/shard_map/all_to_all | solution.py:116
  315.6 128.6 %reduce-scatter.6.cloned.1.call-start = ((), (), s32[]{:S(2)}) async-start(), calls=%async_computation.12 | async-start | bytes 2949120 | tf_op jit(solution)/shard_map/reduce_scatter | solution.py:120
  315.7 7.0 %copy-start.9 = (bf16[128,1024]{1,0:T(8,128)(2,1)S(1)}, bf16[128,1024]{1,0:T(8,128)(2,1)}, u32[]{:S(2)}) copy-start(bf16[128,1024]{1,0:T(8,128)(2,1)} %param.21) | copy-start | bytes 786436
  364.4 58.4 %all-to-all-start.4 = ((bf16[4,576,1024]{2,1,0:T(8,128)(2,1)}), bf16[4,576,1024]{2,1,0:T(8,128)(2,1)}, u32[]{:S(2)}, u32[]{:S(2)}) async-start(bf16[4,576,1024]{2,1,0:T(8,128)(2,1)} %bitcast.71), calls=%async_computation.7 | async-start | bytes 9437184 | tf_op jit(solution)/shard_map/all_to_all | solution.py:116
  422.8 16.9 %all-to-all-start.2 = ((bf16[4,32,4096]{2,1,0:T(8,128)(2,1)}), bf16[4,32,4096]{2,1,0:T(8,128)(2,1)S(1)}, u32[]{:S(2)}, u32[]{:S(2)}) async-start(bf16[4,32,4096]{2,1,0:T(8,128)(2,1)} %bitcast.76), calls=%async_computation.2 | async-start | bytes 2097152 | tf_op jit(solution)/shard_map/all_to_all | solution.py:116
  426.4 18.4 %copy-start.3 = (f32[128,1024]{1,0:T(8,128)S(1)}, f32[128,1024]{1,0:T(8,128)}, u32[]{:S(2)}) copy-start(f32[128,1024]{1,0:T(8,128)} %copy-done.2) | copy-start | bytes 1572868
  440.7 18.5 %all-to-all-start.5 = ((bf16[4,144,1024]{2,1,0:T(8,128)(2,1)}), bf16[4,144,1024]{2,1,0:T(8,128)(2,1)S(1)}, u32[]{:S(2)}, u32[]{:S(2)}) async-start(bf16[4,144,1024]{2,1,0:T(8,128)(2,1)} %bitcast.74), calls=%async_computation.8 | async-start | bytes 2359296 | tf_op jit(solution)/shard_map/all_to_all | solution.py:116
  444.2 37.0 %reduce-scatter.8.cloned.1.call-start = ((), (), s32[]{:S(2)}) async-start(), calls=%async_computation.13 | async-start | bytes 737280 | tf_op jit(solution)/shard_map/reduce_scatter | solution.py:120
  450.6 22.9 %copy-start.11 = (bf16[128,1024]{1,0:T(8,128)(2,1)S(1)}, bf16[128,1024]{1,0:T(8,128)(2,1)}, u32[]{:S(2)}) copy-start(bf16[128,1024]{1,0:T(8,128)(2,1)} %param.11) | copy-start | bytes 786436
  450.6 24.9 %copy-start.5 = (f32[128,8,256]{2,1,0:T(8,128)S(1)}, f32[128,8,256]{2,1,0:T(8,128)}, u32[]{:S(2)}) copy-start(f32[128,8,256]{2,1,0:T(8,128)} %copy-done.4) | copy-start | bytes 3145732
  459.2 10.8 %all-to-all-start.3 = ((bf16[4,8,4096]{2,1,0:T(8,128)(2,1)}), bf16[4,8,4096]{2,1,0:T(8,128)(2,1)}, u32[]{:S(2)}, u32[]{:S(2)}) async-start(bf16[4,8,4096]{2,1,0:T(8,128)(2,1)} %bitcast.19), calls=%async_computation.3 | async-start | bytes 524288 | tf_op jit(solution)/shard_map/all_to_all | solution.py:116
  470.0 10.5 %all-to-all-start.6 = ((bf16[4,36,1024]{2,1,0:T(8,128)(2,1)}), bf16[4,36,1024]{2,1,0:T(8,128)(2,1)S(1)}, u32[]{:S(2)}, u32[]{:S(2)}) async-start(bf16[4,36,1024]{2,1,0:T(8,128)(2,1)} %all_to_all.54), calls=%async_computation.9 | async-start | bytes 655360 | tf_op jit(solution)/shard_map/all_to_all | solution.py:116
  (7 other events, 11.2 us)
Sparse Core Ops, SparseCore 0:
  14.7 114.7 all-gather.1
  233.9 100.4 reduce-scatter.3
  336.8 31.8 reduce-scatter.5
  447.1 20.0 reduce-scatter.7

commit v12 on v11

--- a/solution.py
+++ b/solution.py
@@ -77,7 +77,7 @@
     copy.wait()
 
 
-def pair_exchange(blocks, collective_id):
+def pair_exchange(blocks, collective_id, dtype=jnp.bfloat16):
     halves = blocks.reshape(2, blocks.shape[0] // 2, blocks.shape[1])
     received = pl.pallas_call(
         pair_kernel,
@@ -90,7 +90,7 @@
         ),
     )(halves)
     own = lax.dynamic_index_in_dim(halves, lax.axis_index("core"), 0, keepdims=False)
-    return (own.astype(jnp.float32) + received.astype(jnp.float32)).astype(jnp.bfloat16)
+    return (own.astype(jnp.float32) + received.astype(jnp.float32)).astype(dtype)
 
 
 def in_stage_order(values, order):
@@ -101,21 +101,23 @@
     return grid.reshape(values.shape)
 
 
-def scatter_packed(pieces, order=("core", "x", "z", "y"), direct=False, collective_id=0):
+def scatter_packed(
+    pieces, order=("core", "x", "z", "y"), direct=False, collective_id=0, dtype=jnp.bfloat16
+):
     widths = [p.shape[1] for p in pieces]
-    packed = jnp.concatenate(pieces, axis=1).astype(jnp.bfloat16)
+    packed = jnp.concatenate(pieces, axis=1).astype(dtype)
     sizes = [lax.axis_size(a) for a in AXES]
     count = sizes[0] * sizes[1] * sizes[2] * sizes[3]
     per = packed.shape[0] // count
     blocks = packed
     for axis in order:
         if axis == "core":
-            blocks = pair_exchange(blocks, collective_id)
+            blocks = pair_exchange(blocks, collective_id, dtype)
         elif direct:
             size = lax.axis_size(axis)
             got = lax.all_to_all(blocks, axis, 0, 0, tiled=True)
             got = got.reshape(size, got.shape[0] // size, got.shape[1])
-            blocks = jnp.sum(got.astype(jnp.float32), axis=0).astype(jnp.bfloat16)
+            blocks = jnp.sum(got.astype(jnp.float32), axis=0).astype(dtype)
         else:
             blocks = lax.psum_scatter(blocks, axis, scatter_dimension=0, tiled=True)
     mine = lax.optimization_barrier(blocks).astype(jnp.float32)
@@ -270,7 +272,14 @@
     own_in, own_out = scatter_packed(
         [g_in, g_out], order=ORDER_IN, direct=True, collective_id=2
     )
-    (own_small,) = exchange_packed([pad_cols(g_small)])
+    g_small = in_stage_order(g_small.T, ORDER_IN).T
+    (own_small,) = scatter_packed(
+        [pad_cols(g_small)],
+        order=ORDER_IN,
+        direct=True,
+        collective_id=3,
+        dtype=jnp.float32,
+    )
     return (
         block_out,
         input_grad,

time: 495 us -> 508 us (1.026)
    all_to_all x6 -> x9, starting transfers between devices: 24.3 us -> 41.4 us  [scatter_packed(): got = lax.all_to_all(blocks, axis, 0, 0, tiled=True)]
    all_to_all x1 -> x0, starting transfers between devices: 15 us -> none  [exchange_packed(): blocks = lax.all_to_all(packed.astype(dtype), AXES, 0, 0, tiled=True)]
    all_to_all x6 -> x9, waiting for transfers between devices: 90.9 us -> 95.8 us  [scatter_packed(): got = lax.all_to_all(blocks, axis, 0, 0, tiled=True)]
    pallas_call x3 -> x4, Pallas kernels: 31.8 us -> 36.3 us  [pair_exchange(): pl.pallas_call(pair_kernel, out_shape=jax.ShapeDtypeStruct(halves.shape[1...]
    reduce_sum x7 -> x9, other arithmetic: 12.7 us -> 13 us  [scatter_packed(): blocks = jnp.sum(got.astype(jnp.float32), axis=0).astype(dtype)]
  transfers between devices with their start and end apart: 14 -> 16, of which waited for: 8 -> 8; matrix products, arithmetic and copies ran while one was open for 27% -> 27% of each run, Pallas kernels for 3% -> 4%
where the time goes in v12:
time: 508 us; the launch traced here: 503 us
  waiting for transfers between devices  207 us (41%)
  other arithmetic  74.5 us (15%)
  matrix products  71.3 us (14%)
  local copies, waits for them, and re-layouts  53 us (10%)
  starting transfers between devices  46.3 us (9%)
  Pallas kernels  36.3 us (7%)
  between operations  14.9 us (3%)
    all_gather x1, waiting for transfers between devices, gather_packed(): full = lax.all_gather(packed, AXES, axis=0, tiled=True)  110 us
    all_to_all x9, waiting for transfers between devices, scatter_packed(): got = lax.all_to_all(blocks, axis, 0, 0, tiled=True)  95.8 us
    all_to_all x9, starting transfers between devices, scatter_packed(): got = lax.all_to_all(blocks, axis, 0, 0, tiled=True)  41.4 us
    pallas_call x4, Pallas kernels, pair_exchange(): pl.pallas_call(pair_kernel, out_shape=jax.ShapeDtypeStruct(halves.shape[1...  36.3 us
    convert_element_type x3, other arithmetic, pair_exchange(): (own.astype(jnp.float32) + received.astype(jnp.float32)).astype(dtype)  27.8 us
    concatenate x2, other arithmetic, scatter_packed(): packed = jnp.concatenate(pieces, axis=1).astype(dtype)  18.5 us
    reshape x1, local copies, waits for them, and re-layouts, per_device(): w_down = w_down_packed.reshape(n * down_rows, width)  17.6 us
    reduce_sum x9, other arithmetic, scatter_packed(): blocks = jnp.sum(got.astype(jnp.float32), axis=0).astype(dtype)  13 us
  transfers between devices with their start and end apart: 16, of which 8 were waited for; matrix products, arithmetic and copies ran while one was open for 27% of the time, Pallas kernels for 4%

profile of v12, /device:TPU:0, one launch (start us, length us, event | category | flops | bytes accessed | tf_op | source)
XLA Modules:
  0.0 503.1 jit_solution(15570021984658240210)
XLA Ops:
  19.3 110.3 %all-gather.2.cloned.1.call-done = bf16[1024,18176]{1,0:T(8,128)(2,1)} async-done(((bf16[8,18176]{1,0:T(8,128)(2,1)}), bf16[1024,18176]{1,0:T(8,128)(2,1)}) %all-gather.2.cloned.1.call-update) | async-done | bytes 37224464 | tf_op jit(solution)/shard_map/all_gather | solution.py:31
  138.2 7.8 %slice.148 = bf16[1024,4608]{1,0:T(8,128)(2,1)} slice(bf16[1024,18176]{1,0:T(8,128)(2,1)} %all-gather.2.cloned.1.call-done), slice={[0:1024], [13568:18176]} | slice | bytes 18874368 | tf_op jit(solution)/shard_map/slice | solution.py:34
  146.0 17.6 %reshape.165 = bf16[4608,1024]{1,0:T(8,128)(2,1)} reshape(bf16[1024,4608]{1,0:T(8,128)(2,1)} %slice.148) | data formatting | bytes 18874368 | tf_op jit(solution)/shard_map/reshape | solution.py:163
  163.6 8.2 %convolution_bitcast_fusion = f32[128,4608]{1,0:T(8,128)} fusion(bf16[4608,1024]{1,0:T(8,128)(2,1)} %reshape.165, bf16[128,1024]{1,0:T(8,128)(2,1)S(1)} %copy-done.5), kind=kOutput, calls=%fused_computation.16 | convolution fusion | flops 1207959552 | bytes 12058624 | tf_op jit(solution)/shard_map/dot_general | solution.py:203
  178.1 5.2 %fusion.5 = f32[128,4608]{1,0:T(8,128)S(1)} fusion(bf16[128,1024]{1,0:T(8,128)(2,1)S(1)} %multiply_convert_fusion.6, bf16[1024,18176]{1,0:T(8,128)(2,1)} %all-gather.2.cloned.1.call-done), kind=kOutput, calls=%fused_computation.10 | convolution fusion | flops 1207959552 | bytes 12058624 | tf_op jit(solution)/shard_map/dot_general | solution.py:195
  183.3 5.9 %multiply_convert_fusion.1 = (bf16[128,4608]{1,0:T(8,128)(2,1)S(1)}, bf16[128,4608]{1,0:T(8,128)(2,1)S(1)}, bf16[128,4608]{1,0:T(8,128)(2,1)S(1)}) fusion(f32[128,4608]{1,0:T(8,128)S(1)} %copy-done.4, f32[128,4608]{1,0:T(8,128)S(1)} %fusion.5, bf16[128,1024]{1,0:T(8,128)(2,1)} %copy-done.18, bf16[1024,18176]{1,0:T(8,128)(2,1)} %all-gather.2.cloned.1.call-done), kind=kOutput, calls=%fused_computation.22 | convolution fusion | flops 1216806912 | bytes 17956864 | tf_op jit(solution)/shard_map/dot_general | solution.py:194
  194.9 10.8 %pad_maximum_fusion = bf16[1024,9216]{1,0:T(8,128)(2,1)} fusion(bf16[1024,4608]{1,0:T(8,128)(2,1)S(1)} %fusion.50, bf16[1024,4608]{1,0:T(8,128)(2,1)S(1)} %fusion.49), kind=kLoop, calls=%fused_computation | loop fusion | flops 37748736 | bytes 37748736 | tf_op jit(solution)/shard_map/concatenate | solution.py:108
  205.7 16.0 %shard_map.188 = bf16[512,9216]{1,0:T(8,128)(2,1)} custom-call(bf16[2,512,9216]{2,1,0:T(8,128)(2,1)} %bitcast.74), custom_call_target="tpu_custom_call" | custom-call | tf_op jit(solution)/shard_map/pallas_call | solution.py:82
  221.7 12.1 %fusion = bf16[512,9216]{1,0:T(8,128)(2,1)} fusion(bf16[512,9216]{1,0:T(8,128)(2,1)} %shard_map.188, bf16[2,512,9216]{2,1,0:T(8,128)(2,1)} %bitcast.75, s32[]{:T(128)S(6)} %select_n.10), kind=kLoop, calls=%fused_computation.2 | loop fusion | flops 18874368 | bytes 28311556 | tf_op jit(solution)/shard_map/convert_element_type | solution.py:93
  235.7 7.2 %fusion.3 = f32[128,1024]{1,0:T(8,128)S(1)} fusion(bf16[128,4608]{1,0:T(8,128)(2,1)} %copy-done.13, bf16[1024,18176]{1,0:T(8,128)(2,1)} %all-gather.2.cloned.1.call-done), kind=kOutput, calls=%fused_computation.8 | convolution fusion | flops 1207959552 | bytes 11141120 | tf_op jit(solution)/shard_map/dot_general | solution.py:229
  242.9 6.3 %multiply_reduce_fusion.3 = (f32[1024]{0:T(1024)S(1)}, f32[128]{0:T(128)S(1)}, f32[128,1024]{1,0:T(8,128)S(1)}) fusion(f32[128,1024]{1,0:T(8,128)S(1)} %get-tuple-element.65, f32[128]{0:T(128)S(1)} %get-tuple-element.63, f32[1024]{0:T(1024)S(1)} %get-tuple-element.30, f32[128,1024]{1,0:T(8,128)S(1)} %fusion.3, bf16[128,4608]{1,0:T(8,128)(2,1)S(1)} %copy-done.12, ...), kind=kOutput, calls=%fused_computation.59 | convolution fusion | flops 1208875904 | bytes 12198912 | tf_op jit(solution)/shard_map/dot_general | solution.py:228
  258.1 6.1 %fusion.34 = (f32[1024]{0:T(1024)S(1)}, f32[128]{0:T(128)S(1)}, f32[128,1024]{1,0:T(8,128)}) fusion(bf16[128,1024]{1,0:T(8,128)(2,1)S(1)} %copy-done.7, f32[128]{0:T(128)S(1)} %get-tuple-element.61, f32[1024]{0:T(1024)S(1)} %get-tuple-element.31, bf16[1024,18176]{1,0:T(8,128)(2,1)} %all-gather.2.cloned.1.call-done, ...), kind=kOutput, calls=%fused_computation.48 | convolution fusion | flops 808582016 | bytes 7873536 | tf_op jit(solution)/shard_map/dot_general | solution.py:265
  266.5 4.5 shard_map.186
  273.2 7.3 %all-to-all-start = ((f32[4,128,256]{2,1,0:T(8,128)}), f32[4,128,256]{2,1,0:T(8,128)S(1)}, u32[]{:S(2)}, u32[]{:S(2)}) async-start(f32[4,128,256]{2,1,0:T(8,128)} %bitcast.13), calls=%async_computation | async-start | bytes 1048576 | tf_op jit(solution)/shard_map/all_to_all | solution.py:118
  283.4 4.5 fusion.35
  294.3 7.6 %pad_maximum_fusion.1 = bf16[1024,4096]{1,0:T(8,128)(2,1)} fusion(bf16[1024,1024]{1,0:T(8,128)(2,1)} %fusion.38, bf16[1024,3072]{1,0:T(8,128)(2,1)} %fusion.35), kind=kLoop, calls=%fused_computation.5 | loop fusion | flops 16777216 | bytes 16777216 | tf_op jit(solution)/shard_map/concatenate | solution.py:108
  301.9 7.5 %shard_map.187 = bf16[512,4096]{1,0:T(8,128)(2,1)} custom-call(bf16[2,512,4096]{2,1,0:T(8,128)(2,1)} %bitcast.76), custom_call_target="tpu_custom_call" | custom-call | tf_op jit(solution)/shard_map/pallas_call | solution.py:82
  310.1 5.6 %all-to-all-start.2 = ((f32[4,8,256]{2,1,0:T(8,128)}), f32[4,8,256]{2,1,0:T(8,128)S(1)}, u32[]{:S(2)}, u32[]{:S(2)}) async-start(f32[4,8,256]{2,1,0:T(8,128)} %bitcast.15), calls=%async_computation.2 | async-start | bytes 65536 | tf_op jit(solution)/shard_map/all_to_all | solution.py:118
  315.7 7.3 %fusion.2 = bf16[512,4096]{1,0:T(8,128)(2,1)} fusion(bf16[512,4096]{1,0:T(8,128)(2,1)} %shard_map.187, bf16[2,512,4096]{2,1,0:T(8,128)(2,1)} %bitcast.77, s32[]{:T(128)S(6)} %select_n.10), kind=kLoop, calls=%fused_computation.7 | loop fusion | flops 8388608 | bytes 12582916 | tf_op jit(solution)/shard_map/convert_element_type | solution.py:93
  323.0 5.1 %all-to-all-start.3 = ((bf16[4,128,4096]{2,1,0:T(8,128)(2,1)}), bf16[4,128,4096]{2,1,0:T(8,128)(2,1)}, u32[]{:S(2)}, u32[]{:S(2)}) async-start(bf16[4,128,4096]{2,1,0:T(8,128)(2,1)} %bitcast.79), calls=%async_computation.3 | async-start | bytes 8388608 | tf_op jit(solution)/shard_map/all_to_all | solution.py:118
  334.9 5.0 fusion.36.x_ref
  339.9 8.3 %shard_map.189 = bf16[2304,1024]{1,0:T(8,128)(2,1)} custom-call(bf16[2,2304,1024]{2,1,0:T(8,128)(2,1)} %fusion.36.x_ref), custom_call_target="tpu_custom_call" | custom-call | tf_op jit(solution)/shard_map/pallas_call | solution.py:82
  348.2 8.4 %fusion.1 = bf16[2304,1024]{1,0:T(8,128)(2,1)} fusion(bf16[2304,1024]{1,0:T(8,128)(2,1)} %shard_map.189, bf16[2,2304,1024]{2,1,0:T(8,128)(2,1)} %fusion.36.x_ref, s32[]{:T(128)S(6)} %select_n.10), kind=kLoop, calls=%fused_computation.4 | loop fusion | flops 9437184 | bytes 14155780 | tf_op jit(solution)/shard_map/convert_element_type | solution.py:93
  356.6 20.7 %all-to-all-done.3 = bf16[4,128,4096]{2,1,0:T(8,128)(2,1)} async-done(((bf16[4,128,4096]{2,1,0:T(8,128)(2,1)}), bf16[4,128,4096]{2,1,0:T(8,128)(2,1)}, u32[]{:S(2)}, u32[]{:S(2)}) %all-to-all-start.3) | async-done | bytes 4194336 | tf_op jit(solution)/shard_map/all_to_all | solution.py:118
  377.3 5.0 all-to-all-start.6
  386.6 49.6 %all-to-all-done.6 = bf16[4,576,1024]{2,1,0:T(8,128)(2,1)} async-done(((bf16[4,576,1024]{2,1,0:T(8,128)(2,1)}), bf16[4,576,1024]{2,1,0:T(8,128)(2,1)}, u32[]{:S(2)}, u32[]{:S(2)}) %all-to-all-start.6) | async-done | bytes 4718624 | tf_op jit(solution)/shard_map/all_to_all | solution.py:118
  436.2 4.7 all-to-all-start.4
  440.9 4.8 reduce_sum.195
  445.8 8.5 %all-to-all-done.4 = bf16[4,32,4096]{2,1,0:T(8,128)(2,1)S(1)} async-done(((bf16[4,32,4096]{2,1,0:T(8,128)(2,1)}), bf16[4,32,4096]{2,1,0:T(8,128)(2,1)S(1)}, u32[]{:S(2)}, u32[]{:S(2)}) %all-to-all-start.4) | async-done | bytes 1048608 | tf_op jit(solution)/shard_map/all_to_all | solution.py:118
  459.3 5.8 %fusion.26 = bf16[128,1024]{1,0:T(8,128)(2,1)} fusion(f32[128,1024]{1,0:T(8,128)S(1)} %copy-done.2, bf16[128,4608]{1,0:T(8,128)(2,1)S(1)} %get-tuple-element.49, bf16[4608,1024]{1,0:T(8,128)(2,1)} %reshape.165), kind=kOutput, calls=%fused_computation.33 | convolution fusion | flops 1208221696 | bytes 11403264 | tf_op jit(solution)/shard_map/dot_general | solution.py:199
  467.3 5.9 %all-to-all-done.7 = bf16[4,144,1024]{2,1,0:T(8,128)(2,1)S(1)} async-done(((bf16[4,144,1024]{2,1,0:T(8,128)(2,1)}), bf16[4,144,1024]{2,1,0:T(8,128)(2,1)S(1)}, u32[]{:S(2)}, u32[]{:S(2)}) %all-to-all-start.7) | async-done | bytes 1179680 | tf_op jit(solution)/shard_map/all_to_all | solution.py:118
  477.6 5.6 %all-to-all-done.5 = bf16[4,8,4096]{2,1,0:T(8,128)(2,1)S(1)} async-done(((bf16[4,8,4096]{2,1,0:T(8,128)(2,1)}), bf16[4,8,4096]{2,1,0:T(8,128)(2,1)S(1)}, u32[]{:S(2)}, u32[]{:S(2)}) %all-to-all-start.5) | async-done | bytes 262176 | tf_op jit(solution)/shard_map/all_to_all | solution.py:118
  (152 shorter events, 92.8 us)
Async XLA Ops:
  7.2 122.4 %all-gather.2.cloned.1.call-start = ((), (), s32[]{:S(2)}) async-start(), calls=%async_computation.12 | async-start | bytes 37515264 | tf_op jit(solution)/shard_map/all_gather | solution.py:31
  14.6 333.6 %reduce-scatter.4.cloned.1.call-start = ((), (), s32[]{:S(2)}) async-start(), calls=%async_computation.13 | async-start | bytes 11796480 | tf_op jit(solution)/shard_map/reduce_scatter | solution.py:122
  15.4 2.4 collective-permute-start.1
  135.9 37.9 %copy-start = (f32[128,3072]{1,0:T(8,128)}, f32[128,3072]{1,0:T(8,128)S(1)}, u32[]{:S(2)}) copy-start(f32[128,3072]{1,0:T(8,128)S(1)} %fusion.13) | copy-start | bytes 4718596
  136.0 37.7 %collective-permute-start = (bf16[2,1024]{1,0:T(2,128)(2,1)S(1)}, bf16[2,1024]{1,0:T(2,128)(2,1)S(1)}, u32[]{:S(2)}, u32[]{:S(2)}) collective-permute-start(bf16[2,1024]{1,0:T(2,128)(2,1)S(1)} %slice.138), channel_id=1, source_target_pairs={{0,1},{1,2},{2,3},{3,4},{4,5},{5,6},{6,7},{7,8},{8,9},{9,10},{10,1... | collective-permute-start | bytes 12296 | tf_op jit(solution)/shard_map/ppermute | solution.py:16
  146.0 17.6 %copy-start.5 = (bf16[128,1024]{1,0:T(8,128)(2,1)S(1)}, bf16[128,1024]{1,0:T(8,128)(2,1)}, u32[]{:S(2)}) copy-start(bf16[128,1024]{1,0:T(8,128)(2,1)} %param.21) | copy-start | bytes 786436
  177.2 72.0 %copy-start.1 = (f32[128,1024]{1,0:T(8,128)}, f32[128,1024]{1,0:T(8,128)S(1)}, u32[]{:S(2)}) copy-start(f32[128,1024]{1,0:T(8,128)S(1)} %get-tuple-element.65) | copy-start | bytes 1572868
  178.0 5.2 %copy-start.4 = (f32[128,4608]{1,0:T(8,128)S(1)}, f32[128,4608]{1,0:T(8,128)}, u32[]{:S(2)}) copy-start(f32[128,4608]{1,0:T(8,128)} %convolution_bitcast_fusion) | copy-start | bytes 7077892
  235.6 7.2 %copy-start.12 = (bf16[128,4608]{1,0:T(8,128)(2,1)S(1)}, bf16[128,4608]{1,0:T(8,128)(2,1)}, u32[]{:S(2)}) copy-start(bf16[128,4608]{1,0:T(8,128)(2,1)} %copy-done.11) | copy-start | bytes 3538948
  253.2 11.0 %copy-start.14 = (bf16[128,1024]{1,0:T(8,128)(2,1)}, bf16[128,1024]{1,0:T(8,128)(2,1)S(1)}, u32[]{:S(2)}) copy-start(bf16[128,1024]{1,0:T(8,128)(2,1)S(1)} %get-tuple-element.52) | copy-start | bytes 786436
  253.4 3.3 collective-permute-start.2
  258.1 6.1 %copy-start.19 = (bf16[128,1024]{1,0:T(8,128)(2,1)}, bf16[128,1024]{1,0:T(8,128)(2,1)S(1)}, u32[]{:S(2)}) copy-start(bf16[128,1024]{1,0:T(8,128)(2,1)S(1)} %get-tuple-element.50) | copy-start | bytes 786436
  258.1 6.1 %copy-start.21 = (bf16[128,1024]{1,0:T(8,128)(2,1)}, bf16[128,1024]{1,0:T(8,128)(2,1)S(1)}, u32[]{:S(2)}) copy-start(bf16[128,1024]{1,0:T(8,128)(2,1)S(1)} %get-tuple-element.51) | copy-start | bytes 786436
  264.9 18.5 %copy-start.10 = (bf16[128,2,4,4,4,8]{0,5,4,3,2,1:T(8,128)(2,1)S(1)}, bf16[128,2,4,4,4,8]{0,5,4,3,2,1:T(8,128)(2,1)}, u32[]{:S(2)}) copy-start(bf16[128,2,4,4,4,8]{0,5,4,3,2,1:T(8,128)(2,1)} %copy.77) | copy-start | bytes 786436
  264.9 18.5 %copy-start.15 = (bf16[128,1024]{1,0:T(8,128)(2,1)S(1)}, bf16[128,1024]{1,0:T(8,128)(2,1)}, u32[]{:S(2)}) copy-start(bf16[128,1024]{1,0:T(8,128)(2,1)} %copy-done.14) | copy-start | bytes 786436
  264.9 18.5 %copy-start.20 = (bf16[128,1024]{1,0:T(8,128)(2,1)S(1)}, bf16[128,1024]{1,0:T(8,128)(2,1)}, u32[]{:S(2)}) copy-start(bf16[128,1024]{1,0:T(8,128)(2,1)} %copy-done.19) | copy-start | bytes 786436
  265.2 18.2 %copy-start.22 = (bf16[128,1024]{1,0:T(8,128)(2,1)S(1)}, bf16[128,1024]{1,0:T(8,128)(2,1)}, u32[]{:S(2)}) copy-start(bf16[128,1024]{1,0:T(8,128)(2,1)} %copy-done.21) | copy-start | bytes 786436
  273.2 17.1 %all-to-all-start = ((f32[4,128,256]{2,1,0:T(8,128)}), f32[4,128,256]{2,1,0:T(8,128)S(1)}, u32[]{:S(2)}, u32[]{:S(2)}) async-start(f32[4,128,256]{2,1,0:T(8,128)} %bitcast.13), calls=%async_computation | async-start | bytes 1048576 | tf_op jit(solution)/shard_map/all_to_all | solution.py:118
  290.9 18.5 %all-to-all-start.1 = ((f32[4,32,256]{2,1,0:T(8,128)}), f32[4,32,256]{2,1,0:T(8,128)S(1)}, u32[]{:S(2)}, u32[]{:S(2)}) async-start(f32[4,32,256]{2,1,0:T(8,128)} %bitcast.14), calls=%async_computation.1 | async-start | bytes 262144 | tf_op jit(solution)/shard_map/all_to_all | solution.py:118
  310.1 12.9 %all-to-all-start.2 = ((f32[4,8,256]{2,1,0:T(8,128)}), f32[4,8,256]{2,1,0:T(8,128)S(1)}, u32[]{:S(2)}, u32[]{:S(2)}) async-start(f32[4,8,256]{2,1,0:T(8,128)} %bitcast.15), calls=%async_computation.2 | async-start | bytes 65536 | tf_op jit(solution)/shard_map/all_to_all | solution.py:118
  323.0 54.3 %all-to-all-start.3 = ((bf16[4,128,4096]{2,1,0:T(8,128)(2,1)}), bf16[4,128,4096]{2,1,0:T(8,128)(2,1)}, u32[]{:S(2)}, u32[]{:S(2)}) async-start(bf16[4,128,4096]{2,1,0:T(8,128)(2,1)} %bitcast.79), calls=%async_computation.3 | async-start | bytes 8388608 | tf_op jit(solution)/shard_map/all_to_all | solution.py:118
  328.1 130.6 %reduce-scatter.6.cloned.1.call-start = ((), (), s32[]{:S(2)}) async-start(), calls=%async_computation.14 | async-start | bytes 2949120 | tf_op jit(solution)/shard_map/reduce_scatter | solution.py:122
  328.2 6.7 %copy-start.6 = (bf16[128,1024]{1,0:T(8,128)(2,1)S(1)}, bf16[128,1024]{1,0:T(8,128)(2,1)}, u32[]{:S(2)}) copy-start(bf16[128,1024]{1,0:T(8,128)(2,1)} %param.21) | copy-start | bytes 786436
  377.3 58.9 %all-to-all-start.6 = ((bf16[4,576,1024]{2,1,0:T(8,128)(2,1)}), bf16[4,576,1024]{2,1,0:T(8,128)(2,1)}, u32[]{:S(2)}, u32[]{:S(2)}) async-start(bf16[4,576,1024]{2,1,0:T(8,128)(2,1)} %bitcast.78), calls=%async_computation.9 | async-start | bytes 9437184 | tf_op jit(solution)/shard_map/all_to_all | solution.py:118
  436.2 18.1 %all-to-all-start.4 = ((bf16[4,32,4096]{2,1,0:T(8,128)(2,1)}), bf16[4,32,4096]{2,1,0:T(8,128)(2,1)S(1)}, u32[]{:S(2)}, u32[]{:S(2)}) async-start(bf16[4,32,4096]{2,1,0:T(8,128)(2,1)} %bitcast.85), calls=%async_computation.4 | async-start | bytes 2097152 | tf_op jit(solution)/shard_map/all_to_all | solution.py:118
  440.9 18.4 %copy-start.2 = (f32[128,1024]{1,0:T(8,128)S(1)}, f32[128,1024]{1,0:T(8,128)}, u32[]{:S(2)}) copy-start(f32[128,1024]{1,0:T(8,128)} %copy-done.1) | copy-start | bytes 1572868
  455.2 18.0 %all-to-all-start.7 = ((bf16[4,144,1024]{2,1,0:T(8,128)(2,1)}), bf16[4,144,1024]{2,1,0:T(8,128)(2,1)S(1)}, u32[]{:S(2)}, u32[]{:S(2)}) async-start(bf16[4,144,1024]{2,1,0:T(8,128)(2,1)} %bitcast.83), calls=%async_computation.10 | async-start | bytes 2359296 | tf_op jit(solution)/shard_map/all_to_all | solution.py:118
  458.7 35.7 %reduce-scatter.8.cloned.1.call-start = ((), (), s32[]{:S(2)}) async-start(), calls=%async_computation.15 | async-start | bytes 737280 | tf_op jit(solution)/shard_map/reduce_scatter | solution.py:122
  465.1 21.6 %copy-start.8 = (bf16[128,1024]{1,0:T(8,128)(2,1)S(1)}, bf16[128,1024]{1,0:T(8,128)(2,1)}, u32[]{:S(2)}) copy-start(bf16[128,1024]{1,0:T(8,128)(2,1)} %param.11) | copy-start | bytes 786436
  465.1 21.6 %copy-start.24 = (f32[128,1024]{1,0:T(8,128)S(1)}, f32[128,1024]{1,0:T(8,128)}, u32[]{:S(2)}) copy-start(f32[128,1024]{1,0:T(8,128)} %get-tuple-element.67) | copy-start | bytes 1572868
  473.2 10.1 %all-to-all-start.5 = ((bf16[4,8,4096]{2,1,0:T(8,128)(2,1)}), bf16[4,8,4096]{2,1,0:T(8,128)(2,1)S(1)}, u32[]{:S(2)}, u32[]{:S(2)}) async-start(bf16[4,8,4096]{2,1,0:T(8,128)(2,1)} %bitcast.26), calls=%async_computation.5 | async-start | bytes 524288 | tf_op jit(solution)/shard_map/all_to_all | solution.py:118
  483.2 10.5 %all-to-all-start.8 = ((bf16[4,36,1024]{2,1,0:T(8,128)(2,1)}), bf16[4,36,1024]{2,1,0:T(8,128)(2,1)S(1)}, u32[]{:S(2)}, u32[]{:S(2)}) async-start(bf16[4,36,1024]{2,1,0:T(8,128)(2,1)} %all_to_all.70), calls=%async_computation.11 | async-start | bytes 655360 | tf_op jit(solution)/shard_map/all_to_all | solution.py:118
  (10 other events, 21.0 us)
Sparse Core Ops, SparseCore 0:
  14.7 114.7 all-gather.1
  233.9 90.6 reduce-scatter.3
  348.3 34.5 reduce-scatter.5
  461.6 20.2 reduce-scatter.7

commit v13 on v11

--- a/solution.py
+++ b/solution.py
@@ -39,7 +39,7 @@
 AXES = ("y", "z", "x", "core")
 FSDP = AXES
 ORDER_UP = ("core", "x", "z", "y")
-ORDER_DOWN = ("core", "z", "y", "x")
+ORDER_DOWN = ("core", "y", "z", "x")
 ORDER_IN = ("core", "y", "x", "z")
 
 

time: 495 us -> 494 us (level)
  no operation moved by 1% of the time
where the time goes in v13:
time: 494 us; the launch traced here: 490 us
  waiting for transfers between devices  203 us (41%)
  matrix products  71.3 us (14%)
  other arithmetic  71.2 us (14%)
  local copies, waits for them, and re-layouts  52.3 us (11%)
  starting transfers between devices  45.1 us (9%)
  Pallas kernels  31.8 us (6%)
  between operations  14.9 us (3%)
    all_gather x1, waiting for transfers between devices, gather_packed(): full = lax.all_gather(packed, AXES, axis=0, tiled=True)  110 us
    all_to_all x6, waiting for transfers between devices, scatter_packed(): got = lax.all_to_all(blocks, axis, 0, 0, tiled=True)  89.8 us
    pallas_call x3, Pallas kernels, pair_exchange(): pl.pallas_call(pair_kernel, out_shape=jax.ShapeDtypeStruct(halves.shape[1...  31.8 us
    convert_element_type x3, other arithmetic, pair_exchange(): (own.astype(jnp.float32) + received.astype(jnp.float32)).astype(jnp.bfloa...  27.8 us
    all_to_all x6, starting transfers between devices, scatter_packed(): got = lax.all_to_all(blocks, axis, 0, 0, tiled=True)  25.3 us
    concatenate x2, other arithmetic, scatter_packed(): packed = jnp.concatenate(pieces, axis=1).astype(jnp.bfloat16)  18.8 us
    reshape x1, local copies, waits for them, and re-layouts, per_device(): w_down = w_down_packed.reshape(n * down_rows, width)  17.6 us
    all_to_all x1, starting transfers between devices, exchange_packed(): blocks = lax.all_to_all(packed.astype(dtype), AXES, 0, 0, tiled=True)  15 us
  transfers between devices with their start and end apart: 14, of which 8 were waited for; matrix products, arithmetic and copies ran while one was open for 27% of the time, Pallas kernels for 3%

profile of v13, /device:TPU:0, one launch (start us, length us, event | category | flops | bytes accessed | tf_op | source)
XLA Modules:
  0.0 489.6 jit_solution(12371232451417102223)
XLA Ops:
  19.3 110.3 %all-gather.2.cloned.1.call-done = bf16[1024,18176]{1,0:T(8,128)(2,1)} async-done(((bf16[8,18176]{1,0:T(8,128)(2,1)}), bf16[1024,18176]{1,0:T(8,128)(2,1)}) %all-gather.2.cloned.1.call-update) | async-done | bytes 37224464 | tf_op jit(solution)/shard_map/all_gather | solution.py:31
  138.2 7.8 %slice.148 = bf16[1024,4608]{1,0:T(8,128)(2,1)} slice(bf16[1024,18176]{1,0:T(8,128)(2,1)} %all-gather.2.cloned.1.call-done), slice={[0:1024], [13568:18176]} | slice | bytes 18874368 | tf_op jit(solution)/shard_map/slice | solution.py:34
  146.0 17.6 %reshape.148 = bf16[4608,1024]{1,0:T(8,128)(2,1)} reshape(bf16[1024,4608]{1,0:T(8,128)(2,1)} %slice.148) | data formatting | bytes 18874368 | tf_op jit(solution)/shard_map/reshape | solution.py:161
  163.6 8.2 %convolution_bitcast_fusion = f32[128,4608]{1,0:T(8,128)} fusion(bf16[4608,1024]{1,0:T(8,128)(2,1)} %reshape.148, bf16[128,1024]{1,0:T(8,128)(2,1)S(1)} %copy-done.8), kind=kOutput, calls=%fused_computation.16 | convolution fusion | flops 1207959552 | bytes 12058624 | tf_op jit(solution)/shard_map/dot_general | solution.py:201
  178.1 5.2 %fusion.5 = f32[128,4608]{1,0:T(8,128)S(1)} fusion(bf16[128,1024]{1,0:T(8,128)(2,1)S(1)} %multiply_convert_fusion.6, bf16[1024,18176]{1,0:T(8,128)(2,1)} %all-gather.2.cloned.1.call-done), kind=kOutput, calls=%fused_computation.10 | convolution fusion | flops 1207959552 | bytes 12058624 | tf_op jit(solution)/shard_map/dot_general | solution.py:193
  183.3 5.9 %multiply_convert_fusion.1 = (bf16[128,4608]{1,0:T(8,128)(2,1)S(1)}, bf16[128,4608]{1,0:T(8,128)(2,1)S(1)}, bf16[128,4608]{1,0:T(8,128)(2,1)S(1)}) fusion(f32[128,4608]{1,0:T(8,128)S(1)} %copy-done.7, f32[128,4608]{1,0:T(8,128)S(1)} %fusion.5, bf16[128,1024]{1,0:T(8,128)(2,1)} %copy-done.20, bf16[1024,18176]{1,0:T(8,128)(2,1)} %all-gather.2.cloned.1.call-done), kind=kOutput, calls=%fused_computation.22 | convolution fusion | flops 1216806912 | bytes 17956864 | tf_op jit(solution)/shard_map/dot_general | solution.py:192
  194.9 10.8 %pad_maximum_fusion = bf16[1024,9216]{1,0:T(8,128)(2,1)} fusion(bf16[1024,4608]{1,0:T(8,128)(2,1)S(1)} %fusion.50, bf16[1024,4608]{1,0:T(8,128)(2,1)S(1)} %fusion.49), kind=kLoop, calls=%fused_computation | loop fusion | flops 37748736 | bytes 37748736 | tf_op jit(solution)/shard_map/concatenate | solution.py:106
  205.7 16.0 %shard_map.187 = bf16[512,9216]{1,0:T(8,128)(2,1)} custom-call(bf16[2,512,9216]{2,1,0:T(8,128)(2,1)} %bitcast.67), custom_call_target="tpu_custom_call" | custom-call | tf_op jit(solution)/shard_map/pallas_call | solution.py:82
  221.7 12.1 %fusion = bf16[512,9216]{1,0:T(8,128)(2,1)} fusion(bf16[512,9216]{1,0:T(8,128)(2,1)} %shard_map.187, bf16[2,512,9216]{2,1,0:T(8,128)(2,1)} %bitcast.68, s32[]{:T(128)S(6)} %select_n.8), kind=kLoop, calls=%fused_computation.2 | loop fusion | flops 18874368 | bytes 28311556 | tf_op jit(solution)/shard_map/convert_element_type | solution.py:93
  237.4 7.2 %fusion.3 = f32[128,1024]{1,0:T(8,128)S(1)} fusion(bf16[128,4608]{1,0:T(8,128)(2,1)} %copy-done.15, bf16[1024,18176]{1,0:T(8,128)(2,1)} %all-gather.2.cloned.1.call-done), kind=kOutput, calls=%fused_computation.8 | convolution fusion | flops 1207959552 | bytes 11141120 | tf_op jit(solution)/shard_map/dot_general | solution.py:227
  244.7 5.9 %multiply_reduce_fusion.3 = (f32[1024]{0:T(1024)S(1)}, f32[128]{0:T(128)S(1)}, f32[128,1024]{1,0:T(8,128)S(1)}) fusion(f32[128,1024]{1,0:T(8,128)S(1)} %get-tuple-element.75, f32[128]{0:T(128)S(1)} %get-tuple-element.73, f32[1024]{0:T(1024)S(1)} %get-tuple-element.40, f32[128,1024]{1,0:T(8,128)S(1)} %fusion.3, bf16[128,4608]{1,0:T(8,128)(2,1)S(1)} %copy-done.14, ...), kind=kOutput, calls=%fused_computation.59 | convolution fusion | flops 1208875904 | bytes 12198912 | tf_op jit(solution)/shard_map/dot_general | solution.py:226
  257.6 6.1 %fusion.34 = (f32[1024]{0:T(1024)S(1)}, f32[128]{0:T(128)S(1)}, f32[128,1024]{1,0:T(8,128)}) fusion(bf16[128,1024]{1,0:T(8,128)(2,1)S(1)} %copy-done.10, f32[128]{0:T(128)S(1)} %get-tuple-element.71, f32[1024]{0:T(1024)S(1)} %get-tuple-element.41, bf16[1024,18176]{1,0:T(8,128)(2,1)} %all-gather.2.cloned.1.call-done, ...), kind=kOutput, calls=%fused_computation.49 | convolution fusion | flops 808582016 | bytes 7873536 | tf_op jit(solution)/shard_map/dot_general | solution.py:263
  265.0 15.0 %all-to-all-start = ((f32[128,8,256]{2,1,0:T(8,128)}), f32[128,8,256]{2,1,0:T(8,128)S(1)}, u32[]{:S(2)}, u32[]{:S(2)}) async-start(f32[128,8,256]{2,1,0:T(8,128)} %pad_bitcast_fusion), calls=%async_computation | async-start | bytes 2097152 | tf_op jit(solution)/shard_map/all_to_all | solution.py:50
  280.0 5.7 %fusion.35 = bf16[1024,3072]{1,0:T(8,128)(2,1)} fusion(bf16[128,1024]{0,1:T(8,128)(2,1)} %bitcast.79, bf16[128,1024]{1,0:T(8,128)(2,1)} %copy-done.22, bf16[128,1024]{1,0:T(8,128)(2,1)} %copy-done.16, bf16[128,1024]{1,0:T(8,128)(2,1)} %copy-done.21), kind=kOutput, calls=%fused_computation.73 | convolution fusion | flops 807665664 | bytes 7340032 | tf_op jit(solution)/shard_map/dot_general | solution.py:257
  285.7 8.0 %pad_maximum_fusion.1 = bf16[1024,4096]{1,0:T(8,128)(2,1)} fusion(bf16[1024,1024]{1,0:T(8,128)(2,1)} %fusion.38, bf16[1024,3072]{1,0:T(8,128)(2,1)} %fusion.35), kind=kLoop, calls=%fused_computation.5 | loop fusion | flops 16777216 | bytes 16777216 | tf_op jit(solution)/shard_map/concatenate | solution.py:106
  293.6 7.5 %shard_map.186 = bf16[512,4096]{1,0:T(8,128)(2,1)} custom-call(bf16[2,512,4096]{2,1,0:T(8,128)(2,1)} %bitcast.69), custom_call_target="tpu_custom_call" | custom-call | tf_op jit(solution)/shard_map/pallas_call | solution.py:82
  301.2 7.3 %fusion.2 = bf16[512,4096]{1,0:T(8,128)(2,1)} fusion(bf16[512,4096]{1,0:T(8,128)(2,1)} %shard_map.186, bf16[2,512,4096]{2,1,0:T(8,128)(2,1)} %bitcast.70, s32[]{:T(128)S(6)} %select_n.8), kind=kLoop, calls=%fused_computation.7 | loop fusion | flops 8388608 | bytes 12582916 | tf_op jit(solution)/shard_map/convert_element_type | solution.py:93
  310.8 4.8 all-to-all-start.1
  322.7 5.0 %fusion.36.x_ref = bf16[2,2304,1024]{2,1,0:T(8,128)(2,1)} fusion(bf16[2,2304,128]{2,1,0:T(8,128)(2,1)S(1)} %bitcast.75, bf16[128,1024]{1,0:T(8,128)(2,1)S(1)} %copy-done.9), kind=kOutput, calls=%fused_computation.76 | convolution fusion | flops 1207959552 | bytes 10878976 | tf_op jit(solution)/shard_map/dot_general | solution.py:207
  327.7 8.3 %shard_map.188 = bf16[2304,1024]{1,0:T(8,128)(2,1)} custom-call(bf16[2,2304,1024]{2,1,0:T(8,128)(2,1)} %fusion.36.x_ref), custom_call_target="tpu_custom_call" | custom-call | tf_op jit(solution)/shard_map/pallas_call | solution.py:82
  336.0 8.4 %fusion.1 = bf16[2304,1024]{1,0:T(8,128)(2,1)} fusion(bf16[2304,1024]{1,0:T(8,128)(2,1)} %shard_map.188, bf16[2,2304,1024]{2,1,0:T(8,128)(2,1)} %fusion.36.x_ref, s32[]{:T(128)S(6)} %select_n.8), kind=kLoop, calls=%fused_computation.4 | loop fusion | flops 9437184 | bytes 14155780 | tf_op jit(solution)/shard_map/convert_element_type | solution.py:93
  344.4 20.0 %all-to-all-done.1 = bf16[4,128,4096]{2,1,0:T(8,128)(2,1)} async-done(((bf16[4,128,4096]{2,1,0:T(8,128)(2,1)}), bf16[4,128,4096]{2,1,0:T(8,128)(2,1)}, u32[]{:S(2)}, u32[]{:S(2)}) %all-to-all-start.1) | async-done | bytes 4194336 | tf_op jit(solution)/shard_map/all_to_all | solution.py:116
  364.4 4.9 %all-to-all-start.4 = ((bf16[4,576,1024]{2,1,0:T(8,128)(2,1)}), bf16[4,576,1024]{2,1,0:T(8,128)(2,1)}, u32[]{:S(2)}, u32[]{:S(2)}) async-start(bf16[4,576,1024]{2,1,0:T(8,128)(2,1)} %bitcast.71), calls=%async_computation.7 | async-start | bytes 9437184 | tf_op jit(solution)/shard_map/all_to_all | solution.py:116
  369.3 4.2 reduce_sum.172
  373.6 49.3 %all-to-all-done.4 = bf16[4,576,1024]{2,1,0:T(8,128)(2,1)} async-done(((bf16[4,576,1024]{2,1,0:T(8,128)(2,1)}), bf16[4,576,1024]{2,1,0:T(8,128)(2,1)}, u32[]{:S(2)}, u32[]{:S(2)}) %all-to-all-start.4) | async-done | bytes 4718624 | tf_op jit(solution)/shard_map/all_to_all | solution.py:116
  426.4 4.8 reduce_sum.175
  431.2 8.3 %all-to-all-done.2 = bf16[4,32,4096]{2,1,0:T(8,128)(2,1)S(1)} async-done(((bf16[4,32,4096]{2,1,0:T(8,128)(2,1)}), bf16[4,32,4096]{2,1,0:T(8,128)(2,1)S(1)}, u32[]{:S(2)}, u32[]{:S(2)}) %all-to-all-start.2) | async-done | bytes 1048608 | tf_op jit(solution)/shard_map/all_to_all | solution.py:116
  440.5 4.5 all-to-all-start.5
  445.6 5.8 %fusion.26 = bf16[128,1024]{1,0:T(8,128)(2,1)} fusion(f32[128,1024]{1,0:T(8,128)S(1)} %copy-done.3, bf16[128,4608]{1,0:T(8,128)(2,1)S(1)} %get-tuple-element.59, bf16[4608,1024]{1,0:T(8,128)(2,1)} %reshape.148), kind=kOutput, calls=%fused_computation.33 | convolution fusion | flops 1208221696 | bytes 11403264 | tf_op jit(solution)/shard_map/dot_general | solution.py:197
  453.6 5.4 %all-to-all-done.5 = bf16[4,144,1024]{2,1,0:T(8,128)(2,1)S(1)} async-done(((bf16[4,144,1024]{2,1,0:T(8,128)(2,1)}), bf16[4,144,1024]{2,1,0:T(8,128)(2,1)S(1)}, u32[]{:S(2)}, u32[]{:S(2)}) %all-to-all-start.5) | async-done | bytes 1179680 | tf_op jit(solution)/shard_map/all_to_all | solution.py:116
  459.0 4.0 all-to-all-start.3
  464.1 5.7 %all-to-all-done.3 = bf16[4,8,4096]{2,1,0:T(8,128)(2,1)} async-done(((bf16[4,8,4096]{2,1,0:T(8,128)(2,1)}), bf16[4,8,4096]{2,1,0:T(8,128)(2,1)}, u32[]{:S(2)}, u32[]{:S(2)}) %all-to-all-start.3) | async-done | bytes 262176 | tf_op jit(solution)/shard_map/all_to_all | solution.py:116
  (139 shorter events, 74.7 us)
Async XLA Ops:
  7.2 122.4 %all-gather.2.cloned.1.call-start = ((), (), s32[]{:S(2)}) async-start(), calls=%async_computation.10 | async-start | bytes 37515264 | tf_op jit(solution)/shard_map/all_gather | solution.py:31
  14.6 321.4 %reduce-scatter.4.cloned.1.call-start = ((), (), s32[]{:S(2)}) async-start(), calls=%async_computation.11 | async-start | bytes 11796480 | tf_op jit(solution)/shard_map/reduce_scatter | solution.py:120
  15.4 2.4 collective-permute-start.1
  132.0 4.0 copy-start.17
  135.9 37.9 %copy-start = (f32[128,3072]{1,0:T(8,128)}, f32[128,3072]{1,0:T(8,128)S(1)}, u32[]{:S(2)}) copy-start(f32[128,3072]{1,0:T(8,128)S(1)} %fusion.13) | copy-start | bytes 4718596
  136.0 37.7 %collective-permute-start = (bf16[2,1024]{1,0:T(2,128)(2,1)S(1)}, bf16[2,1024]{1,0:T(2,128)(2,1)S(1)}, u32[]{:S(2)}, u32[]{:S(2)}) collective-permute-start(bf16[2,1024]{1,0:T(2,128)(2,1)S(1)} %slice.138), channel_id=1, source_target_pairs={{0,1},{1,2},{2,3},{3,4},{4,5},{5,6},{6,7},{7,8},{8,9},{9,10},{10,1... | collective-permute-start | bytes 12296 | tf_op jit(solution)/shard_map/ppermute | solution.py:16
  146.0 17.6 %copy-start.8 = (bf16[128,1024]{1,0:T(8,128)(2,1)S(1)}, bf16[128,1024]{1,0:T(8,128)(2,1)}, u32[]{:S(2)}) copy-start(bf16[128,1024]{1,0:T(8,128)(2,1)} %param.21) | copy-start | bytes 786436
  171.8 3.1 copy-start.10
  177.2 73.4 %copy-start.2 = (f32[128,1024]{1,0:T(8,128)}, f32[128,1024]{1,0:T(8,128)S(1)}, u32[]{:S(2)}) copy-start(f32[128,1024]{1,0:T(8,128)S(1)} %get-tuple-element.75) | copy-start | bytes 1572868
  178.0 5.2 %copy-start.7 = (f32[128,4608]{1,0:T(8,128)S(1)}, f32[128,4608]{1,0:T(8,128)}, u32[]{:S(2)}) copy-start(f32[128,4608]{1,0:T(8,128)} %convolution_bitcast_fusion) | copy-start | bytes 7077892
  237.4 7.2 %copy-start.14 = (bf16[128,4608]{1,0:T(8,128)(2,1)S(1)}, bf16[128,4608]{1,0:T(8,128)(2,1)}, u32[]{:S(2)}) copy-start(bf16[128,4608]{1,0:T(8,128)(2,1)} %copy-done.13) | copy-start | bytes 3538948
  250.6 2.9 copy-start.1
  250.6 2.9 copy-start.12
  250.8 4.4 copy-start.19
  253.7 3.9 copy-start.16
  253.9 3.5 collective-permute-start.2
  257.6 6.1 %copy-start.21 = (bf16[128,1024]{1,0:T(8,128)(2,1)}, bf16[128,1024]{1,0:T(8,128)(2,1)S(1)}, u32[]{:S(2)}) copy-start(bf16[128,1024]{1,0:T(8,128)(2,1)S(1)} %get-tuple-element.60) | copy-start | bytes 786436
  257.6 6.1 %copy-start.22 = (bf16[128,1024]{1,0:T(8,128)(2,1)}, bf16[128,1024]{1,0:T(8,128)(2,1)S(1)}, u32[]{:S(2)}) copy-start(bf16[128,1024]{1,0:T(8,128)(2,1)S(1)} %get-tuple-element.61) | copy-start | bytes 786436
  265.0 45.8 %all-to-all-start = ((f32[128,8,256]{2,1,0:T(8,128)}), f32[128,8,256]{2,1,0:T(8,128)S(1)}, u32[]{:S(2)}, u32[]{:S(2)}) async-start(f32[128,8,256]{2,1,0:T(8,128)} %pad_bitcast_fusion), calls=%async_computation | async-start | bytes 2097152 | tf_op jit(solution)/shard_map/all_to_all | solution.py:50
  310.8 4.9 %copy-start.4 = (f32[128,8,256]{2,1,0:T(8,128)}, f32[128,8,256]{2,1,0:T(8,128)S(1)}, u32[]{:S(2)}) copy-start(f32[128,8,256]{2,1,0:T(8,128)S(1)} %all-to-all-done) | copy-start | bytes 3145732
  310.8 53.6 %all-to-all-start.1 = ((bf16[4,128,4096]{2,1,0:T(8,128)(2,1)}), bf16[4,128,4096]{2,1,0:T(8,128)(2,1)}, u32[]{:S(2)}, u32[]{:S(2)}) async-start(bf16[4,128,4096]{2,1,0:T(8,128)(2,1)} %bitcast.72), calls=%async_computation.1 | async-start | bytes 8388608 | tf_op jit(solution)/shard_map/all_to_all | solution.py:116
  315.6 129.4 %reduce-scatter.6.cloned.1.call-start = ((), (), s32[]{:S(2)}) async-start(), calls=%async_computation.12 | async-start | bytes 2949120 | tf_op jit(solution)/shard_map/reduce_scatter | solution.py:120
  315.7 7.0 %copy-start.9 = (bf16[128,1024]{1,0:T(8,128)(2,1)S(1)}, bf16[128,1024]{1,0:T(8,128)(2,1)}, u32[]{:S(2)}) copy-start(bf16[128,1024]{1,0:T(8,128)(2,1)} %param.21) | copy-start | bytes 786436
  364.4 58.4 %all-to-all-start.4 = ((bf16[4,576,1024]{2,1,0:T(8,128)(2,1)}), bf16[4,576,1024]{2,1,0:T(8,128)(2,1)}, u32[]{:S(2)}, u32[]{:S(2)}) async-start(bf16[4,576,1024]{2,1,0:T(8,128)(2,1)} %bitcast.71), calls=%async_computation.7 | async-start | bytes 9437184 | tf_op jit(solution)/shard_map/all_to_all | solution.py:116
  422.8 16.7 %all-to-all-start.2 = ((bf16[4,32,4096]{2,1,0:T(8,128)(2,1)}), bf16[4,32,4096]{2,1,0:T(8,128)(2,1)S(1)}, u32[]{:S(2)}, u32[]{:S(2)}) async-start(bf16[4,32,4096]{2,1,0:T(8,128)(2,1)} %bitcast.76), calls=%async_computation.2 | async-start | bytes 2097152 | tf_op jit(solution)/shard_map/all_to_all | solution.py:116
  426.4 19.2 %copy-start.3 = (f32[128,1024]{1,0:T(8,128)S(1)}, f32[128,1024]{1,0:T(8,128)}, u32[]{:S(2)}) copy-start(f32[128,1024]{1,0:T(8,128)} %copy-done.2) | copy-start | bytes 1572868
  440.5 18.5 %all-to-all-start.5 = ((bf16[4,144,1024]{2,1,0:T(8,128)(2,1)}), bf16[4,144,1024]{2,1,0:T(8,128)(2,1)S(1)}, u32[]{:S(2)}, u32[]{:S(2)}) async-start(bf16[4,144,1024]{2,1,0:T(8,128)(2,1)} %bitcast.74), calls=%async_computation.8 | async-start | bytes 2359296 | tf_op jit(solution)/shard_map/all_to_all | solution.py:116
  445.0 36.0 %reduce-scatter.8.cloned.1.call-start = ((), (), s32[]{:S(2)}) async-start(), calls=%async_computation.13 | async-start | bytes 737280 | tf_op jit(solution)/shard_map/reduce_scatter | solution.py:120
  451.4 21.9 %copy-start.11 = (bf16[128,1024]{1,0:T(8,128)(2,1)S(1)}, bf16[128,1024]{1,0:T(8,128)(2,1)}, u32[]{:S(2)}) copy-start(bf16[128,1024]{1,0:T(8,128)(2,1)} %param.11) | copy-start | bytes 786436
  451.4 23.9 %copy-start.5 = (f32[128,8,256]{2,1,0:T(8,128)S(1)}, f32[128,8,256]{2,1,0:T(8,128)}, u32[]{:S(2)}) copy-start(f32[128,8,256]{2,1,0:T(8,128)} %copy-done.4) | copy-start | bytes 3145732
  459.0 10.8 %all-to-all-start.3 = ((bf16[4,8,4096]{2,1,0:T(8,128)(2,1)}), bf16[4,8,4096]{2,1,0:T(8,128)(2,1)}, u32[]{:S(2)}, u32[]{:S(2)}) async-start(bf16[4,8,4096]{2,1,0:T(8,128)(2,1)} %bitcast.19), calls=%async_computation.3 | async-start | bytes 524288 | tf_op jit(solution)/shard_map/all_to_all | solution.py:116
  469.8 10.5 %all-to-all-start.6 = ((bf16[4,36,1024]{2,1,0:T(8,128)(2,1)}), bf16[4,36,1024]{2,1,0:T(8,128)(2,1)S(1)}, u32[]{:S(2)}, u32[]{:S(2)}) async-start(bf16[4,36,1024]{2,1,0:T(8,128)(2,1)} %all_to_all.54), calls=%async_computation.9 | async-start | bytes 655360 | tf_op jit(solution)/shard_map/all_to_all | solution.py:116
  (7 other events, 11.2 us)
Sparse Core Ops, SparseCore 0:
  14.7 114.7 all-gather.1
  233.9 100.4 reduce-scatter.3
  336.8 31.8 reduce-scatter.5
  447.9 19.6 reduce-scatter.7

commit v14 on v11

--- a/solution.py
+++ b/solution.py
@@ -87,6 +87,11 @@
         scratch_shapes=[pltpu.SemaphoreType.DMA(()), pltpu.SemaphoreType.DMA(())],
         compiler_params=pltpu.CompilerParams(
             collective_id=collective_id, has_side_effects=True
+        ),
+        cost_estimate=pl.CostEstimate(
+            flops=0,
+            transcendentals=0,
+            bytes_accessed=2 * halves[0].size * halves.dtype.itemsize,
         ),
     )(halves)
     own = lax.dynamic_index_in_dim(halves, lax.axis_index("core"), 0, keepdims=False)

time: 495 us -> 495 us (level)
  no operation moved by 1% of the time
where the time goes in v14:
time: 495 us; the launch traced here: 490 us
  waiting for transfers between devices  204 us (41%)
  matrix products  71.3 us (14%)
  other arithmetic  71.2 us (14%)
  local copies, waits for them, and re-layouts  52.3 us (11%)
  starting transfers between devices  44.2 us (9%)
  Pallas kernels  31.8 us (6%)
  between operations  14.9 us (3%)
    all_gather x1, waiting for transfers between devices, gather_packed(): full = lax.all_gather(packed, AXES, axis=0, tiled=True)  110 us
    all_to_all x6, waiting for transfers between devices, scatter_packed(): got = lax.all_to_all(blocks, axis, 0, 0, tiled=True)  90.9 us
    pallas_call x3, Pallas kernels, pair_exchange(): pl.pallas_call(pair_kernel, out_shape=jax.ShapeDtypeStruct(halves.shape[1...  31.8 us
    convert_element_type x3, other arithmetic, pair_exchange(): (own.astype(jnp.float32) + received.astype(jnp.float32)).astype(jnp.bfloa...  27.8 us
    all_to_all x6, starting transfers between devices, scatter_packed(): got = lax.all_to_all(blocks, axis, 0, 0, tiled=True)  24.3 us
    concatenate x2, other arithmetic, scatter_packed(): packed = jnp.concatenate(pieces, axis=1).astype(jnp.bfloat16)  18.8 us
    reshape x1, local copies, waits for them, and re-layouts, per_device(): w_down = w_down_packed.reshape(n * down_rows, width)  17.6 us
    all_to_all x1, starting transfers between devices, exchange_packed(): blocks = lax.all_to_all(packed.astype(dtype), AXES, 0, 0, tiled=True)  15 us
  transfers between devices with their start and end apart: 14, of which 8 were waited for; matrix products, arithmetic and copies ran while one was open for 27% of the time, Pallas kernels for 3%

profile of v14, /device:TPU:0, one launch (start us, length us, event | category | flops | bytes accessed | tf_op | source)
XLA Modules:
  0.0 489.8 jit_solution(10587142110253765782)
XLA Ops:
  19.3 110.3 %all-gather.2.cloned.1.call-done = bf16[1024,18176]{1,0:T(8,128)(2,1)} async-done(((bf16[8,18176]{1,0:T(8,128)(2,1)}), bf16[1024,18176]{1,0:T(8,128)(2,1)}) %all-gather.2.cloned.1.call-update) | async-done | bytes 37224464 | tf_op jit(solution)/shard_map/all_gather | solution.py:31
  132.0 3.9 fusion.13
  138.2 7.8 %slice.148 = bf16[1024,4608]{1,0:T(8,128)(2,1)} slice(bf16[1024,18176]{1,0:T(8,128)(2,1)} %all-gather.2.cloned.1.call-done), slice={[0:1024], [13568:18176]} | slice | bytes 18874368 | tf_op jit(solution)/shard_map/slice | solution.py:34
  146.0 17.6 %reshape.148 = bf16[4608,1024]{1,0:T(8,128)(2,1)} reshape(bf16[1024,4608]{1,0:T(8,128)(2,1)} %slice.148) | data formatting | bytes 18874368 | tf_op jit(solution)/shard_map/reshape | solution.py:166
  163.6 8.2 %convolution_bitcast_fusion = f32[128,4608]{1,0:T(8,128)} fusion(bf16[4608,1024]{1,0:T(8,128)(2,1)} %reshape.148, bf16[128,1024]{1,0:T(8,128)(2,1)S(1)} %copy-done.8), kind=kOutput, calls=%fused_computation.16 | convolution fusion | flops 1207959552 | bytes 12058624 | tf_op jit(solution)/shard_map/dot_general | solution.py:206
  178.1 5.2 %fusion.5 = f32[128,4608]{1,0:T(8,128)S(1)} fusion(bf16[128,1024]{1,0:T(8,128)(2,1)S(1)} %multiply_convert_fusion.6, bf16[1024,18176]{1,0:T(8,128)(2,1)} %all-gather.2.cloned.1.call-done), kind=kOutput, calls=%fused_computation.10 | convolution fusion | flops 1207959552 | bytes 12058624 | tf_op jit(solution)/shard_map/dot_general | solution.py:198
  183.3 5.9 %multiply_convert_fusion.1 = (bf16[128,4608]{1,0:T(8,128)(2,1)S(1)}, bf16[128,4608]{1,0:T(8,128)(2,1)S(1)}, bf16[128,4608]{1,0:T(8,128)(2,1)S(1)}) fusion(f32[128,4608]{1,0:T(8,128)S(1)} %copy-done.7, f32[128,4608]{1,0:T(8,128)S(1)} %fusion.5, bf16[128,1024]{1,0:T(8,128)(2,1)} %copy-done.20, bf16[1024,18176]{1,0:T(8,128)(2,1)} %all-gather.2.cloned.1.call-done), kind=kOutput, calls=%fused_computation.22 | convolution fusion | flops 1216806912 | bytes 17956864 | tf_op jit(solution)/shard_map/dot_general | solution.py:197
  194.9 10.8 %pad_maximum_fusion = bf16[1024,9216]{1,0:T(8,128)(2,1)} fusion(bf16[1024,4608]{1,0:T(8,128)(2,1)S(1)} %fusion.50, bf16[1024,4608]{1,0:T(8,128)(2,1)S(1)} %fusion.49), kind=kLoop, calls=%fused_computation | loop fusion | flops 37748736 | bytes 37748736 | tf_op jit(solution)/shard_map/concatenate | solution.py:111
  205.7 16.0 %shard_map.187 = bf16[512,9216]{1,0:T(8,128)(2,1)} custom-call(bf16[2,512,9216]{2,1,0:T(8,128)(2,1)} %bitcast.67), custom_call_target="tpu_custom_call" | custom-call | bytes 18874368 | tf_op jit(solution)/shard_map/pallas_call | solution.py:82
  221.7 12.1 %fusion = bf16[512,9216]{1,0:T(8,128)(2,1)} fusion(bf16[512,9216]{1,0:T(8,128)(2,1)} %shard_map.187, bf16[2,512,9216]{2,1,0:T(8,128)(2,1)} %bitcast.68, s32[]{:T(128)S(6)} %select_n.8), kind=kLoop, calls=%fused_computation.2 | loop fusion | flops 18874368 | bytes 28311556 | tf_op jit(solution)/shard_map/convert_element_type | solution.py:98
  237.4 7.2 %fusion.3 = f32[128,1024]{1,0:T(8,128)S(1)} fusion(bf16[128,4608]{1,0:T(8,128)(2,1)} %copy-done.15, bf16[1024,18176]{1,0:T(8,128)(2,1)} %all-gather.2.cloned.1.call-done), kind=kOutput, calls=%fused_computation.8 | convolution fusion | flops 1207959552 | bytes 11141120 | tf_op jit(solution)/shard_map/dot_general | solution.py:232
  244.7 5.9 %multiply_reduce_fusion.3 = (f32[1024]{0:T(1024)S(1)}, f32[128]{0:T(128)S(1)}, f32[128,1024]{1,0:T(8,128)S(1)}) fusion(f32[128,1024]{1,0:T(8,128)S(1)} %get-tuple-element.75, f32[128]{0:T(128)S(1)} %get-tuple-element.73, f32[1024]{0:T(1024)S(1)} %get-tuple-element.40, f32[128,1024]{1,0:T(8,128)S(1)} %fusion.3, bf16[128,4608]{1,0:T(8,128)(2,1)S(1)} %copy-done.14, ...), kind=kOutput, calls=%fused_computation.59 | convolution fusion | flops 1208875904 | bytes 12198912 | tf_op jit(solution)/shard_map/dot_general | solution.py:231
  257.6 6.1 %fusion.34 = (f32[1024]{0:T(1024)S(1)}, f32[128]{0:T(128)S(1)}, f32[128,1024]{1,0:T(8,128)}) fusion(bf16[128,1024]{1,0:T(8,128)(2,1)S(1)} %copy-done.10, f32[128]{0:T(128)S(1)} %get-tuple-element.71, f32[1024]{0:T(1024)S(1)} %get-tuple-element.41, bf16[1024,18176]{1,0:T(8,128)(2,1)} %all-gather.2.cloned.1.call-done, ...), kind=kOutput, calls=%fused_computation.49 | convolution fusion | flops 808582016 | bytes 7873536 | tf_op jit(solution)/shard_map/dot_general | solution.py:268
  265.0 15.0 %all-to-all-start = ((f32[128,8,256]{2,1,0:T(8,128)}), f32[128,8,256]{2,1,0:T(8,128)S(1)}, u32[]{:S(2)}, u32[]{:S(2)}) async-start(f32[128,8,256]{2,1,0:T(8,128)} %pad_bitcast_fusion), calls=%async_computation | async-start | bytes 2097152 | tf_op jit(solution)/shard_map/all_to_all | solution.py:50
  280.0 5.7 %fusion.35 = bf16[1024,3072]{1,0:T(8,128)(2,1)} fusion(bf16[128,1024]{0,1:T(8,128)(2,1)} %bitcast.79, bf16[128,1024]{1,0:T(8,128)(2,1)} %copy-done.22, bf16[128,1024]{1,0:T(8,128)(2,1)} %copy-done.16, bf16[128,1024]{1,0:T(8,128)(2,1)} %copy-done.21), kind=kOutput, calls=%fused_computation.73 | convolution fusion | flops 807665664 | bytes 7340032 | tf_op jit(solution)/shard_map/dot_general | solution.py:262
  285.7 8.0 %pad_maximum_fusion.1 = bf16[1024,4096]{1,0:T(8,128)(2,1)} fusion(bf16[1024,1024]{1,0:T(8,128)(2,1)} %fusion.38, bf16[1024,3072]{1,0:T(8,128)(2,1)} %fusion.35), kind=kLoop, calls=%fused_computation.5 | loop fusion | flops 16777216 | bytes 16777216 | tf_op jit(solution)/shard_map/concatenate | solution.py:111
  293.6 7.5 %shard_map.186 = bf16[512,4096]{1,0:T(8,128)(2,1)} custom-call(bf16[2,512,4096]{2,1,0:T(8,128)(2,1)} %bitcast.69), custom_call_target="tpu_custom_call" | custom-call | bytes 8388608 | tf_op jit(solution)/shard_map/pallas_call | solution.py:82
  301.2 7.3 %fusion.2 = bf16[512,4096]{1,0:T(8,128)(2,1)} fusion(bf16[512,4096]{1,0:T(8,128)(2,1)} %shard_map.186, bf16[2,512,4096]{2,1,0:T(8,128)(2,1)} %bitcast.70, s32[]{:T(128)S(6)} %select_n.8), kind=kLoop, calls=%fused_computation.7 | loop fusion | flops 8388608 | bytes 12582916 | tf_op jit(solution)/shard_map/convert_element_type | solution.py:98
  310.8 4.8 all-to-all-start.1
  322.7 5.0 %fusion.36.x_ref = bf16[2,2304,1024]{2,1,0:T(8,128)(2,1)} fusion(bf16[2,2304,128]{2,1,0:T(8,128)(2,1)S(1)} %bitcast.75, bf16[128,1024]{1,0:T(8,128)(2,1)S(1)} %copy-done.9), kind=kOutput, calls=%fused_computation.76 | convolution fusion | flops 1207959552 | bytes 10878976 | tf_op jit(solution)/shard_map/dot_general | solution.py:212
  327.7 8.3 %shard_map.188 = bf16[2304,1024]{1,0:T(8,128)(2,1)} custom-call(bf16[2,2304,1024]{2,1,0:T(8,128)(2,1)} %fusion.36.x_ref), custom_call_target="tpu_custom_call" | custom-call | bytes 9437184 | tf_op jit(solution)/shard_map/pallas_call | solution.py:82
  336.0 8.4 %fusion.1 = bf16[2304,1024]{1,0:T(8,128)(2,1)} fusion(bf16[2304,1024]{1,0:T(8,128)(2,1)} %shard_map.188, bf16[2,2304,1024]{2,1,0:T(8,128)(2,1)} %fusion.36.x_ref, s32[]{:T(128)S(6)} %select_n.8), kind=kLoop, calls=%fused_computation.4 | loop fusion | flops 9437184 | bytes 14155780 | tf_op jit(solution)/shard_map/convert_element_type | solution.py:98
  344.4 20.0 %all-to-all-done.1 = bf16[4,128,4096]{2,1,0:T(8,128)(2,1)} async-done(((bf16[4,128,4096]{2,1,0:T(8,128)(2,1)}), bf16[4,128,4096]{2,1,0:T(8,128)(2,1)}, u32[]{:S(2)}, u32[]{:S(2)}) %all-to-all-start.1) | async-done | bytes 4194336 | tf_op jit(solution)/shard_map/all_to_all | solution.py:121
  364.4 4.9 %all-to-all-start.4 = ((bf16[4,576,1024]{2,1,0:T(8,128)(2,1)}), bf16[4,576,1024]{2,1,0:T(8,128)(2,1)}, u32[]{:S(2)}, u32[]{:S(2)}) async-start(bf16[4,576,1024]{2,1,0:T(8,128)(2,1)} %bitcast.71), calls=%async_computation.7 | async-start | bytes 9437184 | tf_op jit(solution)/shard_map/all_to_all | solution.py:121
  369.3 4.2 reduce_sum.172
  373.6 49.3 %all-to-all-done.4 = bf16[4,576,1024]{2,1,0:T(8,128)(2,1)} async-done(((bf16[4,576,1024]{2,1,0:T(8,128)(2,1)}), bf16[4,576,1024]{2,1,0:T(8,128)(2,1)}, u32[]{:S(2)}, u32[]{:S(2)}) %all-to-all-start.4) | async-done | bytes 4718624 | tf_op jit(solution)/shard_map/all_to_all | solution.py:121
  426.4 4.8 reduce_sum.175
  431.2 8.5 %all-to-all-done.2 = bf16[4,32,4096]{2,1,0:T(8,128)(2,1)S(1)} async-done(((bf16[4,32,4096]{2,1,0:T(8,128)(2,1)}), bf16[4,32,4096]{2,1,0:T(8,128)(2,1)S(1)}, u32[]{:S(2)}, u32[]{:S(2)}) %all-to-all-start.2) | async-done | bytes 1048608 | tf_op jit(solution)/shard_map/all_to_all | solution.py:121
  444.8 5.8 %fusion.26 = bf16[128,1024]{1,0:T(8,128)(2,1)} fusion(f32[128,1024]{1,0:T(8,128)S(1)} %copy-done.3, bf16[128,4608]{1,0:T(8,128)(2,1)S(1)} %get-tuple-element.59, bf16[4608,1024]{1,0:T(8,128)(2,1)} %reshape.148), kind=kOutput, calls=%fused_computation.33 | convolution fusion | flops 1208221696 | bytes 11403264 | tf_op jit(solution)/shard_map/dot_general | solution.py:202
  452.8 6.3 %all-to-all-done.5 = bf16[4,144,1024]{2,1,0:T(8,128)(2,1)S(1)} async-done(((bf16[4,144,1024]{2,1,0:T(8,128)(2,1)}), bf16[4,144,1024]{2,1,0:T(8,128)(2,1)S(1)}, u32[]{:S(2)}, u32[]{:S(2)}) %all-to-all-start.5) | async-done | bytes 1179680 | tf_op jit(solution)/shard_map/all_to_all | solution.py:121
  459.2 4.0 all-to-all-start.3
  464.2 5.7 %all-to-all-done.3 = bf16[4,8,4096]{2,1,0:T(8,128)(2,1)} async-done(((bf16[4,8,4096]{2,1,0:T(8,128)(2,1)}), bf16[4,8,4096]{2,1,0:T(8,128)(2,1)}, u32[]{:S(2)}, u32[]{:S(2)}) %all-to-all-start.3) | async-done | bytes 262176 | tf_op jit(solution)/shard_map/all_to_all | solution.py:121
  (139 shorter events, 74.3 us)
Async XLA Ops:
  7.2 122.4 %all-gather.2.cloned.1.call-start = ((), (), s32[]{:S(2)}) async-start(), calls=%async_computation.10 | async-start | bytes 37515264 | tf_op jit(solution)/shard_map/all_gather | solution.py:31
  14.6 321.4 %reduce-scatter.4.cloned.1.call-start = ((), (), s32[]{:S(2)}) async-start(), calls=%async_computation.11 | async-start | bytes 11796480 | tf_op jit(solution)/shard_map/reduce_scatter | solution.py:125
  15.4 2.4 collective-permute-start.1
  132.0 4.0 copy-start.17
  135.9 37.9 %copy-start = (f32[128,3072]{1,0:T(8,128)}, f32[128,3072]{1,0:T(8,128)S(1)}, u32[]{:S(2)}) copy-start(f32[128,3072]{1,0:T(8,128)S(1)} %fusion.13) | copy-start | bytes 4718596
  136.0 37.7 %collective-permute-start = (bf16[2,1024]{1,0:T(2,128)(2,1)S(1)}, bf16[2,1024]{1,0:T(2,128)(2,1)S(1)}, u32[]{:S(2)}, u32[]{:S(2)}) collective-permute-start(bf16[2,1024]{1,0:T(2,128)(2,1)S(1)} %slice.138), channel_id=1, source_target_pairs={{0,1},{1,2},{2,3},{3,4},{4,5},{5,6},{6,7},{7,8},{8,9},{9,10},{10,1... | collective-permute-start | bytes 12296 | tf_op jit(solution)/shard_map/ppermute | solution.py:16
  146.0 17.6 %copy-start.8 = (bf16[128,1024]{1,0:T(8,128)(2,1)S(1)}, bf16[128,1024]{1,0:T(8,128)(2,1)}, u32[]{:S(2)}) copy-start(bf16[128,1024]{1,0:T(8,128)(2,1)} %param.21) | copy-start | bytes 786436
  171.8 3.1 copy-start.10
  177.2 73.4 %copy-start.2 = (f32[128,1024]{1,0:T(8,128)}, f32[128,1024]{1,0:T(8,128)S(1)}, u32[]{:S(2)}) copy-start(f32[128,1024]{1,0:T(8,128)S(1)} %get-tuple-element.75) | copy-start | bytes 1572868
  178.0 5.2 %copy-start.7 = (f32[128,4608]{1,0:T(8,128)S(1)}, f32[128,4608]{1,0:T(8,128)}, u32[]{:S(2)}) copy-start(f32[128,4608]{1,0:T(8,128)} %convolution_bitcast_fusion) | copy-start | bytes 7077892
  237.4 7.2 %copy-start.14 = (bf16[128,4608]{1,0:T(8,128)(2,1)S(1)}, bf16[128,4608]{1,0:T(8,128)(2,1)}, u32[]{:S(2)}) copy-start(bf16[128,4608]{1,0:T(8,128)(2,1)} %copy-done.13) | copy-start | bytes 3538948
  250.6 2.9 copy-start.1
  250.6 2.9 copy-start.12
  250.8 4.4 copy-start.19
  253.7 3.9 copy-start.16
  253.9 3.5 collective-permute-start.2
  257.6 6.1 %copy-start.21 = (bf16[128,1024]{1,0:T(8,128)(2,1)}, bf16[128,1024]{1,0:T(8,128)(2,1)S(1)}, u32[]{:S(2)}) copy-start(bf16[128,1024]{1,0:T(8,128)(2,1)S(1)} %get-tuple-element.60) | copy-start | bytes 786436
  257.6 6.1 %copy-start.22 = (bf16[128,1024]{1,0:T(8,128)(2,1)}, bf16[128,1024]{1,0:T(8,128)(2,1)S(1)}, u32[]{:S(2)}) copy-start(bf16[128,1024]{1,0:T(8,128)(2,1)S(1)} %get-tuple-element.61) | copy-start | bytes 786436
  265.0 45.8 %all-to-all-start = ((f32[128,8,256]{2,1,0:T(8,128)}), f32[128,8,256]{2,1,0:T(8,128)S(1)}, u32[]{:S(2)}, u32[]{:S(2)}) async-start(f32[128,8,256]{2,1,0:T(8,128)} %pad_bitcast_fusion), calls=%async_computation | async-start | bytes 2097152 | tf_op jit(solution)/shard_map/all_to_all | solution.py:50
  310.8 4.9 %copy-start.4 = (f32[128,8,256]{2,1,0:T(8,128)}, f32[128,8,256]{2,1,0:T(8,128)S(1)}, u32[]{:S(2)}) copy-start(f32[128,8,256]{2,1,0:T(8,128)S(1)} %all-to-all-done) | copy-start | bytes 3145732
  310.8 53.6 %all-to-all-start.1 = ((bf16[4,128,4096]{2,1,0:T(8,128)(2,1)}), bf16[4,128,4096]{2,1,0:T(8,128)(2,1)}, u32[]{:S(2)}, u32[]{:S(2)}) async-start(bf16[4,128,4096]{2,1,0:T(8,128)(2,1)} %bitcast.72), calls=%async_computation.1 | async-start | bytes 8388608 | tf_op jit(solution)/shard_map/all_to_all | solution.py:121
  315.6 128.6 %reduce-scatter.6.cloned.1.call-start = ((), (), s32[]{:S(2)}) async-start(), calls=%async_computation.12 | async-start | bytes 2949120 | tf_op jit(solution)/shard_map/reduce_scatter | solution.py:125
  315.7 7.0 %copy-start.9 = (bf16[128,1024]{1,0:T(8,128)(2,1)S(1)}, bf16[128,1024]{1,0:T(8,128)(2,1)}, u32[]{:S(2)}) copy-start(bf16[128,1024]{1,0:T(8,128)(2,1)} %param.21) | copy-start | bytes 786436
  364.4 58.4 %all-to-all-start.4 = ((bf16[4,576,1024]{2,1,0:T(8,128)(2,1)}), bf16[4,576,1024]{2,1,0:T(8,128)(2,1)}, u32[]{:S(2)}, u32[]{:S(2)}) async-start(bf16[4,576,1024]{2,1,0:T(8,128)(2,1)} %bitcast.71), calls=%async_computation.7 | async-start | bytes 9437184 | tf_op jit(solution)/shard_map/all_to_all | solution.py:121
  422.8 16.9 %all-to-all-start.2 = ((bf16[4,32,4096]{2,1,0:T(8,128)(2,1)}), bf16[4,32,4096]{2,1,0:T(8,128)(2,1)S(1)}, u32[]{:S(2)}, u32[]{:S(2)}) async-start(bf16[4,32,4096]{2,1,0:T(8,128)(2,1)} %bitcast.76), calls=%async_computation.2 | async-start | bytes 2097152 | tf_op jit(solution)/shard_map/all_to_all | solution.py:121
  426.4 18.4 %copy-start.3 = (f32[128,1024]{1,0:T(8,128)S(1)}, f32[128,1024]{1,0:T(8,128)}, u32[]{:S(2)}) copy-start(f32[128,1024]{1,0:T(8,128)} %copy-done.2) | copy-start | bytes 1572868
  440.7 18.5 %all-to-all-start.5 = ((bf16[4,144,1024]{2,1,0:T(8,128)(2,1)}), bf16[4,144,1024]{2,1,0:T(8,128)(2,1)S(1)}, u32[]{:S(2)}, u32[]{:S(2)}) async-start(bf16[4,144,1024]{2,1,0:T(8,128)(2,1)} %bitcast.74), calls=%async_computation.8 | async-start | bytes 2359296 | tf_op jit(solution)/shard_map/all_to_all | solution.py:121
  444.2 37.0 %reduce-scatter.8.cloned.1.call-start = ((), (), s32[]{:S(2)}) async-start(), calls=%async_computation.13 | async-start | bytes 737280 | tf_op jit(solution)/shard_map/reduce_scatter | solution.py:125
  450.6 22.9 %copy-start.11 = (bf16[128,1024]{1,0:T(8,128)(2,1)S(1)}, bf16[128,1024]{1,0:T(8,128)(2,1)}, u32[]{:S(2)}) copy-start(bf16[128,1024]{1,0:T(8,128)(2,1)} %param.11) | copy-start | bytes 786436
  450.6 24.9 %copy-start.5 = (f32[128,8,256]{2,1,0:T(8,128)S(1)}, f32[128,8,256]{2,1,0:T(8,128)}, u32[]{:S(2)}) copy-start(f32[128,8,256]{2,1,0:T(8,128)} %copy-done.4) | copy-start | bytes 3145732
  459.2 10.8 %all-to-all-start.3 = ((bf16[4,8,4096]{2,1,0:T(8,128)(2,1)}), bf16[4,8,4096]{2,1,0:T(8,128)(2,1)}, u32[]{:S(2)}, u32[]{:S(2)}) async-start(bf16[4,8,4096]{2,1,0:T(8,128)(2,1)} %bitcast.19), calls=%async_computation.3 | async-start | bytes 524288 | tf_op jit(solution)/shard_map/all_to_all | solution.py:121
  470.0 10.5 %all-to-all-start.6 = ((bf16[4,36,1024]{2,1,0:T(8,128)(2,1)}), bf16[4,36,1024]{2,1,0:T(8,128)(2,1)S(1)}, u32[]{:S(2)}, u32[]{:S(2)}) async-start(bf16[4,36,1024]{2,1,0:T(8,128)(2,1)} %all_to_all.54), calls=%async_computation.9 | async-start | bytes 655360 | tf_op jit(solution)/shard_map/all_to_all | solution.py:121
  (7 other events, 11.2 us)
Sparse Core Ops, SparseCore 0:
  14.7 114.7 all-gather.1
  233.9 100.4 reduce-scatter.3
  336.8 31.8 reduce-scatter.5
  447.1 20.0 reduce-scatter.7
